TPU v7x, 256 devices: a whole 4x4x8 slice. The times are simulated.
256 devices in a mesh: head: 32 (over y, z), dp: 8 (over x, core).
Axes of the slice: x: 4, y: 4, z: 8, core: 2. Of those that a mesh axis runs over, the one named last changes fastest.
Arguments:
- attn_out: bfloat16 [2048, 8192], P('dp', 'head'), may hold values from -6 to 6
- head_mask: int32 [64], P('head'), may hold values from 0 to 1, as said below
- gate_scale: float32 [64], P('head'), may hold values from 0.25 to 2
- w_out: bfloat16 [8192, 8192], P('head', 'dp'), may hold values from -0.09375 to 0.09375
- grad_out: bfloat16 [2048, 8192], P(('dp', 'head')), may hold values from -6 to 6
Outputs:
- proj_out: bfloat16 [2048, 8192], P(('dp', 'head'))
- grad_attn: bfloat16 [2048, 8192], P('dp', 'head')
- grad_w: float32 [8192, 8192], P('head', 'dp')
Inputs may be any that keep to these rules, and one draw needn't show every extreme that they name: `head_mask`: exactly 32 heads are live.
All inputs are finite; a program needn't handle non-finite values.
Results may differ from a plain program's by a relative error of at most 0.0051.
Values may be sent and summed in bfloat16 or wider, within the bound.
No kernel may reach another device: no remote copies, remote signals or barrier semaphores. Data moves between devices by JAX's collectives and lax.ppermute only.
A program may use at most 128 MiB of HBM per device.

v0:
```python
import jax
import jax.numpy as jnp
from jax import lax
from jax.sharding import PartitionSpec as P


def shards(attn_out, head_mask, gate_scale, w_out, grad_out):
    gate_vals = head_mask.astype(jnp.float32) * gate_scale
    width_each = attn_out.shape[1] // gate_vals.shape[0]
    col_gate = jnp.repeat(gate_vals, width_each)
    gated = (attn_out.astype(jnp.float32) * col_gate[None, :]).astype(jnp.bfloat16)
    weight_rows = lax.all_gather(w_out, "dp", axis=1, tiled=True)
    proj_out = lax.psum_scatter(
        jnp.dot(gated, weight_rows, preferred_element_type=jnp.float32),
        "head",
        scatter_dimension=0,
        tiled=True,
    ).astype(jnp.bfloat16)
    grad_full = lax.all_gather(grad_out, "head", axis=0, tiled=True)
    back_proj = lax.dot_general(
        grad_full, weight_rows, (((1,), (1,)), ((), ())), preferred_element_type=jnp.float32
    )
    grad_attn = (back_proj * col_gate[None, :]).astype(jnp.bfloat16)
    grad_local = lax.dot_general(
        gated, grad_full, (((0,), (0,)), ((), ())), preferred_element_type=jnp.float32
    )
    grad_w = lax.psum_scatter(grad_local, "dp", scatter_dimension=1, tiled=True)
    return (proj_out, grad_attn, grad_w)


def solution(mesh):
    return jax.shard_map(
        shards,
        mesh=mesh,
        in_specs=(P("dp", "head"), P("head"), P("head"), P("head", "dp"), P(("dp", "head"), None)),
        out_specs=(P(("dp", "head"), None), P("dp", "head"), P("head", "dp")),
        check_vma=False,
    )
```

profile of v0, /device:TPU:1, one launch (start us, length us, event | category | flops | bytes accessed | tf_op | source)
XLA Modules:
  0.0 425.7 jit_solution(14172769329056932799)
XLA Ops:
  7.2 0.0 all-gather.3.cloned.1.call-start
  7.2 0.7 all-gather.3.cloned.1.call-update
  7.9 0.0 all-gather.5.cloned.1.call-start
  7.9 0.7 all-gather.5.cloned.1.call-update
  8.6 0.0 reduce-scatter.3.cloned.1.call-start
  8.7 0.7 convert_multiply_fusion
  9.4 0.1 broadcast_bitcast_fusion
  9.4 39.3 %all-gather.3.cloned.1.call-done = bf16[256,8192]{1,0:T(8,128)(2,1)} async-done(((bf16[256,1024]{1,0:T(8,128)(2,1)}), bf16[256,8192]{1,0:T(8,128)(2,1)}) %all-gather.3.cloned.1.call-update) | async-done | bytes 4194320 | tf_op jit(solution)/shard_map/all_gather | solution.py:12
  48.7 6.8 %fusion.2 = f32[256,8192]{1,0:T(8,128)} fusion(bf16[256,8192]{1,0:T(8,128)(2,1)} %all-gather.3.cloned.1.call-done, bf16[256,256]{1,0:T(8,128)(2,1)} %param.5, f32[256]{0:T(256)S(1)} %broadcast_bitcast_fusion), kind=kOutput, calls=%fused_computation.4 | convolution fusion | flops 1073938432 | bytes 12715008 | tf_op jit(solution)/shard_map/dot_general | solution.py:14
  55.5 0.0 copy-start
  55.5 0.0 reduce-scatter.3.cloned.1.call-update
  55.5 0.0 reduce-scatter.5.cloned.1.call-start
  55.6 74.5 %all-gather.5.cloned.1.call-done = bf16[256,8192]{1,0:T(8,128)(2,1)} async-done(((bf16[8,8192]{1,0:T(8,128)(2,1)}), bf16[256,8192]{1,0:T(8,128)(2,1)}) %all-gather.5.cloned.1.call-update) | async-done | bytes 4194320 | tf_op jit(solution)/shard_map/all_gather | solution.py:19
  130.1 0.0 copy-done
  130.1 6.7 %fusion.1 = f32[256,8192]{1,0:T(8,128)} fusion(bf16[256,8192]{1,0:T(8,128)(2,1)} %all-gather.5.cloned.1.call-done, bf16[256,256]{1,0:T(8,128)(2,1)S(1)} %copy-done, f32[256]{0:T(256)S(1)} %broadcast_bitcast_fusion), kind=kOutput, calls=%fused_computation.3 | convolution fusion | flops 1073938432 | bytes 12715008 | tf_op jit(solution)/shard_map/dot_general | solution.py:24
  136.8 0.0 reduce-scatter.5.cloned.1.call-update
  136.8 5.4 %fusion = bf16[256,256]{1,0:T(8,128)(2,1)} fusion(bf16[256,8192]{1,0:T(8,128)(2,1)} %all-gather.5.cloned.1.call-done, bf16[256,8192]{1,0:T(8,128)(2,1)} %all-gather.3.cloned.1.call-done, f32[256]{0:T(256)S(1)} %broadcast_bitcast_fusion), kind=kOutput, calls=%fused_computation.1 | convolution fusion | flops 1073872896 | bytes 8520704 | tf_op jit(solution)/shard_map/dot_general | solution.py:20
  142.2 217.0 %reduce-scatter.3.cloned.1.call-done = f32[8,8192]{1,0:T(8,128)} async-done(((f32[256,8192]{1,0:T(8,128)}), f32[8,8192]{1,0:T(8,128)}) %reduce-scatter.3.cloned.1.call-update) | async-done | bytes 262160 | tf_op jit(solution)/shard_map/reduce_scatter | solution.py:13
  359.2 1.6 convert_element_type.18
  360.8 58.3 %reduce-scatter.5.cloned.1.call-done = f32[256,1024]{1,0:T(8,128)} async-done(((f32[256,8192]{1,0:T(8,128)}), f32[256,1024]{1,0:T(8,128)}) %reduce-scatter.5.cloned.1.call-update) | async-done | bytes 1048592 | tf_op jit(solution)/shard_map/reduce_scatter | solution.py:27
Async XLA Ops:
  7.2 41.6 %all-gather.3.cloned.1.call-start = ((), (), s32[]{:S(2)}) async-start(), calls=%async_computation.2 | async-start | bytes 4718592 | tf_op jit(solution)/shard_map/all_gather | solution.py:12
  7.9 122.2 %all-gather.5.cloned.1.call-start = ((), (), s32[]{:S(2)}) async-start(), calls=%async_computation.4 | async-start | bytes 4325376 | tf_op jit(solution)/shard_map/all_gather | solution.py:19
  8.6 350.5 %reduce-scatter.3.cloned.1.call-start = ((), (), s32[]{:S(2)}) async-start(), calls=%async_computation.3 | async-start | bytes 8650752 | tf_op jit(solution)/shard_map/reduce_scatter | solution.py:13
  55.5 74.6 %copy-start = (bf16[256,256]{1,0:T(8,128)(2,1)S(1)}, bf16[256,256]{1,0:T(8,128)(2,1)}, u32[]{:S(2)}) copy-start(bf16[256,256]{1,0:T(8,128)(2,1)} %param.5) | copy-start | bytes 393220
  55.5 363.6 %reduce-scatter.5.cloned.1.call-start = ((), (), s32[]{:S(2)}) async-start(), calls=%async_computation.5 | async-start | bytes 9437184 | tf_op jit(solution)/shard_map/reduce_scatter | solution.py:27
Sparse Core Ops, SparseCore 0:
  9.8 38.8 all-gather.2
  51.3 78.7 all-gather.4
  134.1 225.0 reduce-scatter.2
  362.3 56.7 reduce-scatter.4
where the time goes:
time: 426 us
  waiting for transfers between devices  391 us (92%)
  matrix products  18.9 us (4%)
  between operations  13.8 us (3%)
    reduce_scatter x1, waiting for transfers between devices, shards(): lax.psum_scatter(jnp.dot(gated, weight_rows, preferred_element_type=jnp.f...  217 us
    all_gather x1, waiting for transfers between devices, shards(): grad_full = lax.all_gather(grad_out, 'head', axis=0, tiled=True)  74.5 us
    reduce_scatter x1, waiting for transfers between devices, shards(): grad_w = lax.psum_scatter(grad_local, 'dp', scatter_dimension=1, tiled=True)  58.3 us
    all_gather x1, waiting for transfers between devices, shards(): weight_rows = lax.all_gather(w_out, 'dp', axis=1, tiled=True)  39.3 us
  transfers between devices with their start and end apart: 4, of which 4 were waited for; matrix products, arithmetic and copies ran while one was open for 5% of the time, Pallas kernels for 0%

commit v1 on v0

v1 whole, which is shorter than its diff:
```python
import jax
import jax.numpy as jnp
from jax import lax
from jax.sharding import Mesh, PartitionSpec as P

BF = jnp.bfloat16
F32 = jnp.float32


def exchange(v, axes):
    return lax.all_to_all(v, axes, split_axis=0, concat_axis=0, tiled=False)


def shards(attn_out, head_mask, gate_scale, w_out, grad_out):
    nx, ny, nz, nc = (lax.axis_size(a) for a in "xyzc")
    core = lax.axis_index("c")
    swap = [(0, 1), (1, 0)]
    t, r = attn_out.shape
    j, d = grad_out.shape
    q = d // (nx * nc * ny)
    gate_vals = head_mask.astype(F32) * gate_scale
    col_gate = jnp.repeat(gate_vals, r // gate_vals.shape[0])
    gated = (attn_out.astype(F32) * col_gate[None, :]).astype(BF)

    a_all = lax.all_gather(gated, ("x", "y"), axis=0, tiled=False)
    a_all = a_all.reshape(nx, ny, t, r)

    g5 = grad_out.reshape(j, nx, nc, ny, q)
    g5 = jnp.where(core == 0, g5, g5[:, :, ::-1])
    g_send = g5.transpose(1, 3, 0, 2, 4).reshape(nx * ny, j, nc * q)
    g_mine = exchange(g_send, ("x", "y"))
    g_mine = jnp.broadcast_to(g_mine[None], (nz,) + g_mine.shape)
    g_all = exchange(g_mine, "z")
    g_all = g_all.transpose(1, 0, 2, 3).reshape(nx * t, nc * q)

    w_send = w_out.reshape(r, ny, q).transpose(1, 0, 2)
    w_mine = exchange(w_send, "y")
    w_other = lax.ppermute(w_mine, "c", swap)
    w_all = jnp.concatenate([w_mine, w_other], axis=2).reshape(ny * r, nc * q)

    a_mat = a_all.transpose(0, 2, 1, 3).reshape(nx * t, ny * r)
    part = jnp.dot(a_mat, w_all, preferred_element_type=F32).astype(BF)
    part = part.reshape(nx * ny, nz, j, nc * q).transpose(1, 0, 2, 3)
    proj = exchange(part, "z").astype(F32).sum(axis=0).astype(BF)
    proj = exchange(proj, ("x", "y")).reshape(nx, ny, j, nc, q)
    proj = proj.transpose(2, 0, 3, 1, 4)
    proj = jnp.where(core == 0, proj, proj[:, :, ::-1])
    proj_out = proj.reshape(j, d)

    back = lax.dot_general(g_all, w_all, (((1,), (1,)), ((), ())), preferred_element_type=F32)
    back = back.astype(BF).reshape(nx, t, ny, r).transpose(0, 2, 1, 3).reshape(nx * ny, t, r)
    back = exchange(back, ("x", "y")).astype(F32).sum(axis=0)
    grad_attn = (back * col_gate[None, :]).astype(BF)

    gw = lax.dot_general(a_mat, g_all, (((0,), (0,)), ((), ())), preferred_element_type=F32)
    gw = gw.reshape(ny, r, nc, q)
    gw = gw[:, :, 0] + lax.ppermute(gw[:, :, 1], "c", swap)
    gw = exchange(gw, "y")
    grad_w = gw.transpose(1, 0, 2).reshape(r, ny * q)
    return (proj_out, grad_attn, grad_w)


def solution(mesh):
    fine = Mesh(mesh.devices.reshape(4, 8, 4, 2), ("y", "z", "x", "c"))
    dp, head = ("x", "c"), ("y", "z")
    return jax.shard_map(
        shards,
        mesh=fine,
        in_specs=(P(dp, head), P(head), P(head), P(head, dp), P(dp + head, None)),
        out_specs=(P(dp + head, None), P(dp, head), P(head, dp)),
        check_vma=False,
    )
```

time: 426 us -> 237 us (0.56)
  waiting for transfers between devices: 391 us -> 142 us
  starting transfers between devices: 0.16 us -> 39.6 us
  local copies, waits for them, and re-layouts: 0.08 us -> 20.5 us
  matrix products: 18.9 us -> 6.41 us
  blocking collectives: 0 us -> 9.55 us
    reduce_scatter x2 -> x0, waiting for transfers between devices: 275 us -> none  [the longest x1 217 us: shards(): lax.psum_scatter(jnp.dot(gated, weight_rows, preferred_element_type=jnp.f...]
    all_to_all x0 -> x6, waiting for transfers between devices: none -> 90.9 us  [exchange(): return lax.all_to_all(v, axes, split_axis=0, concat_axis=0, tiled=False)]
    all_gather x2 -> x1, waiting for transfers between devices: 114 us -> 47.2 us  [shards(): a_all = lax.all_gather(gated, ('x', 'y'), axis=0, tiled=False)]
    all_to_all x0 -> x6, starting transfers between devices: none -> 34.1 us  [exchange(): return lax.all_to_all(v, axes, split_axis=0, concat_axis=0, tiled=False)]
    dot_general x3, matrix products: 18.9 us -> 6.41 us  [the longest x1 2.63 us: shards(): lax.dot_general(g_all, w_all, (((1,), (1,)), ((), ())), preferred_element...]
    all_to_all x0 -> x1, blocking collectives: none -> 9.55 us  [exchange(): return lax.all_to_all(v, axes, split_axis=0, concat_axis=0, tiled=False)]
    reshape x0 -> x8, local copies, waits for them, and re-layouts: none -> 8.68 us  [the longest x2 5.03 us: shards(): back.astype(BF).reshape(nx, t, ny, r).transpose(0, 2, 1, 3)]
    ppermute x0 -> x2, starting transfers between devices: none -> 5.45 us  [the longest x1 3.58 us: shards(): w_other = lax.ppermute(w_mine, 'c', swap)]
  transfers between devices with their start and end apart: 4 -> 9, of which waited for: 4 -> 9; matrix products, arithmetic and copies ran while one was open for 5% -> 4% of each run, Pallas kernels for 0% -> 0%
where the time goes in v1:
time: 237 us; the launch traced here: 236 us
  waiting for transfers between devices  142 us (60%)
  starting transfers between devices  39.6 us (17%)
  local copies, waits for them, and re-layouts  20.5 us (9%)
  between operations  14.3 us (6%)
  blocking collectives  9.55 us (4%)
  matrix products  6.41 us (3%)
  other arithmetic  3.33 us (1%)
    all_to_all x6, waiting for transfers between devices, exchange(): return lax.all_to_all(v, axes, split_axis=0, concat_axis=0, tiled=False)  90.9 us
    all_gather x1, waiting for transfers between devices, shards(): a_all = lax.all_gather(gated, ('x', 'y'), axis=0, tiled=False)  47.2 us
    all_to_all x6, starting transfers between devices, exchange(): return lax.all_to_all(v, axes, split_axis=0, concat_axis=0, tiled=False)  34.1 us
    all_to_all x1, blocking collectives, exchange(): return lax.all_to_all(v, axes, split_axis=0, concat_axis=0, tiled=False)  9.55 us
    reshape x2, local copies, waits for them, and re-layouts, shards(): back.astype(BF).reshape(nx, t, ny, r).transpose(0, 2, 1, 3)  5.03 us
  transfers between devices with their start and end apart: 9, of which 9 were waited for; matrix products, arithmetic and copies ran while one was open for 4% of the time, Pallas kernels for 0%

profile of v1, /device:TPU:1, one launch (start us, length us, event | category | flops | bytes accessed | tf_op | source)
XLA Modules:
  0.0 235.6 jit_solution(11082420818527983955)
XLA Ops:
  9.9 7.6 %all-to-all-start.3 = ((bf16[16,8,512]{2,1,0:T(8,128)(2,1)}), bf16[16,8,512]{2,1,0:T(8,128)(2,1)S(1)}, u32[]{:S(2)}, u32[]{:S(2)}) async-start(bf16[16,8,512]{2,1,0:T(8,128)(2,1)} %reshape.58), calls=%async_computation.3 | async-start | bytes 262144 | tf_op jit(solution)/shard_map/all_to_all | solution.py:11
  18.7 5.6 %all-to-all-done.3 = bf16[16,8,512]{2,1,0:T(8,128)(2,1)S(1)} async-done(((bf16[16,8,512]{2,1,0:T(8,128)(2,1)}), bf16[16,8,512]{2,1,0:T(8,128)(2,1)S(1)}, u32[]{:S(2)}, u32[]{:S(2)}) %all-to-all-start.3) | async-done | bytes 131104 | tf_op jit(solution)/shard_map/all_to_all | solution.py:11
  24.4 9.5 %all_to_all.35 = bf16[4,256,256]{1,2,0:T(8,128)(2,1)S(1)} all-to-all(bf16[4,256,256]{1,2,0:T(8,128)(2,1)S(1)} %bitcast.66), channel_id=1, replica_groups=mesh['y'=4,'z'=8,'x'=4,'c'=2] {'y'}, dimensions={0} | all-to-all | bytes 1048576 | tf_op jit(solution)/shard_map/all_to_all | solution.py:11
  35.0 8.2 %all-to-all-start.4 = ((bf16[8,16,8,512]{3,2,1,0:T(8,128)(2,1)}), bf16[8,16,8,512]{3,2,1,0:T(8,128)(2,1)S(1)}, u32[]{:S(2)}, u32[]{:S(2)}) async-start(bf16[8,16,8,512]{3,2,1,0:T(8,128)(2,1)} %broadcast_in_dim.10), calls=%async_computation.4 | async-start | bytes 2097152 | tf_op jit(solution)/shard_map/all_to_all | solution.py:11
  43.2 3.6 %collective-permute-start = (bf16[4,256,256]{1,2,0:T(8,128)(2,1)S(1)}, bf16[4,256,256]{1,2,0:T(8,128)(2,1)S(1)}, u32[]{:S(2)}, u32[]{:S(2)}) collective-permute-start(bf16[4,256,256]{1,2,0:T(8,128)(2,1)S(1)} %all_to_all.35), channel_id=1, source_target_pairs={{0,1},{1,0},{2,3},{3,2},{4,5},{5,4},{6,7},{7,6},{8,9},{9,8},{10,11... | collective-permute-start | bytes 1572872 | tf_op jit(solution)/shard_map/ppermute | solution.py:38
  46.7 1.5 collective-permute-done
  48.9 20.3 %all-to-all-done.4 = bf16[8,16,8,512]{3,2,1,0:T(8,128)(2,1)S(1)} async-done(((bf16[8,16,8,512]{3,2,1,0:T(8,128)(2,1)}), bf16[8,16,8,512]{3,2,1,0:T(8,128)(2,1)S(1)}, u32[]{:S(2)}, u32[]{:S(2)}) %all-to-all-start.4) | async-done | bytes 1048608 | tf_op jit(solution)/shard_map/all_to_all | solution.py:11
  69.4 2.6 %convolution_convert_fusion = bf16[1024,1024]{1,0:T(8,128)(2,1)} fusion(bf16[1024,512]{1,0:T(8,128)(2,1)S(1)} %bitcast.59, bf16[1024,512]{1,0:T(8,128)(2,1)S(1)} %bitcast.68), kind=kOutput, calls=%fused_computation.1 | convolution fusion | flops 1074790400 | bytes 4194304 | tf_op jit(solution)/shard_map/dot_general | solution.py:50
  72.0 3.3 %reshape.60 = bf16[4,256,4,256]{3,2,1,0:T(4,128)(2,1)S(1)} reshape(bf16[1024,1024]{1,0:T(8,128)(2,1)} %convolution_convert_fusion) | data formatting | bytes 4194304 | tf_op jit(solution)/shard_map/reshape | solution.py:51
  75.3 1.7 copy.35
  77.0 3.8 %all-to-all-start.5 = ((bf16[16,256,256]{2,1,0:T(8,128)(2,1)}), bf16[16,256,256]{2,1,0:T(8,128)(2,1)S(1)}, u32[]{:S(2)}, u32[]{:S(2)}) async-start(bf16[16,256,256]{2,1,0:T(8,128)(2,1)} %bitcast.57), calls=%async_computation.5 | async-start | bytes 4194304 | tf_op jit(solution)/shard_map/all_to_all | solution.py:11
  81.1 24.8 %all-to-all-done.5 = bf16[16,256,256]{2,1,0:T(8,128)(2,1)S(1)} async-done(((bf16[16,256,256]{2,1,0:T(8,128)(2,1)}), bf16[16,256,256]{2,1,0:T(8,128)(2,1)S(1)}, u32[]{:S(2)}, u32[]{:S(2)}) %all-to-all-start.5) | async-done | bytes 2097184 | tf_op jit(solution)/shard_map/all_to_all | solution.py:11
  107.0 1.3 copy.36
  108.3 47.2 %all-gather.3.cloned.1.call-done = bf16[4096,256]{1,0:T(8,128)(2,1)} async-done(((bf16[256,256]{1,0:T(8,128)(2,1)}), bf16[4096,256]{1,0:T(8,128)(2,1)}) %all-gather.3.cloned.1.call-update) | async-done | bytes 2097168 | tf_op jit(solution)/shard_map/all_gather | solution.py:25
  155.5 3.1 %copy.27 = bf16[4,256,4,256]{1,0,3,2:T(4,128)(2,1)S(1)} copy(bf16[4,256,4,256]{3,1,2,0:T(8,128)(2,1)} %bitcast.65) | data formatting | bytes 4194304 | tf_op jit(solution)/shard_map/transpose | solution.py:41
  162.2 6.7 %all-to-all-start.1 = ((bf16[8,16,8,512]{3,2,1,0:T(8,128)(2,1)}), bf16[8,16,8,512]{3,2,1,0:T(8,128)(2,1)S(1)}, u32[]{:S(2)}, u32[]{:S(2)}) async-start(bf16[8,16,8,512]{3,2,1,0:T(8,128)(2,1)} %bitcast.56), calls=%async_computation.1 | async-start | bytes 2097152 | tf_op jit(solution)/shard_map/all_to_all | solution.py:11
  168.9 2.5 %fusion.2 = f32[4,256,2,256]{3,1,2,0:T(8,128)S(1)} fusion(bf16[4,256,1024,1]{2,1,3,0:T(8,128)(2,1)S(1)} %bitcast.64, bf16[2,256,1024,1]{2,1,0,3:T(8,128)(2,1)} %bitcast.70), kind=kOutput, calls=%fused_computation.15 | convolution fusion | flops 1073741824 | bytes 5242880 | tf_op jit(solution)/shard_map/dot_general | solution.py:55
  171.5 1.9 collective-permute-start.1
  173.4 2.3 collective-permute-done.1
  176.8 21.3 %all-to-all-done.1 = bf16[8,16,8,512]{3,2,1,0:T(8,128)(2,1)S(1)} async-done(((bf16[8,16,8,512]{3,2,1,0:T(8,128)(2,1)}), bf16[8,16,8,512]{3,2,1,0:T(8,128)(2,1)S(1)}, u32[]{:S(2)}, u32[]{:S(2)}) %all-to-all-start.1) | async-done | bytes 1048608 | tf_op jit(solution)/shard_map/all_to_all | solution.py:11
  198.1 3.5 %all-to-all-start.6 = ((f32[4,256,256]{2,1,0:T(8,128)}), f32[4,256,256]{2,1,0:T(8,128)S(1)}, u32[]{:S(2)}, u32[]{:S(2)}) async-start(f32[4,256,256]{2,1,0:T(8,128)} %fusion), calls=%async_computation.6 | async-start | bytes 2097152 | tf_op jit(solution)/shard_map/all_to_all | solution.py:11
  202.4 13.7 %all-to-all-done.6 = f32[4,256,256]{2,1,0:T(8,128)S(1)} async-done(((f32[4,256,256]{2,1,0:T(8,128)}), f32[4,256,256]{2,1,0:T(8,128)S(1)}, u32[]{:S(2)}, u32[]{:S(2)}) %all-to-all-start.6) | async-done | bytes 1048608 | tf_op jit(solution)/shard_map/all_to_all | solution.py:11
  216.1 4.2 %all-to-all-start.2 = ((bf16[16,8,512]{2,1,0:T(8,128)(2,1)}), bf16[16,8,512]{2,1,0:T(8,128)(2,1)S(1)}, u32[]{:S(2)}, u32[]{:S(2)}) async-start(bf16[16,8,512]{2,1,0:T(8,128)(2,1)} %reduce_sum.21), calls=%async_computation.2 | async-start | bytes 262144 | tf_op jit(solution)/shard_map/all_to_all | solution.py:11
  222.0 5.0 %all-to-all-done.2 = bf16[16,8,512]{2,1,0:T(8,128)(2,1)S(1)} async-done(((bf16[16,8,512]{2,1,0:T(8,128)(2,1)}), bf16[16,8,512]{2,1,0:T(8,128)(2,1)S(1)}, u32[]{:S(2)}, u32[]{:S(2)}) %all-to-all-start.2) | async-done | bytes 131104 | tf_op jit(solution)/shard_map/all_to_all | solution.py:11
  (43 shorter events, 15.8 us)
Async XLA Ops:
  9.9 14.5 %all-to-all-start.3 = ((bf16[16,8,512]{2,1,0:T(8,128)(2,1)}), bf16[16,8,512]{2,1,0:T(8,128)(2,1)S(1)}, u32[]{:S(2)}, u32[]{:S(2)}) async-start(bf16[16,8,512]{2,1,0:T(8,128)(2,1)} %reshape.58), calls=%async_computation.3 | async-start | bytes 262144 | tf_op jit(solution)/shard_map/all_to_all | solution.py:11
  35.0 34.3 %all-to-all-start.4 = ((bf16[8,16,8,512]{3,2,1,0:T(8,128)(2,1)}), bf16[8,16,8,512]{3,2,1,0:T(8,128)(2,1)S(1)}, u32[]{:S(2)}, u32[]{:S(2)}) async-start(bf16[8,16,8,512]{3,2,1,0:T(8,128)(2,1)} %broadcast_in_dim.10), calls=%async_computation.4 | async-start | bytes 2097152 | tf_op jit(solution)/shard_map/all_to_all | solution.py:11
  43.2 5.1 %collective-permute-start = (bf16[4,256,256]{1,2,0:T(8,128)(2,1)S(1)}, bf16[4,256,256]{1,2,0:T(8,128)(2,1)S(1)}, u32[]{:S(2)}, u32[]{:S(2)}) collective-permute-start(bf16[4,256,256]{1,2,0:T(8,128)(2,1)S(1)} %all_to_all.35), channel_id=1, source_target_pairs={{0,1},{1,0},{2,3},{3,2},{4,5},{5,4},{6,7},{7,6},{8,9},{9,8},{10,11... | collective-permute-start | bytes 1572872 | tf_op jit(solution)/shard_map/ppermute | solution.py:38
  48.9 20.5 %copy-start.2 = (bf16[4,256,512]{2,1,0:T(8,128)(2,1)}, bf16[4,256,512]{2,1,0:T(8,128)(2,1)S(1)}, u32[]{:S(2)}) copy-start(bf16[4,256,512]{2,1,0:T(8,128)(2,1)S(1)} %copy.29) | copy-start | bytes 3145732
  77.0 3.9 %copy-start.5 = (f32[2]{0:T(128)S(1)}, f32[2]{0:T(128)}, u32[]{:S(2)}) copy-start(f32[2]{0:T(128)} %param.7) | copy-start | bytes 28
  77.0 3.9 %copy-start.6 = (s32[2]{0:T(128)S(1)}, s32[2]{0:T(128)}, u32[]{:S(2)}) copy-start(s32[2]{0:T(128)} %param.6) | copy-start | bytes 28
  77.0 28.9 %all-to-all-start.5 = ((bf16[16,256,256]{2,1,0:T(8,128)(2,1)}), bf16[16,256,256]{2,1,0:T(8,128)(2,1)S(1)}, u32[]{:S(2)}, u32[]{:S(2)}) async-start(bf16[16,256,256]{2,1,0:T(8,128)(2,1)} %bitcast.57), calls=%async_computation.5 | async-start | bytes 4194304 | tf_op jit(solution)/shard_map/all_to_all | solution.py:11
  80.9 25.3 %copy-start.4 = (bf16[256,256]{1,0:T(8,128)(2,1)S(1)}, bf16[256,256]{1,0:T(8,128)(2,1)}, u32[]{:S(2)}) copy-start(bf16[256,256]{1,0:T(8,128)(2,1)} %param.5) | copy-start | bytes 393220
  80.9 74.6 %all-gather.3.cloned.1.call-start = ((), (), s32[]{:S(2)}) async-start(), calls=%async_computation.7 | async-start | bytes 2228224 | tf_op jit(solution)/shard_map/all_gather | solution.py:25
  158.6 1.2 copy-start.3
  159.1 2.0 copy-start
  161.1 7.8 %copy-start.1 = (bf16[128,8,4,256]{3,1,2,0:T(8,128)(2,1)S(1)}, bf16[128,8,4,256]{3,1,2,0:T(8,128)(2,1)}, u32[]{:S(2)}) copy-start(bf16[128,8,4,256]{3,1,2,0:T(8,128)(2,1)} %copy-done) | copy-start | bytes 6291460
  162.2 35.9 %all-to-all-start.1 = ((bf16[8,16,8,512]{3,2,1,0:T(8,128)(2,1)}), bf16[8,16,8,512]{3,2,1,0:T(8,128)(2,1)S(1)}, u32[]{:S(2)}, u32[]{:S(2)}) async-start(bf16[8,16,8,512]{3,2,1,0:T(8,128)(2,1)} %bitcast.56), calls=%async_computation.1 | async-start | bytes 2097152 | tf_op jit(solution)/shard_map/all_to_all | solution.py:11
  171.5 4.2 %collective-permute-start.1 = (f32[4,256,256]{2,1,0:T(8,128)S(1)}, f32[4,256,256]{2,1,0:T(8,128)S(1)}, u32[]{:S(2)}, u32[]{:S(2)}) collective-permute-start(f32[4,256,256]{2,1,0:T(8,128)S(1)} %slice_bitcast_fusion), channel_id=1, source_target_pairs={{0,1},{1,0},{2,3},{3,2},{4,5},{5,4},{6,7},{7,6},{8,9},{9,8},{10,11... | collective-permute-start | bytes 3145736 | tf_op jit(solution)/shard_map/ppermute | solution.py:57
  198.1 18.0 %all-to-all-start.6 = ((f32[4,256,256]{2,1,0:T(8,128)}), f32[4,256,256]{2,1,0:T(8,128)S(1)}, u32[]{:S(2)}, u32[]{:S(2)}) async-start(f32[4,256,256]{2,1,0:T(8,128)} %fusion), calls=%async_computation.6 | async-start | bytes 2097152 | tf_op jit(solution)/shard_map/all_to_all | solution.py:11
  216.1 10.9 %all-to-all-start.2 = ((bf16[16,8,512]{2,1,0:T(8,128)(2,1)}), bf16[16,8,512]{2,1,0:T(8,128)(2,1)S(1)}, u32[]{:S(2)}, u32[]{:S(2)}) async-start(bf16[16,8,512]{2,1,0:T(8,128)(2,1)} %reduce_sum.21), calls=%async_computation.2 | async-start | bytes 262144 | tf_op jit(solution)/shard_map/all_to_all | solution.py:11
Sparse Core Ops, SparseCore 0:
  107.1 48.3 all-gather.2

commit v2 on v1

v2 whole, which is shorter than its diff:
```python
import jax
import jax.numpy as jnp
from jax import lax
from jax.sharding import Mesh, PartitionSpec as P

BF = jnp.bfloat16
F32 = jnp.float32


def exchange(v, axes):
    return lax.all_to_all(v, axes, split_axis=0, concat_axis=0, tiled=False)


def exchange_y(v):
    n = v.shape[0]
    me = lax.axis_index("y")
    got = [lax.dynamic_index_in_dim(v, me, 0, keepdims=False)]
    for s in range(1, n):
        piece = lax.dynamic_index_in_dim(v, (me + s) % n, 0, keepdims=False)
        got.append(lax.ppermute(piece, "y", [(i, (i + s) % n) for i in range(n)]))
    ring = jnp.stack([got[(n - 1 - k) % n] for k in range(2 * n - 1)])
    return lax.dynamic_slice_in_dim(ring, n - 1 - me, n, 0)


def shards(attn_out, head_mask, gate_scale, w_out, grad_out):
    nx, ny, nz, nc = (lax.axis_size(a) for a in "xyzc")
    core = lax.axis_index("c")
    swap = [(0, 1), (1, 0)]
    t, r = attn_out.shape
    j, d = grad_out.shape
    q = d // (nx * nc * ny)
    gate_vals = head_mask.astype(F32) * gate_scale
    col_gate = jnp.repeat(gate_vals, r // gate_vals.shape[0])
    gated = (attn_out.astype(F32) * col_gate[None, :]).astype(BF)
    gated = gated.reshape(ny, nz, j, r).transpose(1, 0, 2, 3)
    gated, grad_out = lax.optimization_barrier((gated, grad_out))

    a_all = lax.all_gather(gated.reshape(t, r), ("x", "y"), axis=0, tiled=True)

    g5 = grad_out.reshape(j, nx, nc, ny, q)
    g5 = jnp.where(core == 0, g5, g5[:, :, ::-1])
    g_send = g5.transpose(1, 3, 0, 2, 4).reshape(nx * ny, j, nc * q)
    g_mine = exchange(g_send, ("x", "y"))
    g_mine = jnp.broadcast_to(g_mine[None], (nz,) + g_mine.shape)
    g_all = exchange(g_mine, "z").reshape(nx * t, nc * q)

    w_mine = exchange_y(w_out.reshape(r, ny, q).transpose(1, 0, 2))
    w_other = lax.ppermute(w_mine, "c", swap)
    w_all = jnp.concatenate([w_mine, w_other], axis=2).reshape(ny * r, nc * q)

    a_all, g_all, w_all = lax.optimization_barrier((a_all, g_all, w_all))
    a_mat = a_all.reshape(nx, ny, nz, ny * j, r).transpose(2, 0, 3, 1, 4).reshape(nx * t, ny * r)
    part = jnp.dot(a_mat, w_all, preferred_element_type=F32)
    proj = lax.psum_scatter(part, "z", scatter_dimension=0, tiled=True).astype(BF)
    proj = exchange(proj.reshape(nx * ny, j, nc * q), ("x", "y")).reshape(nx, ny, j, nc, q)
    proj = proj.transpose(2, 0, 3, 1, 4)
    proj = jnp.where(core == 0, proj, proj[:, :, ::-1])
    proj_out = proj.reshape(j, d)

    part, g_all = lax.optimization_barrier((part, g_all))
    back = lax.dot_general(g_all, w_all, (((1,), (1,)), ((), ())), preferred_element_type=F32)
    back = back.astype(BF).reshape(nz, nx, ny * j, ny, r).transpose(1, 3, 0, 2, 4)
    back = exchange(back.reshape(nx * ny, t, r), ("x", "y")).astype(F32).sum(axis=0)
    back = back.reshape(nz, ny, j, r).transpose(1, 0, 2, 3).reshape(t, r)
    grad_attn = (back * col_gate[None, :]).astype(BF)

    gw = lax.dot_general(a_mat, g_all, (((0,), (0,)), ((), ())), preferred_element_type=F32)
    gw = gw.reshape(ny, r, nc, q)
    gw = gw[:, :, 0] + lax.ppermute(gw[:, :, 1], "c", swap)
    gw = exchange_y(gw)
    grad_w = gw.transpose(1, 0, 2).reshape(r, ny * q)
    return (proj_out, grad_attn, grad_w)


def solution(mesh):
    fine = Mesh(mesh.devices.reshape(4, 8, 4, 2), ("y", "z", "x", "c"))
    dp, head = ("x", "c"), ("y", "z")
    return jax.shard_map(
        shards,
        mesh=fine,
        in_specs=(P(dp, head), P(head), P(head), P(head, dp), P(dp + head, None)),
        out_specs=(P(dp + head, None), P(dp, head), P(head, dp)),
        check_vma=False,
    )
```

time: 237 us -> 158 us (0.67)
  waiting for transfers between devices: 142 us -> 65.1 us
  blocking collectives: 9.55 us -> 0 us
  local copies, waits for them, and re-layouts: 20.5 us -> 24.3 us
  other arithmetic: 3.33 us -> 6.98 us
  starting transfers between devices: 39.6 us -> 36.8 us
    all_to_all x6 -> x4, waiting for transfers between devices: 90.9 us -> 30.8 us  [exchange(): return lax.all_to_all(v, axes, split_axis=0, concat_axis=0, tiled=False)]
    all_gather x1, waiting for transfers between devices: 47.2 us -> 0.69 us  [shards(): a_all = lax.all_gather(gated.reshape(t, r), ('x', 'y'), axis=0, tiled=True)]
    ppermute x0 -> x6, waiting for transfers between devices: none -> 32 us  [exchange_y(): got.append(lax.ppermute(piece, 'y', [(i, (i + s) % n) for i in range(n)]))]
    all_to_all x6 -> x4, starting transfers between devices: 34.1 us -> 21.4 us  [exchange(): return lax.all_to_all(v, axes, split_axis=0, concat_axis=0, tiled=False)]
    ppermute x0 -> x6, starting transfers between devices: none -> 10.8 us  [exchange_y(): got.append(lax.ppermute(piece, 'y', [(i, (i + s) % n) for i in range(n)]))]
    all_to_all x1 -> x0, blocking collectives: 9.55 us -> none  [exchange(): return lax.all_to_all(v, axes, split_axis=0, concat_axis=0, tiled=False)]
    dot_general x1 -> x2, local copies, waits for them, and re-layouts: 1.32 us -> 3.87 us  [shards(): lax.dot_general(a_mat, g_all, (((0,), (0,)), ((), ())), preferred_element...]
    reshape x5 -> x3, local copies, waits for them, and re-layouts: 6.86 us -> 5.1 us  [the longest x2 5.07 us: shards(): back.astype(BF).reshape(nz, nx, ny * j, ny, r).transpose(1, 3, 0, 2, 4)]
  transfers between devices with their start and end apart: 9 -> 14, of which waited for: 9 -> 8; matrix products, arithmetic and copies ran while one was open for 4% -> 16% of each run, Pallas kernels for 0% -> 0%
where the time goes in v2:
time: 158 us; the launch traced here: 156 us
  waiting for transfers between devices  65.1 us (41%)
  starting transfers between devices  36.8 us (23%)
  local copies, waits for them, and re-layouts  24.3 us (15%)
  between operations  14.4 us (9%)
  matrix products  8.34 us (5%)
  other arithmetic  6.98 us (4%)
    ppermute x6, waiting for transfers between devices, exchange_y(): got.append(lax.ppermute(piece, 'y', [(i, (i + s) % n) for i in range(n)]))  32 us
    all_to_all x4, waiting for transfers between devices, exchange(): return lax.all_to_all(v, axes, split_axis=0, concat_axis=0, tiled=False)  30.8 us
    all_to_all x4, starting transfers between devices, exchange(): return lax.all_to_all(v, axes, split_axis=0, concat_axis=0, tiled=False)  21.4 us
    ppermute x6, starting transfers between devices, exchange_y(): got.append(lax.ppermute(piece, 'y', [(i, (i + s) % n) for i in range(n)]))  10.8 us
    unnamed x23, local copies, waits for them, and re-layouts  5.25 us
    reshape x2, local copies, waits for them, and re-layouts, shards(): back.astype(BF).reshape(nz, nx, ny * j, ny, r).transpose(1, 3, 0, 2, 4)  5.07 us
    dot_general x2, local copies, waits for them, and re-layouts, shards(): lax.dot_general(a_mat, g_all, (((0,), (0,)), ((), ())), preferred_element...  3.87 us
    transpose x1, local copies, waits for them, and re-layouts, shards(): a_all.reshape(nx, ny, nz, ny * j, r).transpose(2, 0, 3, 1, 4)  3.56 us
  transfers between devices with their start and end apart: 14, of which 8 were waited for; matrix products, arithmetic and copies ran while one was open for 16% of the time, Pallas kernels for 0%

profile of v2, /device:TPU:1, one launch (start us, length us, event | category | flops | bytes accessed | tf_op | source)
XLA Modules:
  0.0 155.9 jit_solution(9332969464736625652)
XLA Ops:
  11.1 3.6 %collective-permute-start = (bf16[256,256]{1,0:T(8,128)(2,1)S(1)}, bf16[256,256]{1,0:T(8,128)(2,1)S(1)}, u32[]{:S(2)}, u32[]{:S(2)}) collective-permute-start(bf16[256,256]{1,0:T(8,128)(2,1)S(1)} %bitcast.109), channel_id=1, source_target_pairs={{0,192},{64,0},{128,64},{192,128},{1,193},{65,1},{129,65},{193,129... | collective-permute-start | bytes 393224 | tf_op jit(solution)/shard_map/ppermute | solution.py:20
  16.5 4.3 %all-to-all-start = ((bf16[16,8,512]{2,1,0:T(8,128)(2,1)}), bf16[16,8,512]{2,1,0:T(8,128)(2,1)S(1)}, u32[]{:S(2)}, u32[]{:S(2)}) async-start(bf16[16,8,512]{2,1,0:T(8,128)(2,1)} %reshape.72), calls=%async_computation | async-start | bytes 262144 | tf_op jit(solution)/shard_map/all_to_all | solution.py:11
  21.0 3.0 %collective-permute-start.1 = (bf16[256,256]{1,0:T(8,128)(2,1)S(1)}, bf16[256,256]{1,0:T(8,128)(2,1)S(1)}, u32[]{:S(2)}, u32[]{:S(2)}) collective-permute-start(bf16[256,256]{1,0:T(8,128)(2,1)S(1)} %bitcast.110), channel_id=1, source_target_pairs={{0,128},{64,192},{128,0},{192,64},{1,129},{65,193},{129,1},{193,65... | collective-permute-start | bytes 393224 | tf_op jit(solution)/shard_map/ppermute | solution.py:20
  24.5 3.1 %all-to-all-done = bf16[16,8,512]{2,1,0:T(8,128)(2,1)S(1)} async-done(((bf16[16,8,512]{2,1,0:T(8,128)(2,1)}), bf16[16,8,512]{2,1,0:T(8,128)(2,1)S(1)}, u32[]{:S(2)}, u32[]{:S(2)}) %all-to-all-start) | async-done | bytes 131104 | tf_op jit(solution)/shard_map/all_to_all | solution.py:11
  28.7 8.2 %all-to-all-start.1 = ((bf16[8,16,8,512]{3,2,1,0:T(8,128)(2,1)}), bf16[8,16,8,512]{3,2,1,0:T(8,128)(2,1)S(1)}, u32[]{:S(2)}, u32[]{:S(2)}) async-start(bf16[8,16,8,512]{3,2,1,0:T(8,128)(2,1)} %broadcast_in_dim.10), calls=%async_computation.1 | async-start | bytes 2097152 | tf_op jit(solution)/shard_map/all_to_all | solution.py:11
  37.1 2.8 %collective-permute-start.3 = (bf16[4,256,256]{2,1,0:T(8,128)(2,1)S(1)}, bf16[4,256,256]{2,1,0:T(8,128)(2,1)S(1)}, u32[]{:S(2)}, u32[]{:S(2)}) collective-permute-start(bf16[4,256,256]{2,1,0:T(8,128)(2,1)S(1)} %constant_dynamic-slice_fusion.1), channel_id=1, source_target_pairs={{0,1},{1,0},{2,3},{3,2},{4,5},{5,4},{6,7},{7,6},{8,9},{9,8},{10,11... | collective-permute-start | bytes 1572872 | tf_op jit(solution)/shard_map/ppermute | solution.py:48
  39.9 1.5 collective-permute-done.3
  42.5 21.6 %all-to-all-done.1 = bf16[8,16,8,512]{3,2,1,0:T(8,128)(2,1)S(1)} async-done(((bf16[8,16,8,512]{3,2,1,0:T(8,128)(2,1)}), bf16[8,16,8,512]{3,2,1,0:T(8,128)(2,1)S(1)}, u32[]{:S(2)}, u32[]{:S(2)}) %all-to-all-start.1) | async-done | bytes 1048608 | tf_op jit(solution)/shard_map/all_to_all | solution.py:11
  64.8 3.6 %copy.28 = bf16[8,4,32,4,256]{4,3,2,1,0:T(4,128)(2,1)S(1)} copy(bf16[8,4,32,4,256]{4,2,0,3,1:T(8,128)(2,1)} %bitcast.97) | data formatting | bytes 4194304 | tf_op jit(solution)/shard_map/transpose | solution.py:52
  69.6 2.6 %fusion.3 = f32[1024,512]{1,0:T(8,128)} fusion(bf16[1024,1024]{1,0:T(8,128)(2,1)S(1)} %bitcast.91, bf16[1024,512]{1,0:T(8,128)(2,1)S(1)} %bitcast.102), kind=kOutput, calls=%fused_computation.38 | convolution fusion | flops 1073741824 | bytes 5242880 | tf_op jit(solution)/shard_map/dot_general | solution.py:53
  73.5 2.6 %copy.37 = bf16[1024,1024]{1,0:T(8,128)(2,1)} copy(bf16[1024,1024]{0,1:T(8,128)(2,1)S(1)} %bitcast.92) | data formatting | bytes 4194304 | tf_op jit(solution)/shard_map/dot_general | solution.py:67
  76.0 3.1 %fusion.4 = f32[4,256,2,256]{1,3,2,0:T(8,128)S(1)} fusion(bf16[4,256,1024,1]{2,1,3,0:T(8,128)(2,1)} %bitcast.98, bf16[2,256,1024,1]{2,1,0,3:T(8,128)(2,1)} %bitcast.104), kind=kOutput, calls=%fused_computation.39 | convolution fusion | flops 1073741824 | bytes 5242880 | tf_op jit(solution)/shard_map/dot_general | solution.py:67
  81.5 1.8 %collective-permute-start.4 = (f32[4,256,256]{1,2,0:T(8,128)}, f32[4,256,256]{1,2,0:T(8,128)S(1)}, u32[]{:S(2)}, u32[]{:S(2)}) collective-permute-start(f32[4,256,256]{1,2,0:T(8,128)} %slice_bitcast_fusion), channel_id=1, source_target_pairs={{0,1},{1,0},{2,3},{3,2},{4,5},{5,4},{6,7},{7,6},{8,9},{9,8},{10,11... | collective-permute-start | bytes 3145736 | tf_op jit(solution)/shard_map/ppermute | solution.py:69
  83.3 2.6 %convolution_convert_fusion = bf16[1024,1024]{1,0:T(8,128)(2,1)} fusion(bf16[1024,512]{1,0:T(8,128)(2,1)S(1)} %bitcast.96, bf16[1024,512]{1,0:T(8,128)(2,1)S(1)} %bitcast.103), kind=kOutput, calls=%fused_computation.1 | convolution fusion | flops 1074790400 | bytes 4194304 | tf_op jit(solution)/shard_map/dot_general | solution.py:61
  85.9 3.3 %reshape.81 = bf16[8,4,32,4,256]{4,3,2,1,0:T(4,128)(2,1)S(1)} reshape(bf16[1024,1024]{1,0:T(8,128)(2,1)} %convolution_convert_fusion) | data formatting | bytes 4194304 | tf_op jit(solution)/shard_map/reshape | solution.py:62
  89.3 1.7 %copy.30 = bf16[8,4,32,4,256]{4,2,0,3,1:T(8,128)(2,1)} copy(bf16[8,4,32,4,256]{4,3,2,1,0:T(4,128)(2,1)S(1)} %reshape.81) | data formatting | bytes 4194304 | tf_op jit(solution)/shard_map/reshape | solution.py:62
  91.0 4.4 %all-to-all-start.3 = ((bf16[16,256,256]{2,1,0:T(8,128)(2,1)}), bf16[16,256,256]{2,1,0:T(8,128)(2,1)S(1)}, u32[]{:S(2)}, u32[]{:S(2)}) async-start(bf16[16,256,256]{2,1,0:T(8,128)(2,1)} %bitcast.90), calls=%async_computation.4 | async-start | bytes 4194304 | tf_op jit(solution)/shard_map/all_to_all | solution.py:11
  96.9 2.7 %collective-permute-start.5 = (f32[256,256]{0,1:T(8,128)S(1)}, f32[256,256]{0,1:T(8,128)S(1)}, u32[]{:S(2)}, u32[]{:S(2)}) collective-permute-start(f32[256,256]{0,1:T(8,128)S(1)} %get-tuple-element.26), channel_id=1, source_target_pairs={{0,192},{64,0},{128,64},{192,128},{1,193},{65,1},{129,65},{193,129... | collective-permute-start | bytes 786440 | tf_op jit(solution)/shard_map/ppermute | solution.py:20
  100.7 24.3 %collective-permute-done.5 = f32[256,256]{0,1:T(8,128)S(1)} collective-permute-done((f32[256,256]{0,1:T(8,128)S(1)}, f32[256,256]{0,1:T(8,128)S(1)}, u32[]{:S(2)}, u32[]{:S(2)}) %collective-permute-start.5) | collective-permute-done | bytes 262176 | tf_op jit(solution)/shard_map/ppermute | solution.py:20
  125.0 2.0 %collective-permute-done.6 = f32[256,256]{0,1:T(8,128)S(1)} collective-permute-done((f32[256,256]{0,1:T(8,128)S(1)}, f32[256,256]{0,1:T(8,128)S(1)}, u32[]{:S(2)}, u32[]{:S(2)}) %collective-permute-start.6) | collective-permute-done | bytes 262176 | tf_op jit(solution)/shard_map/ppermute | solution.py:20
  127.1 5.6 %collective-permute-done.7 = f32[256,256]{0,1:T(8,128)S(1)} collective-permute-done((f32[256,256]{0,1:T(8,128)S(1)}, f32[256,256]{0,1:T(8,128)S(1)}, u32[]{:S(2)}, u32[]{:S(2)}) %collective-permute-start.7) | collective-permute-done | bytes 262176 | tf_op jit(solution)/shard_map/ppermute | solution.py:20
  134.6 1.6 %convert_bitcast_fusion = bf16[16,8,512]{2,1,0:T(8,128)(2,1)} fusion(f32[128,512]{1,0:T(8,128)} %reduce-scatter.2.cloned.1.call-done), kind=kLoop, calls=%fused_computation.29 | loop fusion | flops 65536 | bytes 393216 | tf_op jit(solution)/shard_map/reshape | solution.py:55
  136.3 4.5 %all-to-all-start.2 = ((bf16[16,8,512]{2,1,0:T(8,128)(2,1)}), bf16[16,8,512]{2,1,0:T(8,128)(2,1)S(1)}, u32[]{:S(2)}, u32[]{:S(2)}) async-start(bf16[16,8,512]{2,1,0:T(8,128)(2,1)} %convert_bitcast_fusion), calls=%async_computation.3 | async-start | bytes 262144 | tf_op jit(solution)/shard_map/all_to_all | solution.py:11
  141.4 6.1 %all-to-all-done.2 = bf16[16,8,512]{2,1,0:T(8,128)(2,1)S(1)} async-done(((bf16[16,8,512]{2,1,0:T(8,128)(2,1)}), bf16[16,8,512]{2,1,0:T(8,128)(2,1)S(1)}, u32[]{:S(2)}, u32[]{:S(2)}) %all-to-all-start.2) | async-done | bytes 131104 | tf_op jit(solution)/shard_map/all_to_all | solution.py:11
  (67 shorter events, 20.8 us)
Async XLA Ops:
  7.2 7.6 %copy-start.3 = (bf16[8,8192]{1,0:T(8,128)(2,1)S(1)}, bf16[8,8192]{1,0:T(8,128)(2,1)}, u32[]{:S(2)}) copy-start(bf16[8,8192]{1,0:T(8,128)(2,1)} %param.9) | copy-start | bytes 393220
  7.2 57.6 %all-gather.2.cloned.1.call-start = ((), (), s32[]{:S(2)}) async-start(), calls=%async_computation.5 | async-start | bytes 2228224 | tf_op jit(solution)/shard_map/all_gather | solution.py:38
  11.1 25.8 %collective-permute-start = (bf16[256,256]{1,0:T(8,128)(2,1)S(1)}, bf16[256,256]{1,0:T(8,128)(2,1)S(1)}, u32[]{:S(2)}, u32[]{:S(2)}) collective-permute-start(bf16[256,256]{1,0:T(8,128)(2,1)S(1)} %bitcast.109), channel_id=1, source_target_pairs={{0,192},{64,0},{128,64},{192,128},{1,193},{65,1},{129,65},{193,129... | collective-permute-start | bytes 393224 | tf_op jit(solution)/shard_map/ppermute | solution.py:20
  16.5 11.1 %all-to-all-start = ((bf16[16,8,512]{2,1,0:T(8,128)(2,1)}), bf16[16,8,512]{2,1,0:T(8,128)(2,1)S(1)}, u32[]{:S(2)}, u32[]{:S(2)}) async-start(bf16[16,8,512]{2,1,0:T(8,128)(2,1)} %reshape.72), calls=%async_computation | async-start | bytes 262144 | tf_op jit(solution)/shard_map/all_to_all | solution.py:11
  21.0 16.0 %collective-permute-start.1 = (bf16[256,256]{1,0:T(8,128)(2,1)S(1)}, bf16[256,256]{1,0:T(8,128)(2,1)S(1)}, u32[]{:S(2)}, u32[]{:S(2)}) collective-permute-start(bf16[256,256]{1,0:T(8,128)(2,1)S(1)} %bitcast.110), channel_id=1, source_target_pairs={{0,128},{64,192},{128,0},{192,64},{1,129},{65,193},{129,1},{193,65... | collective-permute-start | bytes 393224 | tf_op jit(solution)/shard_map/ppermute | solution.py:20
  24.0 13.0 %collective-permute-start.2 = (bf16[256,256]{1,0:T(8,128)(2,1)S(1)}, bf16[256,256]{1,0:T(8,128)(2,1)S(1)}, u32[]{:S(2)}, u32[]{:S(2)}) collective-permute-start(bf16[256,256]{1,0:T(8,128)(2,1)S(1)} %bitcast.111), channel_id=1, source_target_pairs={{0,64},{64,128},{128,192},{192,0},{1,65},{65,129},{129,193},{193,1... | collective-permute-start | bytes 393224 | tf_op jit(solution)/shard_map/ppermute | solution.py:20
  28.7 35.4 %all-to-all-start.1 = ((bf16[8,16,8,512]{3,2,1,0:T(8,128)(2,1)}), bf16[8,16,8,512]{3,2,1,0:T(8,128)(2,1)S(1)}, u32[]{:S(2)}, u32[]{:S(2)}) async-start(bf16[8,16,8,512]{3,2,1,0:T(8,128)(2,1)} %broadcast_in_dim.10), calls=%async_computation.1 | async-start | bytes 2097152 | tf_op jit(solution)/shard_map/all_to_all | solution.py:11
  36.9 97.8 %reduce-scatter.2.cloned.1.call-start = ((), (), s32[]{:S(2)}) async-start(), calls=%async_computation.6 | async-start | bytes 2359296 | tf_op jit(solution)/shard_map/reduce_scatter | solution.py:54
  37.1 4.3 %collective-permute-start.3 = (bf16[4,256,256]{2,1,0:T(8,128)(2,1)S(1)}, bf16[4,256,256]{2,1,0:T(8,128)(2,1)S(1)}, u32[]{:S(2)}, u32[]{:S(2)}) collective-permute-start(bf16[4,256,256]{2,1,0:T(8,128)(2,1)S(1)} %constant_dynamic-slice_fusion.1), channel_id=1, source_target_pairs={{0,1},{1,0},{2,3},{3,2},{4,5},{5,4},{6,7},{7,6},{8,9},{9,8},{10,11... | collective-permute-start | bytes 1572872 | tf_op jit(solution)/shard_map/ppermute | solution.py:48
  68.3 1.2 copy-start.1
  79.2 1.3 copy-start
  80.5 2.8 %copy-start.2 = (bf16[4,256,512]{2,1,0:T(8,128)(2,1)S(1)}, bf16[4,256,512]{2,1,0:T(8,128)(2,1)}, u32[]{:S(2)}) copy-start(bf16[4,256,512]{2,1,0:T(8,128)(2,1)} %pad_maximum_fusion) | copy-start | bytes 3145732
  81.5 13.9 %collective-permute-start.4 = (f32[4,256,256]{1,2,0:T(8,128)}, f32[4,256,256]{1,2,0:T(8,128)S(1)}, u32[]{:S(2)}, u32[]{:S(2)}) collective-permute-start(f32[4,256,256]{1,2,0:T(8,128)} %slice_bitcast_fusion), channel_id=1, source_target_pairs={{0,1},{1,0},{2,3},{3,2},{4,5},{5,4},{6,7},{7,6},{8,9},{9,8},{10,11... | collective-permute-start | bytes 3145736 | tf_op jit(solution)/shard_map/ppermute | solution.py:69
  91.0 43.3 %all-to-all-start.3 = ((bf16[16,256,256]{2,1,0:T(8,128)(2,1)}), bf16[16,256,256]{2,1,0:T(8,128)(2,1)S(1)}, u32[]{:S(2)}, u32[]{:S(2)}) async-start(bf16[16,256,256]{2,1,0:T(8,128)(2,1)} %bitcast.90), calls=%async_computation.4 | async-start | bytes 4194304 | tf_op jit(solution)/shard_map/all_to_all | solution.py:11
  96.9 28.1 %collective-permute-start.5 = (f32[256,256]{0,1:T(8,128)S(1)}, f32[256,256]{0,1:T(8,128)S(1)}, u32[]{:S(2)}, u32[]{:S(2)}) collective-permute-start(f32[256,256]{0,1:T(8,128)S(1)} %get-tuple-element.26), channel_id=1, source_target_pairs={{0,192},{64,0},{128,64},{192,128},{1,193},{65,1},{129,65},{193,129... | collective-permute-start | bytes 786440 | tf_op jit(solution)/shard_map/ppermute | solution.py:20
  99.6 27.5 %collective-permute-start.6 = (f32[256,256]{0,1:T(8,128)S(1)}, f32[256,256]{0,1:T(8,128)S(1)}, u32[]{:S(2)}, u32[]{:S(2)}) collective-permute-start(f32[256,256]{0,1:T(8,128)S(1)} %get-tuple-element.25), channel_id=1, source_target_pairs={{0,128},{64,192},{128,0},{192,64},{1,129},{65,193},{129,1},{193,65... | collective-permute-start | bytes 786440 | tf_op jit(solution)/shard_map/ppermute | solution.py:20
  100.1 32.6 %collective-permute-start.7 = (f32[256,256]{0,1:T(8,128)S(1)}, f32[256,256]{0,1:T(8,128)S(1)}, u32[]{:S(2)}, u32[]{:S(2)}) collective-permute-start(f32[256,256]{0,1:T(8,128)S(1)} %get-tuple-element.24), channel_id=1, source_target_pairs={{0,64},{64,128},{128,192},{192,0},{1,65},{65,129},{129,193},{193,1... | collective-permute-start | bytes 786440 | tf_op jit(solution)/shard_map/ppermute | solution.py:20
  136.3 11.2 %all-to-all-start.2 = ((bf16[16,8,512]{2,1,0:T(8,128)(2,1)}), bf16[16,8,512]{2,1,0:T(8,128)(2,1)S(1)}, u32[]{:S(2)}, u32[]{:S(2)}) async-start(bf16[16,8,512]{2,1,0:T(8,128)(2,1)} %convert_bitcast_fusion), calls=%async_computation.3 | async-start | bytes 262144 | tf_op jit(solution)/shard_map/all_to_all | solution.py:11
Sparse Core Ops, SparseCore 0:
  11.0 53.7 all-gather.1
  72.3 38.2 reduce-scatter.1

commit v3 on v1

v3 whole, which is shorter than its diff:
```python
import jax
import jax.numpy as jnp
from jax import lax
from jax.sharding import Mesh, PartitionSpec as P

BF = jnp.bfloat16
F32 = jnp.float32
XC = ("x", "c")


def exchange(v, axes):
    return lax.all_to_all(v, axes, split_axis=0, concat_axis=0, tiled=False)


def shift_y(v, s):
    n = lax.axis_size("y")
    return lax.ppermute(v, "y", [(i, (i + s) % n) for i in range(n)])


def shards(attn_out, head_mask, gate_scale, w_out, grad_out):
    ny, nz = lax.axis_size("y"), lax.axis_size("z")
    nxc = lax.axis_size("x") * lax.axis_size("c")
    me = lax.axis_index("y")
    t, r = attn_out.shape
    j, d = grad_out.shape
    n = d // nxc
    ty = t // ny
    gate_vals = head_mask.astype(F32) * gate_scale
    col_gate = jnp.repeat(gate_vals, r // gate_vals.shape[0])
    gated = (attn_out.astype(F32) * col_gate[None, :]).astype(BF).reshape(ny, ty, r)

    a_y = [lax.dynamic_index_in_dim(gated, (me + s) % ny, 0, keepdims=False) for s in range(ny)]
    a_y = [a_y[0]] + [shift_y(a_y[s], s) for s in range(1, ny)]
    a_y = jnp.concatenate(a_y, axis=1)
    a_all = lax.all_gather(a_y, XC, axis=0, tiled=True)

    w_all = [w_out] + [shift_y(w_out, s) for s in range(1, ny)]

    g = exchange(grad_out.reshape(j, nxc, n).transpose(1, 0, 2), XC)
    g = exchange(jnp.broadcast_to(g[None], (nz,) + g.shape), "z")

    a_all, g, w_all = lax.optimization_barrier((a_all, g, w_all))
    w = jnp.concatenate(w_all, axis=0)
    a = a_all.reshape(nxc, nz, j, ny * r).transpose(1, 0, 2, 3).reshape(nxc * nz * j, ny * r)
    g = g.reshape(nxc * nz * j, n)

    part = jnp.dot(a, w, preferred_element_type=F32).astype(BF)
    proj = exchange(part.reshape(nz, nxc, j, n), "z").astype(F32).sum(axis=0).astype(BF)
    proj = exchange(proj, XC)
    proj_out = proj.transpose(1, 0, 2).reshape(j, d)

    part, g = lax.optimization_barrier((part, g))
    back = lax.dot_general(g, w, (((1,), (1,)), ((), ())), preferred_element_type=F32)
    back = back.reshape(nz, nxc, j, ny * r).transpose(1, 0, 2, 3).reshape(nxc * ty, ny * r)
    back, g = lax.optimization_barrier((back, g))
    mine = lax.psum_scatter(back, XC, scatter_dimension=0, tiled=True)
    mine = [mine[:, s * r : (s + 1) * r] for s in range(ny)]
    mine = [mine[0]] + [shift_y(mine[s], -s) for s in range(1, ny)]
    ring = jnp.stack(mine + mine[:-1])
    mine = lax.dynamic_slice_in_dim(ring, (ny - me) % ny, ny, 0).reshape(t, r)
    grad_attn = (mine * col_gate[None, :]).astype(BF)

    gw = lax.dot_general(a, g, (((0,), (0,)), ((), ())), preferred_element_type=F32)
    gw = gw.reshape(ny, r, n)
    grad_w = gw[0]
    for s in range(1, ny):
        grad_w = grad_w + shift_y(gw[s].astype(BF), -s).astype(F32)
    return (proj_out, grad_attn, grad_w)


def solution(mesh):
    fine = Mesh(mesh.devices.reshape(4, 8, 4, 2), ("y", "z", "x", "c"))
    dp, head = XC, ("y", "z")
    return jax.shard_map(
        shards,
        mesh=fine,
        in_specs=(P(dp, head), P(head), P(head), P(head, dp), P(dp + head, None)),
        out_specs=(P(dp + head, None), P(dp, head), P(head, dp)),
        check_vma=False,
    )
```

time: 237 us -> 132 us (0.56)
  waiting for transfers between devices: 142 us -> 55.3 us
  local copies, waits for them, and re-layouts: 20.5 us -> 10.4 us
  blocking collectives: 9.55 us -> 0 us
  other arithmetic: 3.33 us -> 6.3 us
    all_to_all x6 -> x4, waiting for transfers between devices: 90.9 us -> 31 us  [exchange(): return lax.all_to_all(v, axes, split_axis=0, concat_axis=0, tiled=False)]
    all_gather x1, waiting for transfers between devices: 47.2 us -> 0.01 us  [shards(): a_all = lax.all_gather(a_y, XC, axis=0, tiled=True)]
    ppermute x2 -> x12, waiting for transfers between devices: 3.82 us -> 24.3 us  [shift_y(): return lax.ppermute(v, 'y', [(i, (i + s) % n) for i in range(n)])]
    all_to_all x6 -> x4, starting transfers between devices: 34.1 us -> 22.7 us  [exchange(): return lax.all_to_all(v, axes, split_axis=0, concat_axis=0, tiled=False)]
    ppermute x2 -> x12, starting transfers between devices: 5.45 us -> 15.4 us  [shift_y(): return lax.ppermute(v, 'y', [(i, (i + s) % n) for i in range(n)])]
    all_to_all x1 -> x0, blocking collectives: 9.55 us -> none  [exchange(): return lax.all_to_all(v, axes, split_axis=0, concat_axis=0, tiled=False)]
    reshape x8 -> x1, local copies, waits for them, and re-layouts: 8.68 us -> 1.49 us  [shards(): back.reshape(nz, nxc, j, ny * r).transpose(1, 0, 2, 3)]
  transfers between devices with their start and end apart: 9 -> 18, of which waited for: 9 -> 8; matrix products, arithmetic and copies ran while one was open for 4% -> 8% of each run, Pallas kernels for 0% -> 0%
where the time goes in v3:
time: 132 us; the launch traced here: 131 us
  waiting for transfers between devices  55.3 us (42%)
  starting transfers between devices  38.2 us (29%)
  between operations  14.2 us (11%)
  local copies, waits for them, and re-layouts  10.4 us (8%)
  matrix products  6.77 us (5%)
  other arithmetic  6.3 us (5%)
    all_to_all x4, waiting for transfers between devices, exchange(): return lax.all_to_all(v, axes, split_axis=0, concat_axis=0, tiled=False)  31 us
    ppermute x12, waiting for transfers between devices, shift_y(): return lax.ppermute(v, 'y', [(i, (i + s) % n) for i in range(n)])  24.3 us
    all_to_all x4, starting transfers between devices, exchange(): return lax.all_to_all(v, axes, split_axis=0, concat_axis=0, tiled=False)  22.7 us
    ppermute x12, starting transfers between devices, shift_y(): return lax.ppermute(v, 'y', [(i, (i + s) % n) for i in range(n)])  15.4 us
    unnamed x16, local copies, waits for them, and re-layouts  3.28 us
    dot_general x1, matrix products, shards(): lax.dot_general(a, g, (((0,), (0,)), ((), ())), preferred_element_type=F32)  3.24 us
  transfers between devices with their start and end apart: 18, of which 8 were waited for; matrix products, arithmetic and copies ran while one was open for 8% of the time, Pallas kernels for 0%

profile of v3, /device:TPU:1, one launch (start us, length us, event | category | flops | bytes accessed | tf_op | source)
XLA Modules:
  0.0 131.3 jit_solution(14200731419022160437)
XLA Ops:
  8.9 3.6 %collective-permute-start.2 = (bf16[64,256]{1,0:T(8,128)(2,1)S(1)}, bf16[64,256]{1,0:T(8,128)(2,1)S(1)}, u32[]{:S(2)}, u32[]{:S(2)}) collective-permute-start(bf16[64,256]{1,0:T(8,128)(2,1)S(1)} %get-tuple-element.28), channel_id=1, source_target_pairs={{0,192},{64,0},{128,64},{192,128},{1,193},{65,1},{129,65},{193,129... | collective-permute-start | bytes 98312 | tf_op jit(solution)/shard_map/ppermute | solution.py:17
  13.6 5.8 %all-to-all-start = ((bf16[8,8,1024]{2,1,0:T(8,128)(2,1)}), bf16[8,8,1024]{2,1,0:T(8,128)(2,1)S(1)}, u32[]{:S(2)}, u32[]{:S(2)}) async-start(bf16[8,8,1024]{2,1,0:T(8,128)(2,1)} %bitcast.61), calls=%async_computation | async-start | bytes 262144 | tf_op jit(solution)/shard_map/all_to_all | solution.py:12
  20.2 4.6 %all-to-all-done = bf16[8,8,1024]{2,1,0:T(8,128)(2,1)S(1)} async-done(((bf16[8,8,1024]{2,1,0:T(8,128)(2,1)}), bf16[8,8,1024]{2,1,0:T(8,128)(2,1)S(1)}, u32[]{:S(2)}, u32[]{:S(2)}) %all-to-all-start) | async-done | bytes 131104 | tf_op jit(solution)/shard_map/all_to_all | solution.py:12
  24.7 1.1 broadcast_in_dim.10
  25.8 8.2 %all-to-all-start.1 = ((bf16[8,8,8,1024]{3,2,1,0:T(8,128)(2,1)}), bf16[8,8,8,1024]{3,2,1,0:T(8,128)(2,1)S(1)}, u32[]{:S(2)}, u32[]{:S(2)}) async-start(bf16[8,8,8,1024]{3,2,1,0:T(8,128)(2,1)} %broadcast_in_dim.10), calls=%async_computation.1 | async-start | bytes 2097152 | tf_op jit(solution)/shard_map/all_to_all | solution.py:12
  34.0 1.7 %collective-permute-start.4 = (bf16[256,1024]{1,0:T(8,128)(2,1)S(1)}, bf16[256,1024]{1,0:T(8,128)(2,1)S(1)}, u32[]{:S(2)}, u32[]{:S(2)}) collective-permute-start(bf16[256,1024]{1,0:T(8,128)(2,1)S(1)} %copy-done), channel_id=1, source_target_pairs={{0,128},{64,192},{128,0},{192,64},{1,129},{65,193},{129,1},{193,65... | collective-permute-start | bytes 1572872 | tf_op jit(solution)/shard_map/ppermute | solution.py:17
  36.7 1.8 %collective-permute-start.5 = (bf16[256,1024]{1,0:T(8,128)(2,1)S(1)}, bf16[256,1024]{1,0:T(8,128)(2,1)}, u32[]{:S(2)}, u32[]{:S(2)}) collective-permute-start(bf16[256,1024]{1,0:T(8,128)(2,1)S(1)} %copy-done), channel_id=1, source_target_pairs={{0,192},{64,0},{128,64},{192,128},{1,193},{65,1},{129,65},{193,129... | collective-permute-start | bytes 1572872 | tf_op jit(solution)/shard_map/ppermute | solution.py:17
  38.5 9.5 %collective-permute-done.4 = bf16[256,1024]{1,0:T(8,128)(2,1)S(1)} collective-permute-done((bf16[256,1024]{1,0:T(8,128)(2,1)S(1)}, bf16[256,1024]{1,0:T(8,128)(2,1)S(1)}, u32[]{:S(2)}, u32[]{:S(2)}) %collective-permute-start.4) | collective-permute-done | bytes 524320 | tf_op jit(solution)/shard_map/ppermute | solution.py:17
  48.0 12.8 %collective-permute-done.3 = bf16[256,1024]{1,0:T(8,128)(2,1)S(1)} collective-permute-done((bf16[256,1024]{1,0:T(8,128)(2,1)S(1)}, bf16[256,1024]{1,0:T(8,128)(2,1)S(1)}, u32[]{:S(2)}, u32[]{:S(2)}) %collective-permute-start.3) | collective-permute-done | bytes 524320 | tf_op jit(solution)/shard_map/ppermute | solution.py:17
  61.5 1.7 %all-to-all-done.1 = bf16[8,8,8,1024]{3,2,1,0:T(8,128)(2,1)S(1)} async-done(((bf16[8,8,8,1024]{3,2,1,0:T(8,128)(2,1)}), bf16[8,8,8,1024]{3,2,1,0:T(8,128)(2,1)S(1)}, u32[]{:S(2)}, u32[]{:S(2)}) %all-to-all-start.1) | async-done | bytes 1048608 | tf_op jit(solution)/shard_map/all_to_all | solution.py:12
  63.2 1.4 %copy.9 = bf16[8,8,8,1024]{3,2,1,0:T(8,128)(2,1)S(1)} copy(bf16[8,8,8,1024]{3,2,0,1:T(8,128)(2,1)} %bitcast.58) | data formatting | bytes 2097152 | tf_op jit(solution)/shard_map/transpose | solution.py:44
  65.8 2.2 %convolution_convert_fusion = bf16[512,1024]{1,0:T(8,128)(2,1)} fusion(bf16[512,1024]{1,0:T(8,128)(2,1)S(1)} %bitcast.52, bf16[1024,1024]{1,0:T(8,128)(2,1)S(1)} %constant_dynamic-update-slice_fusion), kind=kOutput, calls=%fused_computation | convolution fusion | flops 1074266112 | bytes 4194304 | tf_op jit(solution)/shard_map/dot_general | solution.py:47
  68.0 1.3 fusion.8
  69.3 1.5 %copy.10 = f32[8,8,8,1024]{3,2,0,1:T(8,128)} copy(f32[8,8,8,1024]{3,2,1,0:T(8,128)S(1)} %bitcast.56) | data formatting | bytes 4194304 | tf_op jit(solution)/shard_map/reshape | solution.py:54
  70.8 5.0 %all-to-all-start.2 = ((bf16[8,8,8,1024]{3,2,1,0:T(8,128)(2,1)}), bf16[8,8,8,1024]{3,2,1,0:T(8,128)(2,1)S(1)}, u32[]{:S(2)}, u32[]{:S(2)}) async-start(bf16[8,8,8,1024]{3,2,1,0:T(8,128)(2,1)} %bitcast.57), calls=%async_computation.2 | async-start | bytes 2097152 | tf_op jit(solution)/shard_map/all_to_all | solution.py:12
  75.8 3.2 %fusion.7 = (bf16[1024,1024]{1,0:T(8,128)(2,1)S(1)}, f32[1024,1024]{1,0:T(8,128)}) fusion(bf16[512,1024]{1,0:T(8,128)(2,1)S(1)} %bitcast.53, bf16[512,1024]{1,0:T(8,128)(2,1)S(1)} %bitcast.55), kind=kOutput, calls=%fused_computation.29 | convolution fusion | flops 1074790400 | bytes 8388608 | tf_op jit(solution)/shard_map/dot_general | solution.py:63
  80.1 1.3 collective-permute-start.9
  81.6 1.4 %collective-permute-start.10 = (bf16[256,1024]{1,0:T(8,128)(2,1)S(1)}, bf16[256,1024]{1,0:T(8,128)(2,1)S(1)}, u32[]{:S(2)}, u32[]{:S(2)}) collective-permute-start(bf16[256,1024]{1,0:T(8,128)(2,1)S(1)} %get-tuple-element.23), channel_id=1, source_target_pairs={{0,128},{64,192},{128,0},{192,64},{1,129},{65,193},{129,1},{193,65... | collective-permute-start | bytes 1572872 | tf_op jit(solution)/shard_map/ppermute | solution.py:17
  83.0 22.1 %all-to-all-done.2 = bf16[8,8,8,1024]{3,2,1,0:T(8,128)(2,1)S(1)} async-done(((bf16[8,8,8,1024]{3,2,1,0:T(8,128)(2,1)}), bf16[8,8,8,1024]{3,2,1,0:T(8,128)(2,1)S(1)}, u32[]{:S(2)}, u32[]{:S(2)}) %all-to-all-start.2) | async-done | bytes 1048608 | tf_op jit(solution)/shard_map/all_to_all | solution.py:12
  105.9 3.8 %all-to-all-start.3 = ((bf16[8,8,1024]{2,1,0:T(8,128)(2,1)}), bf16[8,8,1024]{2,1,0:T(8,128)(2,1)S(1)}, u32[]{:S(2)}, u32[]{:S(2)}) async-start(bf16[8,8,1024]{2,1,0:T(8,128)(2,1)} %reduce_sum.12), calls=%async_computation.3 | async-start | bytes 262144 | tf_op jit(solution)/shard_map/all_to_all | solution.py:12
  109.7 2.5 %fusion.1 = f32[256,1024]{1,0:T(8,128)} fusion(f32[1024,1024]{1,0:T(8,128)} %get-tuple-element.32, bf16[256,1024]{1,0:T(8,128)(2,1)S(1)} %collective-permute-done.11, bf16[256,1024]{1,0:T(8,128)(2,1)S(1)} %collective-permute-done.10, bf16[256,1024]{1,0:T(8,128)(2,1)S(1)} %collective-permute-done.9), kind=kLoop, calls=%fused_computation.3 | loop fusion | flops 1572864 | bytes 3670016 | tf_op jit(solution)/shard_map/add | solution.py:67
  112.2 2.8 %all-to-all-done.3 = bf16[8,8,1024]{2,1,0:T(8,128)(2,1)S(1)} async-done(((bf16[8,8,1024]{2,1,0:T(8,128)(2,1)}), bf16[8,8,1024]{2,1,0:T(8,128)(2,1)S(1)}, u32[]{:S(2)}, u32[]{:S(2)}) %all-to-all-start.3) | async-done | bytes 131104 | tf_op jit(solution)/shard_map/all_to_all | solution.py:12
  116.8 1.6 %collective-permute-start.7 = (f32[64,256]{1,0:T(8,128)S(1)}, f32[64,256]{1,0:T(8,128)S(1)}, u32[]{:S(2)}, u32[]{:S(2)}) collective-permute-start(f32[64,256]{1,0:T(8,128)S(1)} %get-tuple-element.25), channel_id=1, source_target_pairs={{0,128},{64,192},{128,0},{192,64},{1,129},{65,193},{129,1},{193,65... | collective-permute-start | bytes 196616 | tf_op jit(solution)/shard_map/ppermute | solution.py:17
  120.2 1.6 %collective-permute-done.6 = f32[64,256]{1,0:T(8,128)S(1)} collective-permute-done((f32[64,256]{1,0:T(8,128)S(1)}, f32[64,256]{1,0:T(8,128)S(1)}, u32[]{:S(2)}, u32[]{:S(2)}) %collective-permute-start.6) | collective-permute-done | bytes 65568 | tf_op jit(solution)/shard_map/ppermute | solution.py:17
  (49 shorter events, 14.8 us)
Async XLA Ops:
  8.9 25.1 %copy-start = (bf16[256,1024]{1,0:T(8,128)(2,1)S(1)}, bf16[256,1024]{1,0:T(8,128)(2,1)}, u32[]{:S(2)}) copy-start(bf16[256,1024]{1,0:T(8,128)(2,1)} %param.8) | copy-start | bytes 1572868
  8.9 10.5 %collective-permute-start.2 = (bf16[64,256]{1,0:T(8,128)(2,1)S(1)}, bf16[64,256]{1,0:T(8,128)(2,1)S(1)}, u32[]{:S(2)}, u32[]{:S(2)}) collective-permute-start(bf16[64,256]{1,0:T(8,128)(2,1)S(1)} %get-tuple-element.28), channel_id=1, source_target_pairs={{0,192},{64,0},{128,64},{192,128},{1,193},{65,1},{129,65},{193,129... | collective-permute-start | bytes 98312 | tf_op jit(solution)/shard_map/ppermute | solution.py:17
  12.6 6.9 %collective-permute-start.1 = (bf16[64,256]{1,0:T(8,128)(2,1)S(1)}, bf16[64,256]{1,0:T(8,128)(2,1)S(1)}, u32[]{:S(2)}, u32[]{:S(2)}) collective-permute-start(bf16[64,256]{1,0:T(8,128)(2,1)S(1)} %get-tuple-element.29), channel_id=1, source_target_pairs={{0,128},{64,192},{128,0},{192,64},{1,129},{65,193},{129,1},{193,65... | collective-permute-start | bytes 98312 | tf_op jit(solution)/shard_map/ppermute | solution.py:17
  12.9 6.5 %collective-permute-start = (bf16[64,256]{1,0:T(8,128)(2,1)S(1)}, bf16[64,256]{1,0:T(8,128)(2,1)S(1)}, u32[]{:S(2)}, u32[]{:S(2)}) collective-permute-start(bf16[64,256]{1,0:T(8,128)(2,1)S(1)} %get-tuple-element.30), channel_id=1, source_target_pairs={{0,64},{64,128},{128,192},{192,0},{1,65},{65,129},{129,193},{193,1... | collective-permute-start | bytes 98312 | tf_op jit(solution)/shard_map/ppermute | solution.py:17
  13.6 11.1 %all-to-all-start = ((bf16[8,8,1024]{2,1,0:T(8,128)(2,1)}), bf16[8,8,1024]{2,1,0:T(8,128)(2,1)S(1)}, u32[]{:S(2)}, u32[]{:S(2)}) async-start(bf16[8,8,1024]{2,1,0:T(8,128)(2,1)} %bitcast.61), calls=%async_computation | async-start | bytes 262144 | tf_op jit(solution)/shard_map/all_to_all | solution.py:12
  19.4 42.1 %all-gather.2.cloned.1.call-start = ((), (), s32[]{:S(2)}) async-start(), calls=%async_computation.5 | async-start | bytes 1179648 | tf_op jit(solution)/shard_map/all_gather | solution.py:35
  25.8 37.4 %all-to-all-start.1 = ((bf16[8,8,8,1024]{3,2,1,0:T(8,128)(2,1)}), bf16[8,8,8,1024]{3,2,1,0:T(8,128)(2,1)S(1)}, u32[]{:S(2)}, u32[]{:S(2)}) async-start(bf16[8,8,8,1024]{3,2,1,0:T(8,128)(2,1)} %broadcast_in_dim.10), calls=%async_computation.1 | async-start | bytes 2097152 | tf_op jit(solution)/shard_map/all_to_all | solution.py:12
  34.0 80.9 %reduce-scatter.2.cloned.1.call-start = ((), (), s32[]{:S(2)}) async-start(), calls=%async_computation.6 | async-start | bytes 2359296 | tf_op jit(solution)/shard_map/reduce_scatter | solution.py:56
  34.0 13.9 %collective-permute-start.4 = (bf16[256,1024]{1,0:T(8,128)(2,1)S(1)}, bf16[256,1024]{1,0:T(8,128)(2,1)S(1)}, u32[]{:S(2)}, u32[]{:S(2)}) collective-permute-start(bf16[256,1024]{1,0:T(8,128)(2,1)S(1)} %copy-done), channel_id=1, source_target_pairs={{0,128},{64,192},{128,0},{192,64},{1,129},{65,193},{129,1},{193,65... | collective-permute-start | bytes 1572872 | tf_op jit(solution)/shard_map/ppermute | solution.py:17
  35.8 24.9 %collective-permute-start.3 = (bf16[256,1024]{1,0:T(8,128)(2,1)S(1)}, bf16[256,1024]{1,0:T(8,128)(2,1)S(1)}, u32[]{:S(2)}, u32[]{:S(2)}) collective-permute-start(bf16[256,1024]{1,0:T(8,128)(2,1)S(1)} %copy-done), channel_id=1, source_target_pairs={{0,64},{64,128},{128,192},{192,0},{1,65},{65,129},{129,193},{193,1... | collective-permute-start | bytes 1572872 | tf_op jit(solution)/shard_map/ppermute | solution.py:17
  36.7 24.8 %collective-permute-start.5 = (bf16[256,1024]{1,0:T(8,128)(2,1)S(1)}, bf16[256,1024]{1,0:T(8,128)(2,1)}, u32[]{:S(2)}, u32[]{:S(2)}) collective-permute-start(bf16[256,1024]{1,0:T(8,128)(2,1)S(1)} %copy-done), channel_id=1, source_target_pairs={{0,192},{64,0},{128,64},{192,128},{1,193},{65,1},{129,65},{193,129... | collective-permute-start | bytes 1572872 | tf_op jit(solution)/shard_map/ppermute | solution.py:17
  60.7 0.8 copy-start.1
  63.2 1.4 %copy-start.2 = (bf16[256,1024]{1,0:T(8,128)(2,1)S(1)}, bf16[256,1024]{1,0:T(8,128)(2,1)}, u32[]{:S(2)}) copy-start(bf16[256,1024]{1,0:T(8,128)(2,1)} %copy-done.1) | copy-start | bytes 1572868
  70.8 34.2 %all-to-all-start.2 = ((bf16[8,8,8,1024]{3,2,1,0:T(8,128)(2,1)}), bf16[8,8,8,1024]{3,2,1,0:T(8,128)(2,1)S(1)}, u32[]{:S(2)}, u32[]{:S(2)}) async-start(bf16[8,8,8,1024]{3,2,1,0:T(8,128)(2,1)} %bitcast.57), calls=%async_computation.2 | async-start | bytes 2097152 | tf_op jit(solution)/shard_map/all_to_all | solution.py:12
  80.1 29.5 %collective-permute-start.9 = (bf16[256,1024]{1,0:T(8,128)(2,1)}, bf16[256,1024]{1,0:T(8,128)(2,1)S(1)}, u32[]{:S(2)}, u32[]{:S(2)}) collective-permute-start(bf16[256,1024]{1,0:T(8,128)(2,1)} %get-tuple-element.21), channel_id=1, source_target_pairs={{0,192},{64,0},{128,64},{192,128},{1,193},{65,1},{129,65},{193,129... | collective-permute-start | bytes 1572872 | tf_op jit(solution)/shard_map/ppermute | solution.py:17
  81.4 28.2 %collective-permute-start.11 = (bf16[256,1024]{1,0:T(8,128)(2,1)}, bf16[256,1024]{1,0:T(8,128)(2,1)S(1)}, u32[]{:S(2)}, u32[]{:S(2)}) collective-permute-start(bf16[256,1024]{1,0:T(8,128)(2,1)} %get-tuple-element.22), channel_id=1, source_target_pairs={{0,64},{64,128},{128,192},{192,0},{1,65},{65,129},{129,193},{193,1... | collective-permute-start | bytes 1572872 | tf_op jit(solution)/shard_map/ppermute | solution.py:17
  81.6 28.1 %collective-permute-start.10 = (bf16[256,1024]{1,0:T(8,128)(2,1)S(1)}, bf16[256,1024]{1,0:T(8,128)(2,1)S(1)}, u32[]{:S(2)}, u32[]{:S(2)}) collective-permute-start(bf16[256,1024]{1,0:T(8,128)(2,1)S(1)} %get-tuple-element.23), channel_id=1, source_target_pairs={{0,128},{64,192},{128,0},{192,64},{1,129},{65,193},{129,1},{193,65... | collective-permute-start | bytes 1572872 | tf_op jit(solution)/shard_map/ppermute | solution.py:17
  105.9 9.1 %all-to-all-start.3 = ((bf16[8,8,1024]{2,1,0:T(8,128)(2,1)}), bf16[8,8,1024]{2,1,0:T(8,128)(2,1)S(1)}, u32[]{:S(2)}, u32[]{:S(2)}) async-start(bf16[8,8,1024]{2,1,0:T(8,128)(2,1)} %reduce_sum.12), calls=%async_computation.3 | async-start | bytes 262144 | tf_op jit(solution)/shard_map/all_to_all | solution.py:12
  115.9 6.3 %collective-permute-start.8 = (f32[64,256]{1,0:T(8,128)S(1)}, f32[64,256]{1,0:T(8,128)S(1)}, u32[]{:S(2)}, u32[]{:S(2)}) collective-permute-start(f32[64,256]{1,0:T(8,128)S(1)} %get-tuple-element.24), channel_id=1, source_target_pairs={{0,64},{64,128},{128,192},{192,0},{1,65},{65,129},{129,193},{193,1... | collective-permute-start | bytes 196616 | tf_op jit(solution)/shard_map/ppermute | solution.py:17
  116.8 5.3 %collective-permute-start.7 = (f32[64,256]{1,0:T(8,128)S(1)}, f32[64,256]{1,0:T(8,128)S(1)}, u32[]{:S(2)}, u32[]{:S(2)}) collective-permute-start(f32[64,256]{1,0:T(8,128)S(1)} %get-tuple-element.25), channel_id=1, source_target_pairs={{0,128},{64,192},{128,0},{192,64},{1,129},{65,193},{129,1},{193,65... | collective-permute-start | bytes 196616 | tf_op jit(solution)/shard_map/ppermute | solution.py:17
  118.4 3.4 %collective-permute-start.6 = (f32[64,256]{1,0:T(8,128)S(1)}, f32[64,256]{1,0:T(8,128)S(1)}, u32[]{:S(2)}, u32[]{:S(2)}) collective-permute-start(f32[64,256]{1,0:T(8,128)S(1)} %get-tuple-element.26), channel_id=1, source_target_pairs={{0,192},{64,0},{128,64},{192,128},{1,193},{65,1},{129,65},{193,129... | collective-permute-start | bytes 196616 | tf_op jit(solution)/shard_map/ppermute | solution.py:17
Sparse Core Ops, SparseCore 0:
  22.7 28.1 all-gather.1
  71.0 30.3 reduce-scatter.1

commit v4 on v3

v4 whole, which is shorter than its diff:
```python
import jax
import jax.numpy as jnp
from jax import lax
from jax.sharding import Mesh, PartitionSpec as P

BF = jnp.bfloat16
F32 = jnp.float32
XC = ("x", "c")


def exchange(v, axes):
    return lax.all_to_all(v, axes, split_axis=0, concat_axis=0, tiled=False)


def shift(v, axis, s):
    n = lax.axis_size(axis)
    return lax.ppermute(v, axis, [(i, (i + s) % n) for i in range(n)])


def relative(v):
    nx = v.shape[0]
    ring = jnp.concatenate([v[::-1], v[::-1]])
    v = lax.dynamic_slice_in_dim(ring, nx - 1 - lax.axis_index("x"), nx, 0)
    return jnp.where(lax.axis_index("c") == 0, v, v[:, ::-1])


def shards(attn_out, head_mask, gate_scale, w_out, grad_out):
    nx, ny, nz, nc = (lax.axis_size(a) for a in "xyzc")
    me = lax.axis_index("y")
    t, r = attn_out.shape
    j, d = grad_out.shape
    n = d // (nx * nc)
    ty = t // ny
    half = r // 2

    g = exchange(grad_out.reshape(j, nx * nc, n).transpose(1, 0, 2), XC)
    g = relative(g.reshape(nx, nc, j, n)).transpose(1, 0, 2, 3)

    gate_vals = head_mask.astype(F32) * gate_scale
    col_gate = jnp.repeat(gate_vals, r // gate_vals.shape[0])
    gated = (attn_out.astype(F32) * col_gate[None, :]).astype(BF).reshape(ny, ty, r)

    a = [lax.dynamic_index_in_dim(gated, (me + s) % ny, 0, keepdims=False) for s in range(ny)]
    a = [a[0]] + [shift(a[s], "y", s) for s in range(1, ny)]
    a = jnp.concatenate(a, axis=1)
    a, g = lax.optimization_barrier((a, g.reshape(nc * nx * j, n)))
    g = lax.all_gather(g, "z", axis=0, tiled=True)
    a = jnp.stack([a] + [shift(a, "x", s) for s in range(1, nx)])
    a = jnp.stack([a, shift(a, "c", 1)])

    w1, w3 = shift(w_out, "y", 1), shift(w_out, "y", -1)
    w2 = [shift(w1[:half], "y", 1), shift(w3[half:], "y", -1)]
    a, w = lax.optimization_barrier((a, [w_out, w1, *w2, w3]))
    w = jnp.concatenate(w, axis=0)
    a = a.reshape(nc * nx, nz, j, ny * r).transpose(1, 0, 2, 3).reshape(nx * nc * ty, ny * r)

    part = jnp.dot(a, w, preferred_element_type=F32).astype(BF)
    proj = exchange(part.reshape(nz, nc, nx, j, n), "z").astype(F32).sum(axis=0).astype(BF)
    proj = relative(proj.transpose(1, 0, 2, 3)).reshape(nx * nc, j, n)
    proj = exchange(proj, XC)
    proj_out = proj.transpose(1, 0, 2).reshape(j, d)

    back = lax.dot_general(g, w, (((1,), (1,)), ((), ())), preferred_element_type=F32)
    back = back.reshape(nz, nc, nx, j, ny * r).transpose(1, 2, 0, 3, 4)
    own = back[0] + shift(back[1].astype(BF), "c", 1).astype(F32)
    mine = own[0]
    for s in range(1, nx):
        mine = mine + shift(own[s].astype(BF), "x", -s).astype(F32)
    mine = mine.reshape(ty, ny * r)
    mine = [mine[:, s * r : (s + 1) * r] for s in range(ny)]
    mine = [mine[0]] + [shift(mine[s], "y", -s) for s in range(1, ny)]
    ring = jnp.stack(mine + mine[:-1])
    mine = lax.dynamic_slice_in_dim(ring, (ny - me) % ny, ny, 0).reshape(t, r)
    grad_attn = (mine * col_gate[None, :]).astype(BF)

    back, g = lax.optimization_barrier((back, g))
    gw = lax.dot_general(a, g, (((0,), (0,)), ((), ())), preferred_element_type=F32)
    gw = gw.reshape(ny, 2, half, n)
    near = gw[1].at[0].add(shift(gw[2, 0].astype(BF), "y", -1).astype(F32))
    far = gw[3].at[1].add(shift(gw[2, 1].astype(BF), "y", 1).astype(F32))
    near, far = shift(near.astype(BF), "y", -1), shift(far.astype(BF), "y", 1)
    grad_w = (gw[0] + near.astype(F32) + far.astype(F32)).reshape(r, n)
    return (proj_out, grad_attn, grad_w)


def solution(mesh):
    fine = Mesh(mesh.devices.reshape(4, 8, 4, 2), ("y", "z", "x", "c"))
    dp, head = XC, ("y", "z")
    return jax.shard_map(
        shards,
        mesh=fine,
        in_specs=(P(dp, head), P(head), P(head), P(head, dp), P(dp + head, None)),
        out_specs=(P(dp + head, None), P(dp, head), P(head, dp)),
        check_vma=False,
    )
```

time: 132 us -> 125 us (0.947)
  waiting for transfers between devices: 55.3 us -> 26.8 us
  starting transfers between devices: 38.2 us -> 54.1 us
  local copies, waits for them, and re-layouts: 10.4 us -> 15.4 us
    all_to_all x4 -> x3, waiting for transfers between devices: 31 us -> 5.23 us  [exchange(): return lax.all_to_all(v, axes, split_axis=0, concat_axis=0, tiled=False)]
    ppermute x12 -> x22, starting transfers between devices: 15.4 us -> 33 us  [shift(): return lax.ppermute(v, axis, [(i, (i + s) % n) for i in range(n)])]
    ppermute x12 -> x22, waiting for transfers between devices: 24.3 us -> 16.5 us  [shift(): return lax.ppermute(v, axis, [(i, (i + s) % n) for i in range(n)])]
    unnamed x16 -> x23, local copies, waits for them, and re-layouts: 3.28 us -> 9.32 us
    all_gather x1, waiting for transfers between devices: 0.01 us -> 5.12 us  [shards(): g = lax.all_gather(g, 'z', axis=0, tiled=True)]
    dot_general x1, matrix products: 1.29 us -> 3.28 us  [shards(): lax.dot_general(g, w, (((1,), (1,)), ((), ())), preferred_element_type=F32)]
    dot_general x1, matrix products: 3.24 us -> 1.32 us  [shards(): lax.dot_general(a, g, (((0,), (0,)), ((), ())), preferred_element_type=F32)]
    all_to_all x4 -> x3, starting transfers between devices: 22.7 us -> 21.1 us  [exchange(): return lax.all_to_all(v, axes, split_axis=0, concat_axis=0, tiled=False)]
  transfers between devices with their start and end apart: 18 -> 26, of which waited for: 8 -> 10; matrix products, arithmetic and copies ran while one was open for 8% -> 18% of each run, Pallas kernels for 0% -> 0%
where the time goes in v4:
time: 125 us; the launch traced here: 123 us
  starting transfers between devices  54.1 us (43%)
  waiting for transfers between devices  26.8 us (21%)
  local copies, waits for them, and re-layouts  15.4 us (12%)
  between operations  14.3 us (11%)
  matrix products  6.85 us (5%)
  other arithmetic  5.94 us (5%)
    ppermute x22, starting transfers between devices, shift(): return lax.ppermute(v, axis, [(i, (i + s) % n) for i in range(n)])  33 us
    all_to_all x3, starting transfers between devices, exchange(): return lax.all_to_all(v, axes, split_axis=0, concat_axis=0, tiled=False)  21.1 us
    ppermute x22, waiting for transfers between devices, shift(): return lax.ppermute(v, axis, [(i, (i + s) % n) for i in range(n)])  16.5 us
    unnamed x23, local copies, waits for them, and re-layouts  9.32 us
    all_to_all x3, waiting for transfers between devices, exchange(): return lax.all_to_all(v, axes, split_axis=0, concat_axis=0, tiled=False)  5.23 us
    all_gather x1, waiting for transfers between devices, shards(): g = lax.all_gather(g, 'z', axis=0, tiled=True)  5.12 us
    dot_general x1, matrix products, shards(): lax.dot_general(g, w, (((1,), (1,)), ((), ())), preferred_element_type=F32)  3.28 us
  transfers between devices with their start and end apart: 26, of which 10 were waited for; matrix products, arithmetic and copies ran while one was open for 18% of the time, Pallas kernels for 0%

profile of v4, /device:TPU:1, one launch (start us, length us, event | category | flops | bytes accessed | tf_op | source)
XLA Modules:
  0.0 123.5 jit_solution(1273256435222813369)
XLA Ops:
  9.0 3.6 %collective-permute-start.2 = (bf16[64,256]{1,0:T(8,128)(2,1)S(1)}, bf16[64,256]{1,0:T(8,128)(2,1)S(1)}, u32[]{:S(2)}, u32[]{:S(2)}) collective-permute-start(bf16[64,256]{1,0:T(8,128)(2,1)S(1)} %get-tuple-element.62), channel_id=1, source_target_pairs={{0,192},{64,0},{128,64},{192,128},{1,193},{65,1},{129,65},{193,129... | collective-permute-start | bytes 98312 | tf_op jit(solution)/shard_map/ppermute | solution.py:17
  13.7 5.8 %all-to-all-start = ((bf16[8,8,1024]{2,1,0:T(8,128)(2,1)}), bf16[8,8,1024]{2,1,0:T(8,128)(2,1)S(1)}, u32[]{:S(2)}, u32[]{:S(2)}) async-start(bf16[8,8,1024]{2,1,0:T(8,128)(2,1)} %bitcast.130), calls=%async_computation | async-start | bytes 262144 | tf_op jit(solution)/shard_map/all_to_all | solution.py:12
  19.5 5.2 %all-to-all-done = bf16[8,8,1024]{2,1,0:T(8,128)(2,1)S(1)} async-done(((bf16[8,8,1024]{2,1,0:T(8,128)(2,1)}), bf16[8,8,1024]{2,1,0:T(8,128)(2,1)S(1)}, u32[]{:S(2)}, u32[]{:S(2)}) %all-to-all-start) | async-done | bytes 131104 | tf_op jit(solution)/shard_map/all_to_all | solution.py:12
  27.7 1.7 %collective-permute-start.7 = (bf16[256,1024]{1,0:T(8,128)(2,1)S(1)}, bf16[256,1024]{1,0:T(8,128)(2,1)S(1)}, u32[]{:S(2)}, u32[]{:S(2)}) collective-permute-start(bf16[256,1024]{1,0:T(8,128)(2,1)S(1)} %copy-done.1), channel_id=1, source_target_pairs={{0,64},{64,128},{128,192},{192,0},{1,65},{65,129},{129,193},{193,1... | collective-permute-start | bytes 1572872 | tf_op jit(solution)/shard_map/ppermute | solution.py:17
  31.8 3.6 %collective-permute-done.3 = bf16[64,1024]{1,0:T(8,128)(2,1)S(1)} collective-permute-done((bf16[64,1024]{1,0:T(8,128)(2,1)S(1)}, bf16[64,1024]{1,0:T(8,128)(2,1)S(1)}, u32[]{:S(2)}, u32[]{:S(2)}) %collective-permute-start.3) | collective-permute-done | bytes 131104 | tf_op jit(solution)/shard_map/ppermute | solution.py:17
  36.8 4.1 %collective-permute-done.7 = bf16[256,1024]{1,0:T(8,128)(2,1)S(1)} collective-permute-done((bf16[256,1024]{1,0:T(8,128)(2,1)S(1)}, bf16[256,1024]{1,0:T(8,128)(2,1)S(1)}, u32[]{:S(2)}, u32[]{:S(2)}) %collective-permute-start.7) | collective-permute-done | bytes 524320 | tf_op jit(solution)/shard_map/ppermute | solution.py:17
  42.1 2.4 %collective-permute-start.10 = (bf16[128,1024]{1,0:T(8,128)(2,1)S(1)}, bf16[128,1024]{1,0:T(8,128)(2,1)S(1)}, u32[]{:S(2)}, u32[]{:S(2)}) collective-permute-start(bf16[128,1024]{1,0:T(8,128)(2,1)S(1)} %slice.128), channel_id=1, source_target_pairs={{0,192},{64,0},{128,64},{192,128},{1,193},{65,1},{129,65},{193,129... | collective-permute-start | bytes 786440 | tf_op jit(solution)/shard_map/ppermute | solution.py:17
  44.5 3.8 %collective-permute-done.8 = bf16[128,1024]{1,0:T(8,128)(2,1)S(1)} collective-permute-done((bf16[128,1024]{1,0:T(8,128)(2,1)}, bf16[128,1024]{1,0:T(8,128)(2,1)S(1)}, u32[]{:S(2)}, u32[]{:S(2)}) %collective-permute-start.8) | collective-permute-done | bytes 262176 | tf_op jit(solution)/shard_map/ppermute | solution.py:17
  50.0 2.2 %convolution_convert_fusion = bf16[512,1024]{1,0:T(8,128)(2,1)} fusion(bf16[512,1024]{1,0:T(8,128)(2,1)S(1)} %bitcast.112, bf16[1024,1024]{1,0:T(8,128)(2,1)S(1)} %constant_dynamic-update-slice_fusion), kind=kOutput, calls=%fused_computation | convolution fusion | flops 1074266112 | bytes 4194304 | tf_op jit(solution)/shard_map/dot_general | solution.py:57
  52.3 8.5 %all-to-all-start.1 = ((bf16[8,2,4,8,1024]{4,3,2,1,0:T(8,128)(2,1)}), bf16[8,2,4,8,1024]{4,3,2,1,0:T(8,128)(2,1)S(1)}, u32[]{:S(2)}, u32[]{:S(2)}) async-start(bf16[8,2,4,8,1024]{4,3,2,1,0:T(8,128)(2,1)} %bitcast.20), calls=%async_computation.1 | async-start | bytes 2097152 | tf_op jit(solution)/shard_map/all_to_all | solution.py:12
  60.7 5.1 %all-gather.2.cloned.1.call-done = bf16[512,1024]{1,0:T(8,128)(2,1)} async-done(((bf16[64,1024]{1,0:T(8,128)(2,1)}), bf16[512,1024]{1,0:T(8,128)(2,1)}) %all-gather.2.cloned.1.call-update) | async-done | bytes 1048592 | tf_op jit(solution)/shard_map/all_gather | solution.py:47
  65.9 3.3 %fusion.21 = f32[512,1024]{1,0:T(8,128)S(1)} fusion(bf16[512,1024]{1,0:T(8,128)(2,1)} %all-gather.2.cloned.1.call-done, bf16[1024,1024]{1,0:T(8,128)(2,1)} %copy-done.5), kind=kOutput, calls=%fused_computation.61 | convolution fusion | flops 1073741824 | bytes 5242880 | tf_op jit(solution)/shard_map/dot_general | solution.py:63
  69.2 7.4 %collective-permute-start.11 = (bf16[4,8,8,1024]{3,2,0,1:T(8,128)(2,1)S(1)}, bf16[4,8,8,1024]{3,2,0,1:T(8,128)(2,1)S(1)}, u32[]{:S(2)}, u32[]{:S(2)}) collective-permute-start(bf16[4,8,8,1024]{3,2,0,1:T(8,128)(2,1)S(1)} %fusion.1), channel_id=1, source_target_pairs={{0,1},{1,0},{2,3},{3,2},{4,5},{5,4},{6,7},{7,6},{8,9},{9,8},{10,11... | collective-permute-start | bytes 1572872 | tf_op jit(solution)/shard_map/ppermute | solution.py:17
  78.0 2.1 %collective-permute-start.18 = (bf16[128,1024]{1,0:T(8,128)(2,1)S(1)}, bf16[128,1024]{1,0:T(8,128)(2,1)S(1)}, u32[]{:S(2)}, u32[]{:S(2)}) collective-permute-start(bf16[128,1024]{1,0:T(8,128)(2,1)S(1)} %get-tuple-element.51), channel_id=1, source_target_pairs={{0,192},{64,0},{128,64},{192,128},{1,193},{65,1},{129,65},{193,129... | collective-permute-start | bytes 786440 | tf_op jit(solution)/shard_map/ppermute | solution.py:17
  81.9 1.9 %collective-permute-start.12 = (bf16[8,8,1024]{2,1,0:T(8,128)(2,1)S(1)}, bf16[8,8,1024]{2,1,0:T(8,128)(2,1)S(1)}, u32[]{:S(2)}, u32[]{:S(2)}) collective-permute-start(bf16[8,8,1024]{2,1,0:T(8,128)(2,1)S(1)} %get-tuple-element.53), channel_id=1, source_target_pairs={{0,6},{2,0},{4,2},{6,4},{1,7},{3,1},{5,3},{7,5},{8,14},{10,8},{12,... | collective-permute-start | bytes 393224 | tf_op jit(solution)/shard_map/ppermute | solution.py:17
  83.8 1.9 %collective-permute-start.13 = (bf16[8,8,1024]{2,1,0:T(8,128)(2,1)S(1)}, bf16[8,8,1024]{2,1,0:T(8,128)(2,1)S(1)}, u32[]{:S(2)}, u32[]{:S(2)}) collective-permute-start(bf16[8,8,1024]{2,1,0:T(8,128)(2,1)S(1)} %get-tuple-element.55), channel_id=1, source_target_pairs={{0,4},{2,6},{4,0},{6,2},{1,5},{3,7},{5,1},{7,3},{8,12},{10,14},{12... | collective-permute-start | bytes 393224 | tf_op jit(solution)/shard_map/ppermute | solution.py:17
  87.0 1.9 %collective-permute-done.20 = bf16[128,1024]{1,0:T(8,128)(2,1)S(1)} collective-permute-done((bf16[128,1024]{1,0:T(8,128)(2,1)S(1)}, bf16[128,1024]{1,0:T(8,128)(2,1)S(1)}, u32[]{:S(2)}, u32[]{:S(2)}) %collective-permute-start.20) | collective-permute-done | bytes 262176 | tf_op jit(solution)/shard_map/ppermute | solution.py:17
  93.1 2.8 %collective-permute-start.16 = (f32[64,256]{1,0:T(8,128)}, f32[64,256]{1,0:T(8,128)}, u32[]{:S(2)}, u32[]{:S(2)}) collective-permute-start(f32[64,256]{1,0:T(8,128)} %get-tuple-element.59), channel_id=1, source_target_pairs={{0,128},{64,192},{128,0},{192,64},{1,129},{65,193},{129,1},{193,65... | collective-permute-start | bytes 196616 | tf_op jit(solution)/shard_map/ppermute | solution.py:17
  98.2 6.8 %all-to-all-start.2 = ((bf16[8,8,1024]{2,1,0:T(8,128)(2,1)}), bf16[8,8,1024]{2,1,0:T(8,128)(2,1)S(1)}, u32[]{:S(2)}, u32[]{:S(2)}) async-start(bf16[8,8,1024]{2,1,0:T(8,128)(2,1)} %bitcast.22), calls=%async_computation.2 | async-start | bytes 262144 | tf_op jit(solution)/shard_map/all_to_all | solution.py:12
  105.2 1.5 %bitcast_dynamic-update-slice_fusion.3 = f32[7,64,256]{2,1,0:T(8,128)} fusion(f32[7,64,256]{2,1,0:T(8,128)} %fusion.13, f32[64,256]{1,0:T(8,128)} %collective-permute-done.15), kind=kLoop, calls=%fused_computation.40 | loop fusion | bytes 131072
  106.7 1.5 %bitcast_dynamic-update-slice_fusion.1 = f32[7,64,256]{2,1,0:T(8,128)} fusion(f32[7,64,256]{2,1,0:T(8,128)} %bitcast_dynamic-update-slice_fusion.3, f32[64,256]{1,0:T(8,128)} %collective-permute-done.16), kind=kLoop, calls=%fused_computation.38 | loop fusion | bytes 131072
  108.1 1.5 %bitcast_dynamic-update-slice_fusion = f32[7,64,256]{2,1,0:T(8,128)} fusion(f32[7,64,256]{2,1,0:T(8,128)} %bitcast_dynamic-update-slice_fusion.1, f32[64,256]{1,0:T(8,128)} %collective-permute-done.17), kind=kLoop, calls=%fused_computation.37 | loop fusion | bytes 131072
  110.2 1.5 %bitcast_dynamic-update-slice_fusion.4 = f32[7,64,256]{2,1,0:T(8,128)} fusion(f32[7,64,256]{2,1,0:T(8,128)} %fusion.14, f32[64,256]{1,0:T(8,128)} %collective-permute-done.15), kind=kLoop, calls=%fused_computation.41 | loop fusion | bytes 131072
  111.7 1.5 %bitcast_dynamic-update-slice_fusion.2 = f32[7,64,256]{2,1,0:T(8,128)} fusion(f32[7,64,256]{2,1,0:T(8,128)} %bitcast_dynamic-update-slice_fusion.4, f32[64,256]{1,0:T(8,128)} %collective-permute-done.16), kind=kLoop, calls=%fused_computation.39 | loop fusion | bytes 131072 | tf_op jit(solution)/shard_map/stack | solution.py:72
  (88 shorter events, 27.8 us)
Async XLA Ops:
  9.0 10.5 %collective-permute-start.2 = (bf16[64,256]{1,0:T(8,128)(2,1)S(1)}, bf16[64,256]{1,0:T(8,128)(2,1)S(1)}, u32[]{:S(2)}, u32[]{:S(2)}) collective-permute-start(bf16[64,256]{1,0:T(8,128)(2,1)S(1)} %get-tuple-element.62), channel_id=1, source_target_pairs={{0,192},{64,0},{128,64},{192,128},{1,193},{65,1},{129,65},{193,129... | collective-permute-start | bytes 98312 | tf_op jit(solution)/shard_map/ppermute | solution.py:17
  12.6 6.9 %collective-permute-start.1 = (bf16[64,256]{1,0:T(8,128)(2,1)S(1)}, bf16[64,256]{1,0:T(8,128)(2,1)S(1)}, u32[]{:S(2)}, u32[]{:S(2)}) collective-permute-start(bf16[64,256]{1,0:T(8,128)(2,1)S(1)} %get-tuple-element.63), channel_id=1, source_target_pairs={{0,128},{64,192},{128,0},{192,64},{1,129},{65,193},{129,1},{193,65... | collective-permute-start | bytes 98312 | tf_op jit(solution)/shard_map/ppermute | solution.py:17
  13.0 6.5 %collective-permute-start = (bf16[64,256]{1,0:T(8,128)(2,1)S(1)}, bf16[64,256]{1,0:T(8,128)(2,1)S(1)}, u32[]{:S(2)}, u32[]{:S(2)}) collective-permute-start(bf16[64,256]{1,0:T(8,128)(2,1)S(1)} %get-tuple-element.64), channel_id=1, source_target_pairs={{0,64},{64,128},{128,192},{192,0},{1,65},{65,129},{129,193},{193,1... | collective-permute-start | bytes 98312 | tf_op jit(solution)/shard_map/ppermute | solution.py:17
  13.7 11.1 %all-to-all-start = ((bf16[8,8,1024]{2,1,0:T(8,128)(2,1)}), bf16[8,8,1024]{2,1,0:T(8,128)(2,1)S(1)}, u32[]{:S(2)}, u32[]{:S(2)}) async-start(bf16[8,8,1024]{2,1,0:T(8,128)(2,1)} %bitcast.130), calls=%async_computation | async-start | bytes 262144 | tf_op jit(solution)/shard_map/all_to_all | solution.py:12
  19.5 46.4 %all-gather.2.cloned.1.call-start = ((), (), s32[]{:S(2)}) async-start(), calls=%async_computation.3 | async-start | bytes 1179648 | tf_op jit(solution)/shard_map/all_gather | solution.py:47
  27.6 7.8 %collective-permute-start.3 = (bf16[64,1024]{1,0:T(8,128)(2,1)S(1)}, bf16[64,1024]{1,0:T(8,128)(2,1)S(1)}, u32[]{:S(2)}, u32[]{:S(2)}) collective-permute-start(bf16[64,1024]{1,0:T(8,128)(2,1)S(1)} %pad_maximum_fusion.2), channel_id=1, source_target_pairs={{0,2},{2,4},{4,6},{6,0},{1,3},{3,5},{5,7},{7,1},{8,10},{10,12},{12... | collective-permute-start | bytes 393224 | tf_op jit(solution)/shard_map/ppermute | solution.py:17
  27.7 13.3 %collective-permute-start.7 = (bf16[256,1024]{1,0:T(8,128)(2,1)S(1)}, bf16[256,1024]{1,0:T(8,128)(2,1)S(1)}, u32[]{:S(2)}, u32[]{:S(2)}) collective-permute-start(bf16[256,1024]{1,0:T(8,128)(2,1)S(1)} %copy-done.1), channel_id=1, source_target_pairs={{0,64},{64,128},{128,192},{192,0},{1,65},{65,129},{129,193},{193,1... | collective-permute-start | bytes 1572872 | tf_op jit(solution)/shard_map/ppermute | solution.py:17
  29.3 12.7 %collective-permute-start.9 = (bf16[256,1024]{1,0:T(8,128)(2,1)S(1)}, bf16[256,1024]{1,0:T(8,128)(2,1)S(1)}, u32[]{:S(2)}, u32[]{:S(2)}) collective-permute-start(bf16[256,1024]{1,0:T(8,128)(2,1)S(1)} %copy-done.1), channel_id=1, source_target_pairs={{0,192},{64,0},{128,64},{192,128},{1,193},{65,1},{129,65},{193,129... | collective-permute-start | bytes 1572872 | tf_op jit(solution)/shard_map/ppermute | solution.py:17
  35.5 9.0 %collective-permute-start.6 = (bf16[4,64,1024]{2,1,0:T(8,128)(2,1)S(1)}, bf16[4,64,1024]{2,1,0:T(8,128)(2,1)S(1)}, u32[]{:S(2)}, u32[]{:S(2)}) collective-permute-start(bf16[4,64,1024]{2,1,0:T(8,128)(2,1)S(1)} %get-tuple-element.57), channel_id=1, source_target_pairs={{0,1},{1,0},{2,3},{3,2},{4,5},{5,4},{6,7},{7,6},{8,9},{9,8},{10,11... | collective-permute-start | bytes 1572872 | tf_op jit(solution)/shard_map/ppermute | solution.py:17
  41.7 6.6 %collective-permute-start.8 = (bf16[128,1024]{1,0:T(8,128)(2,1)}, bf16[128,1024]{1,0:T(8,128)(2,1)S(1)}, u32[]{:S(2)}, u32[]{:S(2)}) collective-permute-start(bf16[128,1024]{1,0:T(8,128)(2,1)} %slice.127), channel_id=1, source_target_pairs={{0,64},{64,128},{128,192},{192,0},{1,65},{65,129},{129,193},{193,1... | collective-permute-start | bytes 786440 | tf_op jit(solution)/shard_map/ppermute | solution.py:17
  42.1 6.2 %collective-permute-start.10 = (bf16[128,1024]{1,0:T(8,128)(2,1)S(1)}, bf16[128,1024]{1,0:T(8,128)(2,1)S(1)}, u32[]{:S(2)}, u32[]{:S(2)}) collective-permute-start(bf16[128,1024]{1,0:T(8,128)(2,1)S(1)} %slice.128), channel_id=1, source_target_pairs={{0,192},{64,0},{128,64},{192,128},{1,193},{65,1},{129,65},{193,129... | collective-permute-start | bytes 786440 | tf_op jit(solution)/shard_map/ppermute | solution.py:17
  52.3 44.9 %all-to-all-start.1 = ((bf16[8,2,4,8,1024]{4,3,2,1,0:T(8,128)(2,1)}), bf16[8,2,4,8,1024]{4,3,2,1,0:T(8,128)(2,1)S(1)}, u32[]{:S(2)}, u32[]{:S(2)}) async-start(bf16[8,2,4,8,1024]{4,3,2,1,0:T(8,128)(2,1)} %bitcast.20), calls=%async_computation.1 | async-start | bytes 2097152 | tf_op jit(solution)/shard_map/all_to_all | solution.py:12
  69.2 12.5 %collective-permute-start.11 = (bf16[4,8,8,1024]{3,2,0,1:T(8,128)(2,1)S(1)}, bf16[4,8,8,1024]{3,2,0,1:T(8,128)(2,1)S(1)}, u32[]{:S(2)}, u32[]{:S(2)}) collective-permute-start(bf16[4,8,8,1024]{3,2,0,1:T(8,128)(2,1)S(1)} %fusion.1), channel_id=1, source_target_pairs={{0,1},{1,0},{2,3},{3,2},{4,5},{5,4},{6,7},{7,6},{8,9},{9,8},{10,11... | collective-permute-start | bytes 1572872 | tf_op jit(solution)/shard_map/ppermute | solution.py:17
  78.0 9.0 %collective-permute-start.18 = (bf16[128,1024]{1,0:T(8,128)(2,1)S(1)}, bf16[128,1024]{1,0:T(8,128)(2,1)S(1)}, u32[]{:S(2)}, u32[]{:S(2)}) collective-permute-start(bf16[128,1024]{1,0:T(8,128)(2,1)S(1)} %get-tuple-element.51), channel_id=1, source_target_pairs={{0,192},{64,0},{128,64},{192,128},{1,193},{65,1},{129,65},{193,129... | collective-permute-start | bytes 786440 | tf_op jit(solution)/shard_map/ppermute | solution.py:17
  80.1 8.8 %collective-permute-start.20 = (bf16[128,1024]{1,0:T(8,128)(2,1)S(1)}, bf16[128,1024]{1,0:T(8,128)(2,1)S(1)}, u32[]{:S(2)}, u32[]{:S(2)}) collective-permute-start(bf16[128,1024]{1,0:T(8,128)(2,1)S(1)} %get-tuple-element.52), channel_id=1, source_target_pairs={{0,64},{64,128},{128,192},{192,0},{1,65},{65,129},{129,193},{193,1... | collective-permute-start | bytes 786440 | tf_op jit(solution)/shard_map/ppermute | solution.py:17
  81.9 9.4 %collective-permute-start.12 = (bf16[8,8,1024]{2,1,0:T(8,128)(2,1)S(1)}, bf16[8,8,1024]{2,1,0:T(8,128)(2,1)S(1)}, u32[]{:S(2)}, u32[]{:S(2)}) collective-permute-start(bf16[8,8,1024]{2,1,0:T(8,128)(2,1)S(1)} %get-tuple-element.53), channel_id=1, source_target_pairs={{0,6},{2,0},{4,2},{6,4},{1,7},{3,1},{5,3},{7,5},{8,14},{10,8},{12,... | collective-permute-start | bytes 393224 | tf_op jit(solution)/shard_map/ppermute | solution.py:17
  83.8 7.6 %collective-permute-start.14 = (bf16[8,8,1024]{2,1,0:T(8,128)(2,1)S(1)}, bf16[8,8,1024]{2,1,0:T(8,128)(2,1)S(1)}, u32[]{:S(2)}, u32[]{:S(2)}) collective-permute-start(bf16[8,8,1024]{2,1,0:T(8,128)(2,1)S(1)} %get-tuple-element.54), channel_id=1, source_target_pairs={{0,2},{2,4},{4,6},{6,0},{1,3},{3,5},{5,7},{7,1},{8,10},{10,12},{12... | collective-permute-start | bytes 393224 | tf_op jit(solution)/shard_map/ppermute | solution.py:17
  83.8 7.7 %collective-permute-start.13 = (bf16[8,8,1024]{2,1,0:T(8,128)(2,1)S(1)}, bf16[8,8,1024]{2,1,0:T(8,128)(2,1)S(1)}, u32[]{:S(2)}, u32[]{:S(2)}) collective-permute-start(bf16[8,8,1024]{2,1,0:T(8,128)(2,1)S(1)} %get-tuple-element.55), channel_id=1, source_target_pairs={{0,4},{2,6},{4,0},{6,2},{1,5},{3,7},{5,1},{7,3},{8,12},{10,14},{12... | collective-permute-start | bytes 393224 | tf_op jit(solution)/shard_map/ppermute | solution.py:17
  89.9 24.9 %collective-permute-start.19 = (bf16[2,128,1024]{2,1,0:T(8,128)(2,1)}, bf16[2,128,1024]{2,1,0:T(8,128)(2,1)S(1)}, u32[]{:S(2)}, u32[]{:S(2)}) collective-permute-start(bf16[2,128,1024]{2,1,0:T(8,128)(2,1)} %get-tuple-element.47), channel_id=1, source_target_pairs={{0,192},{64,0},{128,64},{192,128},{1,193},{65,1},{129,65},{193,129... | collective-permute-start | bytes 1572872 | tf_op jit(solution)/shard_map/ppermute | solution.py:17
  90.2 24.6 %collective-permute-start.21 = (bf16[2,128,1024]{2,1,0:T(8,128)(2,1)}, bf16[2,128,1024]{2,1,0:T(8,128)(2,1)S(1)}, u32[]{:S(2)}, u32[]{:S(2)}) collective-permute-start(bf16[2,128,1024]{2,1,0:T(8,128)(2,1)} %get-tuple-element.48), channel_id=1, source_target_pairs={{0,64},{64,128},{128,192},{192,0},{1,65},{65,129},{129,193},{193,1... | collective-permute-start | bytes 1572872 | tf_op jit(solution)/shard_map/ppermute | solution.py:17
  92.3 15.9 %collective-permute-start.17 = (f32[64,256]{1,0:T(8,128)}, f32[64,256]{1,0:T(8,128)}, u32[]{:S(2)}, u32[]{:S(2)}) collective-permute-start(f32[64,256]{1,0:T(8,128)} %get-tuple-element.58), channel_id=1, source_target_pairs={{0,64},{64,128},{128,192},{192,0},{1,65},{65,129},{129,193},{193,1... | collective-permute-start | bytes 196616 | tf_op jit(solution)/shard_map/ppermute | solution.py:17
  93.1 13.6 %collective-permute-start.16 = (f32[64,256]{1,0:T(8,128)}, f32[64,256]{1,0:T(8,128)}, u32[]{:S(2)}, u32[]{:S(2)}) collective-permute-start(f32[64,256]{1,0:T(8,128)} %get-tuple-element.59), channel_id=1, source_target_pairs={{0,128},{64,192},{128,0},{192,64},{1,129},{65,193},{129,1},{193,65... | collective-permute-start | bytes 196616 | tf_op jit(solution)/shard_map/ppermute | solution.py:17
  95.8 9.4 %collective-permute-start.15 = (f32[64,256]{1,0:T(8,128)}, f32[64,256]{1,0:T(8,128)}, u32[]{:S(2)}, u32[]{:S(2)}) collective-permute-start(f32[64,256]{1,0:T(8,128)} %get-tuple-element.60), channel_id=1, source_target_pairs={{0,192},{64,0},{128,64},{192,128},{1,193},{65,1},{129,65},{193,129... | collective-permute-start | bytes 196616 | tf_op jit(solution)/shard_map/ppermute | solution.py:17
  98.2 16.6 %all-to-all-start.2 = ((bf16[8,8,1024]{2,1,0:T(8,128)(2,1)}), bf16[8,8,1024]{2,1,0:T(8,128)(2,1)S(1)}, u32[]{:S(2)}, u32[]{:S(2)}) async-start(bf16[8,8,1024]{2,1,0:T(8,128)(2,1)} %bitcast.22), calls=%async_computation.2 | async-start | bytes 262144 | tf_op jit(solution)/shard_map/all_to_all | solution.py:12
  (8 other events, 50.1 us)
Sparse Core Ops, SparseCore 0:
  27.8 38.0 all-gather.1

commit v5 on v4

v5 whole, which is shorter than its diff:
```python
import jax
import jax.numpy as jnp
from jax import lax
from jax.experimental import pallas as pl
from jax.experimental.pallas import tpu as pltpu
from jax.sharding import Mesh, PartitionSpec as P

BF = jnp.bfloat16
F32 = jnp.float32
XC = ("x", "c")
FWD = 2**30
BWD = 2**36
VMEM = pl.BlockSpec(memory_space=pltpu.VMEM)
SMEM = pl.BlockSpec(memory_space=pltpu.SMEM)


def exchange(v, axes):
    return lax.all_to_all(v, axes, split_axis=0, concat_axis=0, tiled=False)


def shift(v, axis, s):
    n = lax.axis_size(axis)
    return lax.ppermute(v, axis, [(i, (i + s) % n) for i in range(n)])


def place(where, e, s, nx):
    return ((where[0] - s) & (nx - 1)) * 2 + (where[1] ^ e)


def forward(where, own, other, w0, w1, w2a, w2b, w3, out):
    nx, ty, _ = own.shape
    nz, _, j, n = out.shape
    r = w0.shape[0]
    half = r // 2
    for e, a in enumerate((own, other)):
        rows = a[...].reshape(nx * ty, a.shape[2])
        total = jnp.dot(rows[:, :r], w0[...], preferred_element_type=F32)
        total += jnp.dot(rows[:, r : 2 * r], w1[...], preferred_element_type=F32)
        total += jnp.dot(rows[:, 2 * r : 2 * r + half], w2a[...], preferred_element_type=F32)
        total += jnp.dot(rows[:, 2 * r + half : 3 * r], w2b[...], preferred_element_type=F32)
        total += jnp.dot(rows[:, 3 * r :], w3[...], preferred_element_type=F32)
        for s in range(nx):
            out[:, place(where, e, s, nx)] = total[s * ty : (s + 1) * ty].reshape(nz, j, n)


def backward(where, g, w0, w1, w2a, w2b, w3, out, g_rel, rows):
    nz, nxc, j, n = g.shape
    ny, ty, r = out.shape[1:]
    half = r // 2
    for k in range(nxc):
        rows[k * ty : (k + 1) * ty] = g[:, k].astype(F32).reshape(ty, n).astype(BF)
    for e in range(2):
        for s in range(nxc // 2):
            k = e * (nxc // 2) + s
            at = pl.multiple_of(place(where, e, s, nxc // 2) * ty, ty)
            g_rel[k * ty : (k + 1) * ty] = rows[pl.ds(at, ty)]
    across = (((1,), (1,)), ((), ()))
    for s, w in enumerate(((w0,), (w1,), (w2a, w2b), (w3,))):
        at = (where[2] - s) & (ny - 1)
        width = r // len(w)
        for i, part in enumerate(w):
            v = lax.dot_general(rows[...], part[...], across, preferred_element_type=F32)
            out[:, at, :, i * width : (i + 1) * width] = v.astype(BF).reshape(nxc, ty, width)


def call(kernel, out_shape, *args, scratch=(), flops):
    return pl.pallas_call(
        kernel,
        out_shape=out_shape,
        in_specs=[SMEM] + [VMEM] * (len(args) - 1),
        out_specs=jax.tree.map(lambda _: VMEM, out_shape),
        scratch_shapes=scratch,
        cost_estimate=pl.CostEstimate(flops=flops, bytes_accessed=flops // 400, transcendentals=0),
        compiler_params=pltpu.CompilerParams(vmem_limit_bytes=32 * 1024 * 1024),
    )(*args)


def shards(attn_out, head_mask, gate_scale, w_out, grad_out):
    nx, ny, nz, nc = (lax.axis_size(a) for a in "xyzc")
    me = lax.axis_index("y")
    where = jnp.stack([lax.axis_index("x"), lax.axis_index("c"), me]).astype(jnp.int32)
    t, r = attn_out.shape
    j, d = grad_out.shape
    n = d // (nx * nc)
    ty = t // ny
    half = r // 2

    w1, w3 = shift(w_out, "y", 1), shift(w_out, "y", -1)
    g = exchange(grad_out.reshape(j, nx * nc, n).transpose(1, 0, 2), XC)

    gate_vals = head_mask.astype(F32) * gate_scale
    col_gate = jnp.repeat(gate_vals, r // gate_vals.shape[0])
    gated = (attn_out.astype(F32) * col_gate[None, :]).astype(BF).reshape(ny, ty, r)

    a = [lax.dynamic_index_in_dim(gated, (me + s) % ny, 0, keepdims=False) for s in range(ny)]
    a = [a[0]] + [shift(a[s], "y", s) for s in range(1, ny)]
    a = jnp.concatenate(a, axis=1)
    a, g, w1, w3 = lax.optimization_barrier((a, g, w1, w3))
    g = exchange(jnp.broadcast_to(g[None], (nz,) + g.shape), "z")
    a = jnp.stack([a] + [shift(a, "x", s) for s in range(1, nx)])
    w2a, w2b = shift(w1[:half], "y", 1), shift(w3[half:], "y", -1)
    other = shift(a, "c", 1)
    w = (w_out, w1, w2a, w2b, w3)

    part = call(
        forward, jax.ShapeDtypeStruct((nz, nx * nc, j, n), F32), where, a, other, *w,
        flops=FWD,
    )
    proj = lax.psum_scatter(part, "z", scatter_dimension=0, tiled=False).astype(BF)
    proj = exchange(proj, XC)
    proj_out = proj.transpose(1, 0, 2).reshape(j, d)

    part, g = lax.optimization_barrier((part, g))
    back, g_rel = call(
        backward,
        (
            jax.ShapeDtypeStruct((nx * nc, ny, ty, r), BF),
            jax.ShapeDtypeStruct((nx * nc * ty, n), BF),
        ),
        where, g, *w,
        scratch=[pltpu.VMEM((nx * nc * ty, n), BF)],
        flops=BWD,
    )
    mine = exchange(back.reshape(nx * nc * ny, ty, r), ("x", "c", "y"))
    mine = mine.astype(F32).reshape(nx * nc, t, r).sum(axis=0)
    grad_attn = (mine * col_gate[None, :]).astype(BF)

    a_rel = jnp.concatenate([a, other]).reshape(nx * nc * ty, ny * r)
    gw = lax.dot_general(a_rel, g_rel, (((0,), (0,)), ((), ())), preferred_element_type=F32)
    gw = gw.reshape(ny, 2, half, n)
    near = gw[1].at[0].add(shift(gw[2, 0].astype(BF), "y", -1).astype(F32))
    far = gw[3].at[1].add(shift(gw[2, 1].astype(BF), "y", 1).astype(F32))
    near, far = shift(near.astype(BF), "y", -1), shift(far.astype(BF), "y", 1)
    grad_w = (gw[0] + near.astype(F32) + far.astype(F32)).reshape(r, n)
    return (proj_out, grad_attn, grad_w)


def solution(mesh):
    fine = Mesh(mesh.devices.reshape(4, 8, 4, 2), ("y", "z", "x", "c"))
    dp, head = XC, ("y", "z")
    return jax.shard_map(
        shards,
        mesh=fine,
        in_specs=(P(dp, head), P(head), P(head), P(head, dp), P(dp + head, None)),
        out_specs=(P(dp + head, None), P(dp, head), P(head, dp)),
        check_vma=False,
    )
```

time: 125 us -> 135 us (1.080)
  waiting for transfers between devices: 26.8 us -> 53.5 us
  starting transfers between devices: 54.1 us -> 45.2 us
  local copies, waits for them, and re-layouts: 15.4 us -> 7.84 us
  Pallas kernels: 0 us -> 6.51 us
  matrix products: 6.85 us -> 1.29 us
    ppermute x22 -> x15, waiting for transfers between devices: 16.5 us -> 36.6 us  [shift(): return lax.ppermute(v, axis, [(i, (i + s) % n) for i in range(n)])]
    ppermute x22 -> x15, starting transfers between devices: 33 us -> 19.6 us  [shift(): return lax.ppermute(v, axis, [(i, (i + s) % n) for i in range(n)])]
    all_to_all x3 -> x4, waiting for transfers between devices: 5.23 us -> 16.9 us  [exchange(): return lax.all_to_all(v, axes, split_axis=0, concat_axis=0, tiled=False)]
    pallas_call x0 -> x2, Pallas kernels: none -> 6.51 us  [call(): pl.pallas_call(kernel, out_shape=out_shape, in_specs=[SMEM] + [VMEM] * (l...]
    dot_general x3 -> x1, matrix products: 6.85 us -> 1.29 us  [shards(): lax.dot_general(a_rel, g_rel, (((0,), (0,)), ((), ())), preferred_element...]
    all_gather x1 -> x0, waiting for transfers between devices: 5.12 us -> none  [shards(): g = lax.all_gather(g, 'z', axis=0, tiled=True)]
    all_to_all x3 -> x4, starting transfers between devices: 21.1 us -> 25.6 us  [exchange(): return lax.all_to_all(v, axes, split_axis=0, concat_axis=0, tiled=False)]
    unnamed x23 -> x19, local copies, waits for them, and re-layouts: 9.32 us -> 5.49 us
  transfers between devices with their start and end apart: 26 -> 20, of which waited for: 10 -> 13; matrix products, arithmetic and copies ran while one was open for 18% -> 5% of each run, Pallas kernels for 0% -> 5%
where the time goes in v5:
time: 135 us; the launch traced here: 134 us
  waiting for transfers between devices  53.5 us (40%)
  starting transfers between devices  45.2 us (33%)
  between operations  14.2 us (11%)
  local copies, waits for them, and re-layouts  7.84 us (6%)
  Pallas kernels  6.51 us (5%)
  other arithmetic  5.53 us (4%)
    ppermute x15, waiting for transfers between devices, shift(): return lax.ppermute(v, axis, [(i, (i + s) % n) for i in range(n)])  36.6 us
    all_to_all x4, starting transfers between devices, exchange(): return lax.all_to_all(v, axes, split_axis=0, concat_axis=0, tiled=False)  25.6 us
    ppermute x15, starting transfers between devices, shift(): return lax.ppermute(v, axis, [(i, (i + s) % n) for i in range(n)])  19.6 us
    all_to_all x4, waiting for transfers between devices, exchange(): return lax.all_to_all(v, axes, split_axis=0, concat_axis=0, tiled=False)  16.9 us
    pallas_call x2, Pallas kernels, call(): pl.pallas_call(kernel, out_shape=out_shape, in_specs=[SMEM] + [VMEM] * (l...  6.51 us
    unnamed x19, local copies, waits for them, and re-layouts  5.49 us
  transfers between devices with their start and end apart: 20, of which 13 were waited for; matrix products, arithmetic and copies ran while one was open for 5% of the time, Pallas kernels for 5%

profile of v5, /device:TPU:1, one launch (start us, length us, event | category | flops | bytes accessed | tf_op | source)
XLA Modules:
  0.0 134.2 jit_solution(7739933881683243574)
XLA Ops:
  7.2 3.6 %collective-permute-start.4 = (bf16[256,1024]{1,0:T(8,128)(2,1)}, bf16[256,1024]{1,0:T(8,128)(2,1)S(1)}, u32[]{:S(2)}, u32[]{:S(2)}) collective-permute-start(bf16[256,1024]{1,0:T(8,128)(2,1)} %w0.3), channel_id=1, source_target_pairs={{0,192},{64,0},{128,64},{192,128},{1,193},{65,1},{129,65},{193,129... | collective-permute-start | bytes 1572872 | tf_op jit(solution)/shard_map/ppermute | solution.py:23
  12.5 2.8 %collective-permute-start.2 = (bf16[64,256]{1,0:T(8,128)(2,1)S(1)}, bf16[64,256]{1,0:T(8,128)(2,1)S(1)}, u32[]{:S(2)}, u32[]{:S(2)}) collective-permute-start(bf16[64,256]{1,0:T(8,128)(2,1)S(1)} %get-tuple-element.48), channel_id=1, source_target_pairs={{0,192},{64,0},{128,64},{192,128},{1,193},{65,1},{129,65},{193,129... | collective-permute-start | bytes 98312 | tf_op jit(solution)/shard_map/ppermute | solution.py:23
  15.9 6.1 %all-to-all-start = ((bf16[8,8,1024]{2,1,0:T(8,128)(2,1)}), bf16[8,8,1024]{2,1,0:T(8,128)(2,1)S(1)}, u32[]{:S(2)}, u32[]{:S(2)}) async-start(bf16[8,8,1024]{2,1,0:T(8,128)(2,1)} %bitcast.68), calls=%async_computation | async-start | bytes 262144 | tf_op jit(solution)/shard_map/all_to_all | solution.py:18
  24.1 1.7 %collective-permute-done = bf16[64,256]{1,0:T(8,128)(2,1)S(1)} collective-permute-done((bf16[64,256]{1,0:T(8,128)(2,1)S(1)}, bf16[64,256]{1,0:T(8,128)(2,1)S(1)}, u32[]{:S(2)}, u32[]{:S(2)}) %collective-permute-start) | collective-permute-done | bytes 32800 | tf_op jit(solution)/shard_map/ppermute | solution.py:23
  25.8 1.5 %all-to-all-done = bf16[8,8,1024]{2,1,0:T(8,128)(2,1)S(1)} async-done(((bf16[8,8,1024]{2,1,0:T(8,128)(2,1)}), bf16[8,8,1024]{2,1,0:T(8,128)(2,1)S(1)}, u32[]{:S(2)}, u32[]{:S(2)}) %all-to-all-start) | async-done | bytes 131104 | tf_op jit(solution)/shard_map/all_to_all | solution.py:18
  28.4 8.2 %all-to-all-start.2 = ((bf16[8,8,8,1024]{3,2,1,0:T(8,128)(2,1)}), bf16[8,8,8,1024]{3,2,1,0:T(8,128)(2,1)S(1)}, u32[]{:S(2)}, u32[]{:S(2)}) async-start(bf16[8,8,8,1024]{3,2,1,0:T(8,128)(2,1)} %broadcast_in_dim.10), calls=%async_computation.3 | async-start | bytes 2097152 | tf_op jit(solution)/shard_map/all_to_all | solution.py:18
  39.2 1.8 %collective-permute-start.10 = (bf16[128,1024]{1,0:T(8,128)(2,1)S(1)}, bf16[128,1024]{1,0:T(8,128)(2,1)S(1)}, u32[]{:S(2)}, u32[]{:S(2)}) collective-permute-start(bf16[128,1024]{1,0:T(8,128)(2,1)S(1)} %slice.75), channel_id=1, source_target_pairs={{0,192},{64,0},{128,64},{192,128},{1,193},{65,1},{129,65},{193,129... | collective-permute-start | bytes 786440 | tf_op jit(solution)/shard_map/ppermute | solution.py:23
  41.3 2.0 %collective-permute-done.6 = bf16[64,1024]{1,0:T(8,128)(2,1)S(1)} collective-permute-done((bf16[64,1024]{1,0:T(8,128)(2,1)S(1)}, bf16[64,1024]{1,0:T(8,128)(2,1)S(1)}, u32[]{:S(2)}, u32[]{:S(2)}) %collective-permute-start.6) | collective-permute-done | bytes 131104 | tf_op jit(solution)/shard_map/ppermute | solution.py:23
  43.3 1.3 %collective-permute-done.5 = bf16[64,1024]{1,0:T(8,128)(2,1)S(1)} collective-permute-done((bf16[64,1024]{1,0:T(8,128)(2,1)S(1)}, bf16[64,1024]{1,0:T(8,128)(2,1)S(1)}, u32[]{:S(2)}, u32[]{:S(2)}) %collective-permute-start.5) | collective-permute-done | bytes 131104 | tf_op jit(solution)/shard_map/ppermute | solution.py:23
  44.7 3.8 %collective-permute-start.8 = (bf16[4,64,1024]{2,1,0:T(8,128)(2,1)S(1)}, bf16[4,64,1024]{2,1,0:T(8,128)(2,1)S(1)}, u32[]{:S(2)}, u32[]{:S(2)}) collective-permute-start(bf16[4,64,1024]{2,1,0:T(8,128)(2,1)S(1)} %pad_maximum_fusion.own), channel_id=1, source_target_pairs={{0,1},{1,0},{2,3},{3,2},{4,5},{5,4},{6,7},{7,6},{8,9},{9,8},{10,11... | collective-permute-start | bytes 1572872 | tf_op jit(solution)/shard_map/ppermute | solution.py:23
  50.1 3.4 %shard_map.76 = f32[8,8,8,1024]{3,2,1,0:T(8,128)} custom-call(s32[3]{0:T(128)S(1)} %pad_add_fusion.where, bf16[4,64,1024]{2,1,0:T(8,128)(2,1)S(1)} %pad_maximum_fusion.own, bf16[4,64,1024]{2,1,0:T(8,128)(2,1)S(1)} %collective-permute-done.8.other, bf16[256,1024]{1,0:T(8,128)(2,1)S(1)} %copy-done.2, bf16[256,1024]{1,0:T(8,128)(2,1)S(1)} %collective-permute-done.3.w1, ...), custom_call_target="tpu_custom_call" | custom-call | flops 1073741824 | bytes 2684354 | tf_op jit(solution)/shard_map/pallas_call | solution.py:67
  55.0 10.8 %all-to-all-done.2.g = bf16[8,8,8,1024]{3,2,1,0:T(8,128)(2,1)S(1)} async-done(((bf16[8,8,8,1024]{3,2,1,0:T(8,128)(2,1)}), bf16[8,8,8,1024]{3,2,1,0:T(8,128)(2,1)S(1)}, u32[]{:S(2)}, u32[]{:S(2)}) %all-to-all-start.2) | async-done | bytes 1048608 | tf_op jit(solution)/shard_map/all_to_all | solution.py:18
  66.8 1.2 copy-done.1
  68.9 3.1 %shard_map.77 = (bf16[8,4,64,256]{3,2,1,0:T(8,128)(2,1)}, bf16[512,1024]{1,0:T(8,128)(2,1)S(1)}) custom-call(s32[3]{0:T(128)S(1)} %pad_add_fusion.where, bf16[8,8,8,1024]{3,2,1,0:T(8,128)(2,1)S(1)} %copy-done.1, bf16[256,1024]{1,0:T(8,128)(2,1)S(1)} %copy-done.2, bf16[256,1024]{1,0:T(8,128)(2,1)S(1)} %collective-permute-done.3.w1, ...), custom_call_target="tpu_custom_call" | custom-call | flops 68719476736 | bytes 171798688 | tf_op jit(solution)/shard_map/pallas_call | solution.py:67
  72.0 5.4 %all-to-all-start.3 = ((bf16[32,64,256]{2,1,0:T(8,128)(2,1)}), bf16[32,64,256]{2,1,0:T(8,128)(2,1)S(1)}, u32[]{:S(2)}, u32[]{:S(2)}) async-start(bf16[32,64,256]{2,1,0:T(8,128)(2,1)} %bitcast.18), calls=%async_computation.4 | async-start | bytes 2097152 | tf_op jit(solution)/shard_map/all_to_all | solution.py:18
  77.4 1.3 fusion.5
  78.8 2.7 %collective-permute-start.11 = (bf16[128,1024]{1,0:T(8,128)(2,1)S(1)}, bf16[128,1024]{1,0:T(8,128)(2,1)S(1)}, u32[]{:S(2)}, u32[]{:S(2)}) collective-permute-start(bf16[128,1024]{1,0:T(8,128)(2,1)S(1)} %get-tuple-element.45), channel_id=1, source_target_pairs={{0,192},{64,0},{128,64},{192,128},{1,193},{65,1},{129,65},{193,129... | collective-permute-start | bytes 786440 | tf_op jit(solution)/shard_map/ppermute | solution.py:23
  81.6 14.9 %collective-permute-done.11 = bf16[128,1024]{1,0:T(8,128)(2,1)S(1)} collective-permute-done((bf16[128,1024]{1,0:T(8,128)(2,1)S(1)}, bf16[128,1024]{1,0:T(8,128)(2,1)S(1)}, u32[]{:S(2)}, u32[]{:S(2)}) %collective-permute-start.11) | collective-permute-done | bytes 262176 | tf_op jit(solution)/shard_map/ppermute | solution.py:23
  96.5 1.9 %collective-permute-done.13 = bf16[128,1024]{1,0:T(8,128)(2,1)S(1)} collective-permute-done((bf16[128,1024]{1,0:T(8,128)(2,1)S(1)}, bf16[128,1024]{1,0:T(8,128)(2,1)S(1)}, u32[]{:S(2)}, u32[]{:S(2)}) %collective-permute-start.13) | collective-permute-done | bytes 262176 | tf_op jit(solution)/shard_map/ppermute | solution.py:23
  98.6 1.5 %collective-permute-start.14 = (bf16[2,128,1024]{2,1,0:T(8,128)(2,1)S(1)}, bf16[2,128,1024]{2,1,0:T(8,128)(2,1)S(1)}, u32[]{:S(2)}, u32[]{:S(2)}) collective-permute-start(bf16[2,128,1024]{2,1,0:T(8,128)(2,1)S(1)} %get-tuple-element.42), channel_id=1, source_target_pairs={{0,64},{64,128},{128,192},{192,0},{1,65},{65,129},{129,193},{193,1... | collective-permute-start | bytes 1572872 | tf_op jit(solution)/shard_map/ppermute | solution.py:23
  100.2 11.5 %collective-permute-done.12 = bf16[2,128,1024]{2,1,0:T(8,128)(2,1)S(1)} collective-permute-done((bf16[2,128,1024]{2,1,0:T(8,128)(2,1)S(1)}, bf16[2,128,1024]{2,1,0:T(8,128)(2,1)S(1)}, u32[]{:S(2)}, u32[]{:S(2)}) %collective-permute-start.12) | collective-permute-done | bytes 524320 | tf_op jit(solution)/shard_map/ppermute | solution.py:23
  113.8 1.6 %convert_bitcast_fusion = bf16[8,8,1024]{2,1,0:T(8,128)(2,1)} fusion(f32[1,8,8,1024]{3,2,1,0:T(8,128)} %reduce-scatter.2.cloned.1.call-done), kind=kLoop, calls=%fused_computation.14 | loop fusion | flops 65536 | bytes 393216 | tf_op jit(solution)/shard_map/convert_element_type | solution.py:109
  115.4 6.0 %all-to-all-start.1 = ((bf16[8,8,1024]{2,1,0:T(8,128)(2,1)}), bf16[8,8,1024]{2,1,0:T(8,128)(2,1)S(1)}, u32[]{:S(2)}, u32[]{:S(2)}) async-start(bf16[8,8,1024]{2,1,0:T(8,128)(2,1)} %convert_bitcast_fusion), calls=%async_computation.2 | async-start | bytes 262144 | tf_op jit(solution)/shard_map/all_to_all | solution.py:18
  122.1 4.6 %all-to-all-done.1 = bf16[8,8,1024]{2,1,0:T(8,128)(2,1)S(1)} async-done(((bf16[8,8,1024]{2,1,0:T(8,128)(2,1)}), bf16[8,8,1024]{2,1,0:T(8,128)(2,1)S(1)}, u32[]{:S(2)}, u32[]{:S(2)}) %all-to-all-start.1) | async-done | bytes 131104 | tf_op jit(solution)/shard_map/all_to_all | solution.py:18
  (58 shorter events, 17.4 us)
Async XLA Ops:
  7.2 20.2 %collective-permute-start.4 = (bf16[256,1024]{1,0:T(8,128)(2,1)}, bf16[256,1024]{1,0:T(8,128)(2,1)S(1)}, u32[]{:S(2)}, u32[]{:S(2)}) collective-permute-start(bf16[256,1024]{1,0:T(8,128)(2,1)} %w0.3), channel_id=1, source_target_pairs={{0,192},{64,0},{128,64},{192,128},{1,193},{65,1},{129,65},{193,129... | collective-permute-start | bytes 1572872 | tf_op jit(solution)/shard_map/ppermute | solution.py:23
  10.8 16.5 %collective-permute-start.3 = (bf16[256,1024]{1,0:T(8,128)(2,1)}, bf16[256,1024]{1,0:T(8,128)(2,1)S(1)}, u32[]{:S(2)}, u32[]{:S(2)}) collective-permute-start(bf16[256,1024]{1,0:T(8,128)(2,1)} %w0.3), channel_id=1, source_target_pairs={{0,64},{64,128},{128,192},{192,0},{1,65},{65,129},{129,193},{193,1... | collective-permute-start | bytes 1572872 | tf_op jit(solution)/shard_map/ppermute | solution.py:23
  12.5 10.4 %collective-permute-start.2 = (bf16[64,256]{1,0:T(8,128)(2,1)S(1)}, bf16[64,256]{1,0:T(8,128)(2,1)S(1)}, u32[]{:S(2)}, u32[]{:S(2)}) collective-permute-start(bf16[64,256]{1,0:T(8,128)(2,1)S(1)} %get-tuple-element.48), channel_id=1, source_target_pairs={{0,192},{64,0},{128,64},{192,128},{1,193},{65,1},{129,65},{193,129... | collective-permute-start | bytes 98312 | tf_op jit(solution)/shard_map/ppermute | solution.py:23
  15.3 8.8 %collective-permute-start.1 = (bf16[64,256]{1,0:T(8,128)(2,1)S(1)}, bf16[64,256]{1,0:T(8,128)(2,1)S(1)}, u32[]{:S(2)}, u32[]{:S(2)}) collective-permute-start(bf16[64,256]{1,0:T(8,128)(2,1)S(1)} %get-tuple-element.49), channel_id=1, source_target_pairs={{0,128},{64,192},{128,0},{192,64},{1,129},{65,193},{129,1},{193,65... | collective-permute-start | bytes 98312 | tf_op jit(solution)/shard_map/ppermute | solution.py:23
  15.3 10.5 %collective-permute-start = (bf16[64,256]{1,0:T(8,128)(2,1)S(1)}, bf16[64,256]{1,0:T(8,128)(2,1)S(1)}, u32[]{:S(2)}, u32[]{:S(2)}) collective-permute-start(bf16[64,256]{1,0:T(8,128)(2,1)S(1)} %get-tuple-element.50), channel_id=1, source_target_pairs={{0,64},{64,128},{128,192},{192,0},{1,65},{65,129},{129,193},{193,1... | collective-permute-start | bytes 98312 | tf_op jit(solution)/shard_map/ppermute | solution.py:23
  15.9 11.4 %all-to-all-start = ((bf16[8,8,1024]{2,1,0:T(8,128)(2,1)}), bf16[8,8,1024]{2,1,0:T(8,128)(2,1)S(1)}, u32[]{:S(2)}, u32[]{:S(2)}) async-start(bf16[8,8,1024]{2,1,0:T(8,128)(2,1)} %bitcast.68), calls=%async_computation | async-start | bytes 262144 | tf_op jit(solution)/shard_map/all_to_all | solution.py:18
  28.4 37.4 %all-to-all-start.2 = ((bf16[8,8,8,1024]{3,2,1,0:T(8,128)(2,1)}), bf16[8,8,8,1024]{3,2,1,0:T(8,128)(2,1)S(1)}, u32[]{:S(2)}, u32[]{:S(2)}) async-start(bf16[8,8,8,1024]{3,2,1,0:T(8,128)(2,1)} %broadcast_in_dim.10), calls=%async_computation.3 | async-start | bytes 2097152 | tf_op jit(solution)/shard_map/all_to_all | solution.py:18
  36.6 13.5 %copy-start.2 = (bf16[256,1024]{1,0:T(8,128)(2,1)S(1)}, bf16[256,1024]{1,0:T(8,128)(2,1)}, u32[]{:S(2)}) copy-start(bf16[256,1024]{1,0:T(8,128)(2,1)} %w0.3) | copy-start | bytes 1572868
  36.6 77.2 %reduce-scatter.2.cloned.1.call-start = ((), (), s32[]{:S(2)}) async-start(), calls=%async_computation.5 | async-start | bytes 2359296 | tf_op jit(solution)/shard_map/reduce_scatter | solution.py:109
  36.7 4.6 %collective-permute-start.7 = (bf16[64,1024]{1,0:T(8,128)(2,1)S(1)}, bf16[64,1024]{1,0:T(8,128)(2,1)S(1)}, u32[]{:S(2)}, u32[]{:S(2)}) collective-permute-start(bf16[64,1024]{1,0:T(8,128)(2,1)S(1)} %pad_maximum_fusion.1), channel_id=1, source_target_pairs={{0,6},{2,0},{4,2},{6,4},{1,7},{3,1},{5,3},{7,5},{8,14},{10,8},{12,... | collective-permute-start | bytes 393224 | tf_op jit(solution)/shard_map/ppermute | solution.py:23
  37.9 5.4 %collective-permute-start.6 = (bf16[64,1024]{1,0:T(8,128)(2,1)S(1)}, bf16[64,1024]{1,0:T(8,128)(2,1)S(1)}, u32[]{:S(2)}, u32[]{:S(2)}) collective-permute-start(bf16[64,1024]{1,0:T(8,128)(2,1)S(1)} %pad_maximum_fusion.1), channel_id=1, source_target_pairs={{0,4},{2,6},{4,0},{6,2},{1,5},{3,7},{5,1},{7,3},{8,12},{10,14},{12... | collective-permute-start | bytes 393224 | tf_op jit(solution)/shard_map/ppermute | solution.py:23
  39.1 5.5 %collective-permute-start.5 = (bf16[64,1024]{1,0:T(8,128)(2,1)S(1)}, bf16[64,1024]{1,0:T(8,128)(2,1)S(1)}, u32[]{:S(2)}, u32[]{:S(2)}) collective-permute-start(bf16[64,1024]{1,0:T(8,128)(2,1)S(1)} %pad_maximum_fusion.1), channel_id=1, source_target_pairs={{0,2},{2,4},{4,6},{6,0},{1,3},{3,5},{5,7},{7,1},{8,10},{10,12},{12... | collective-permute-start | bytes 393224 | tf_op jit(solution)/shard_map/ppermute | solution.py:23
  39.2 9.4 %collective-permute-start.10 = (bf16[128,1024]{1,0:T(8,128)(2,1)S(1)}, bf16[128,1024]{1,0:T(8,128)(2,1)S(1)}, u32[]{:S(2)}, u32[]{:S(2)}) collective-permute-start(bf16[128,1024]{1,0:T(8,128)(2,1)S(1)} %slice.75), channel_id=1, source_target_pairs={{0,192},{64,0},{128,64},{192,128},{1,193},{65,1},{129,65},{193,129... | collective-permute-start | bytes 786440 | tf_op jit(solution)/shard_map/ppermute | solution.py:23
  41.0 7.6 %collective-permute-start.9 = (bf16[128,1024]{1,0:T(8,128)(2,1)S(1)}, bf16[128,1024]{1,0:T(8,128)(2,1)S(1)}, u32[]{:S(2)}, u32[]{:S(2)}) collective-permute-start(bf16[128,1024]{1,0:T(8,128)(2,1)S(1)} %slice.74), channel_id=1, source_target_pairs={{0,64},{64,128},{128,192},{192,0},{1,65},{65,129},{129,193},{193,1... | collective-permute-start | bytes 786440 | tf_op jit(solution)/shard_map/ppermute | solution.py:23
  44.7 5.3 %collective-permute-start.8 = (bf16[4,64,1024]{2,1,0:T(8,128)(2,1)S(1)}, bf16[4,64,1024]{2,1,0:T(8,128)(2,1)S(1)}, u32[]{:S(2)}, u32[]{:S(2)}) collective-permute-start(bf16[4,64,1024]{2,1,0:T(8,128)(2,1)S(1)} %pad_maximum_fusion.own), channel_id=1, source_target_pairs={{0,1},{1,0},{2,3},{3,2},{4,5},{5,4},{6,7},{7,6},{8,9},{9,8},{10,11... | collective-permute-start | bytes 1572872 | tf_op jit(solution)/shard_map/ppermute | solution.py:23
  48.6 1.0 copy-start.5
  66.8 1.2 copy-start.1
  72.0 5.4 %copy-start.6 = (bf16[8,64,1024]{2,1,0:T(8,128)(2,1)S(1)}, bf16[8,64,1024]{2,1,0:T(8,128)(2,1)}, u32[]{:S(2)}) copy-start(bf16[8,64,1024]{2,1,0:T(8,128)(2,1)} %constant_dynamic-update-slice_fusion) | copy-start | bytes 3145732
  72.0 41.6 %all-to-all-start.3 = ((bf16[32,64,256]{2,1,0:T(8,128)(2,1)}), bf16[32,64,256]{2,1,0:T(8,128)(2,1)S(1)}, u32[]{:S(2)}, u32[]{:S(2)}) async-start(bf16[32,64,256]{2,1,0:T(8,128)(2,1)} %bitcast.18), calls=%async_computation.4 | async-start | bytes 2097152 | tf_op jit(solution)/shard_map/all_to_all | solution.py:18
  78.8 17.7 %collective-permute-start.11 = (bf16[128,1024]{1,0:T(8,128)(2,1)S(1)}, bf16[128,1024]{1,0:T(8,128)(2,1)S(1)}, u32[]{:S(2)}, u32[]{:S(2)}) collective-permute-start(bf16[128,1024]{1,0:T(8,128)(2,1)S(1)} %get-tuple-element.45), channel_id=1, source_target_pairs={{0,192},{64,0},{128,64},{192,128},{1,193},{65,1},{129,65},{193,129... | collective-permute-start | bytes 786440 | tf_op jit(solution)/shard_map/ppermute | solution.py:23
  81.4 17.0 %collective-permute-start.13 = (bf16[128,1024]{1,0:T(8,128)(2,1)S(1)}, bf16[128,1024]{1,0:T(8,128)(2,1)S(1)}, u32[]{:S(2)}, u32[]{:S(2)}) collective-permute-start(bf16[128,1024]{1,0:T(8,128)(2,1)S(1)} %get-tuple-element.46), channel_id=1, source_target_pairs={{0,64},{64,128},{128,192},{192,0},{1,65},{65,129},{129,193},{193,1... | collective-permute-start | bytes 786440 | tf_op jit(solution)/shard_map/ppermute | solution.py:23
  98.6 13.1 %collective-permute-start.12 = (bf16[2,128,1024]{2,1,0:T(8,128)(2,1)S(1)}, bf16[2,128,1024]{2,1,0:T(8,128)(2,1)S(1)}, u32[]{:S(2)}, u32[]{:S(2)}) collective-permute-start(bf16[2,128,1024]{2,1,0:T(8,128)(2,1)S(1)} %get-tuple-element.41), channel_id=1, source_target_pairs={{0,192},{64,0},{128,64},{192,128},{1,193},{65,1},{129,65},{193,129... | collective-permute-start | bytes 1572872 | tf_op jit(solution)/shard_map/ppermute | solution.py:23
  98.6 13.8 %collective-permute-start.14 = (bf16[2,128,1024]{2,1,0:T(8,128)(2,1)S(1)}, bf16[2,128,1024]{2,1,0:T(8,128)(2,1)S(1)}, u32[]{:S(2)}, u32[]{:S(2)}) collective-permute-start(bf16[2,128,1024]{2,1,0:T(8,128)(2,1)S(1)} %get-tuple-element.42), channel_id=1, source_target_pairs={{0,64},{64,128},{128,192},{192,0},{1,65},{65,129},{129,193},{193,1... | collective-permute-start | bytes 1572872 | tf_op jit(solution)/shard_map/ppermute | solution.py:23
  115.4 11.3 %all-to-all-start.1 = ((bf16[8,8,1024]{2,1,0:T(8,128)(2,1)}), bf16[8,8,1024]{2,1,0:T(8,128)(2,1)S(1)}, u32[]{:S(2)}, u32[]{:S(2)}) async-start(bf16[8,8,1024]{2,1,0:T(8,128)(2,1)} %convert_bitcast_fusion), calls=%async_computation.2 | async-start | bytes 262144 | tf_op jit(solution)/shard_map/all_to_all | solution.py:18
  (3 other events, 2.6 us)
Sparse Core Ops, SparseCore 0:
  54.3 37.9 reduce-scatter.1

commit v6 on v5

--- a/solution.py
+++ b/solution.py
@@ -43,16 +43,19 @@
             out[:, place(where, e, s, nx)] = total[s * ty : (s + 1) * ty].reshape(nz, j, n)
 
 
-def backward(where, g, w0, w1, w2a, w2b, w3, out, g_rel, rows):
-    nz, nxc, j, n = g.shape
-    ny, ty, r = out.shape[1:]
+def backward(where, g, w0, w1, w2a, w2b, w3, own, other, g_rel, rows):
+    n = g.shape[3]
+    nx, ny, ty, r = own.shape
     half = r // 2
-    for k in range(nxc):
-        rows[k * ty : (k + 1) * ty] = g[:, k].astype(F32).reshape(ty, n).astype(BF)
     for e in range(2):
-        for s in range(nxc // 2):
-            k = e * (nxc // 2) + s
-            at = pl.multiple_of(place(where, e, s, nxc // 2) * ty, ty)
+        for x in range(nx):
+            k = e * nx + x
+            v = g[:, 2 * x + (where[1] ^ e)]
+            rows[k * ty : (k + 1) * ty] = v.astype(F32).reshape(ty, n).astype(BF)
+    for e in range(2):
+        for s in range(nx):
+            k = e * nx + s
+            at = pl.multiple_of((e * nx + ((where[0] - s) & (nx - 1))) * ty, ty)
             g_rel[k * ty : (k + 1) * ty] = rows[pl.ds(at, ty)]
     across = (((1,), (1,)), ((), ()))
     for s, w in enumerate(((w0,), (w1,), (w2a, w2b), (w3,))):
@@ -60,7 +63,9 @@
         width = r // len(w)
         for i, part in enumerate(w):
             v = lax.dot_general(rows[...], part[...], across, preferred_element_type=F32)
-            out[:, at, :, i * width : (i + 1) * width] = v.astype(BF).reshape(nxc, ty, width)
+            v = v.reshape(2, nx, ty, width)
+            own[:, at, :, i * width : (i + 1) * width] = v[0]
+            other[:, at, :, i * width : (i + 1) * width] = v[1].astype(BF)
 
 
 def call(kernel, out_shape, *args, scratch=(), flops):
@@ -107,22 +112,20 @@
         flops=FWD,
     )
     proj = lax.psum_scatter(part, "z", scatter_dimension=0, tiled=False).astype(BF)
-    proj = exchange(proj, XC)
-    proj_out = proj.transpose(1, 0, 2).reshape(j, d)
 
-    part, g = lax.optimization_barrier((part, g))
-    back, g_rel = call(
+    own, back, g_rel = call(
         backward,
         (
-            jax.ShapeDtypeStruct((nx * nc, ny, ty, r), BF),
+            jax.ShapeDtypeStruct((nx, ny, ty, r), F32),
+            jax.ShapeDtypeStruct((nx, ny, ty, r), BF),
             jax.ShapeDtypeStruct((nx * nc * ty, n), BF),
         ),
         where, g, *w,
         scratch=[pltpu.VMEM((nx * nc * ty, n), BF)],
         flops=BWD,
     )
-    mine = exchange(back.reshape(nx * nc * ny, ty, r), ("x", "c", "y"))
-    mine = mine.astype(F32).reshape(nx * nc, t, r).sum(axis=0)
+    mine = (own + shift(back, "c", 1).astype(F32)).astype(BF).reshape(nx * ny, ty, r)
+    mine = exchange(mine, ("x", "y")).astype(F32).reshape(nx, t, r).sum(axis=0)
     grad_attn = (mine * col_gate[None, :]).astype(BF)
 
     a_rel = jnp.concatenate([a, other]).reshape(nx * nc * ty, ny * r)
@@ -131,7 +134,10 @@
     near = gw[1].at[0].add(shift(gw[2, 0].astype(BF), "y", -1).astype(F32))
     far = gw[3].at[1].add(shift(gw[2, 1].astype(BF), "y", 1).astype(F32))
     near, far = shift(near.astype(BF), "y", -1), shift(far.astype(BF), "y", 1)
+    proj = exchange(proj, XC)
+    near, far, proj = lax.optimization_barrier((near, far, proj))
     grad_w = (gw[0] + near.astype(F32) + far.astype(F32)).reshape(r, n)
+    proj_out = proj.transpose(1, 0, 2).reshape(j, d)
     return (proj_out, grad_attn, grad_w)
 
 

time: 135 us -> 117 us (0.87)
  waiting for transfers between devices: 53.5 us -> 31 us
  starting transfers between devices: 45.2 us -> 48.3 us
  other arithmetic: 5.53 us -> 8.36 us
    ppermute x15 -> x16, waiting for transfers between devices: 36.6 us -> 7.59 us  [shift(): return lax.ppermute(v, axis, [(i, (i + s) % n) for i in range(n)])]
    reduce_scatter x1, waiting for transfers between devices: 0.02 us -> 3.43 us  [shards(): lax.psum_scatter(part, 'z', scatter_dimension=0, tiled=False).astype(BF)]
    all_to_all x4, waiting for transfers between devices: 16.9 us -> 20 us  [exchange(): return lax.all_to_all(v, axes, split_axis=0, concat_axis=0, tiled=False)]
    slice x1, local copies, waits for them, and re-layouts: 0.15 us -> 2.54 us  [shards(): far = gw[3].at[1].add(shift(gw[2, 1].astype(BF), 'y', 1).astype(F32))]
    unnamed x19 -> x17, local copies, waits for them, and re-layouts: 5.49 us -> 3.32 us
    ppermute x15 -> x16, starting transfers between devices: 19.6 us -> 21.6 us  [shift(): return lax.ppermute(v, axis, [(i, (i + s) % n) for i in range(n)])]
    scatter-add x1, other arithmetic: 0.15 us -> 2.09 us  [shards(): far = gw[3].at[1].add(shift(gw[2, 1].astype(BF), 'y', 1).astype(F32))]
  transfers between devices with their start and end apart: 20 -> 21, of which waited for: 13 -> 11; matrix products, arithmetic and copies ran while one was open for 5% -> 10% of each run, Pallas kernels for 5% -> 5%
where the time goes in v6:
time: 117 us
  starting transfers between devices  48.3 us (41%)
  waiting for transfers between devices  31 us (26%)
  between operations  14.2 us (12%)
  other arithmetic  8.36 us (7%)
  local copies, waits for them, and re-layouts  8.05 us (7%)
  Pallas kernels  5.6 us (5%)
  matrix products  1.29 us (1%)
    all_to_all x4, starting transfers between devices, exchange(): return lax.all_to_all(v, axes, split_axis=0, concat_axis=0, tiled=False)  26.7 us
    ppermute x16, starting transfers between devices, shift(): return lax.ppermute(v, axis, [(i, (i + s) % n) for i in range(n)])  21.6 us
    all_to_all x4, waiting for transfers between devices, exchange(): return lax.all_to_all(v, axes, split_axis=0, concat_axis=0, tiled=False)  20 us
    ppermute x16, waiting for transfers between devices, shift(): return lax.ppermute(v, axis, [(i, (i + s) % n) for i in range(n)])  7.59 us
    pallas_call x2, Pallas kernels, call(): pl.pallas_call(kernel, out_shape=out_shape, in_specs=[SMEM] + [VMEM] * (l...  5.6 us
    reduce_scatter x1, waiting for transfers between devices, shards(): lax.psum_scatter(part, 'z', scatter_dimension=0, tiled=False).astype(BF)  3.43 us
    unnamed x17, local copies, waits for them, and re-layouts  3.32 us
    slice x1, local copies, waits for them, and re-layouts, shards(): far = gw[3].at[1].add(shift(gw[2, 1].astype(BF), 'y', 1).astype(F32))  2.54 us
  transfers between devices with their start and end apart: 21, of which 11 were waited for; matrix products, arithmetic and copies ran while one was open for 10% of the time, Pallas kernels for 5%

profile of v6, /device:TPU:1, one launch (start us, length us, event | category | flops | bytes accessed | tf_op | source)
XLA Modules:
  0.0 116.8 jit_solution(9719515198975180436)
XLA Ops:
  7.2 3.6 %collective-permute-start.4 = (bf16[256,1024]{1,0:T(8,128)(2,1)}, bf16[256,1024]{1,0:T(8,128)(2,1)S(1)}, u32[]{:S(2)}, u32[]{:S(2)}) collective-permute-start(bf16[256,1024]{1,0:T(8,128)(2,1)} %w0.3), channel_id=1, source_target_pairs={{0,192},{64,0},{128,64},{192,128},{1,193},{65,1},{129,65},{193,129... | collective-permute-start | bytes 1572872 | tf_op jit(solution)/shard_map/ppermute | solution.py:23
  12.5 2.8 %collective-permute-start.2 = (bf16[64,256]{1,0:T(8,128)(2,1)S(1)}, bf16[64,256]{1,0:T(8,128)(2,1)S(1)}, u32[]{:S(2)}, u32[]{:S(2)}) collective-permute-start(bf16[64,256]{1,0:T(8,128)(2,1)S(1)} %get-tuple-element.54), channel_id=1, source_target_pairs={{0,192},{64,0},{128,64},{192,128},{1,193},{65,1},{129,65},{193,129... | collective-permute-start | bytes 98312 | tf_op jit(solution)/shard_map/ppermute | solution.py:23
  16.0 6.1 %all-to-all-start = ((bf16[8,8,1024]{2,1,0:T(8,128)(2,1)}), bf16[8,8,1024]{2,1,0:T(8,128)(2,1)S(1)}, u32[]{:S(2)}, u32[]{:S(2)}) async-start(bf16[8,8,1024]{2,1,0:T(8,128)(2,1)} %bitcast.67), calls=%async_computation | async-start | bytes 262144 | tf_op jit(solution)/shard_map/all_to_all | solution.py:18
  24.1 1.7 %collective-permute-done = bf16[64,256]{1,0:T(8,128)(2,1)S(1)} collective-permute-done((bf16[64,256]{1,0:T(8,128)(2,1)S(1)}, bf16[64,256]{1,0:T(8,128)(2,1)S(1)}, u32[]{:S(2)}, u32[]{:S(2)}) %collective-permute-start) | collective-permute-done | bytes 32800 | tf_op jit(solution)/shard_map/ppermute | solution.py:23
  25.8 1.5 %all-to-all-done = bf16[8,8,1024]{2,1,0:T(8,128)(2,1)S(1)} async-done(((bf16[8,8,1024]{2,1,0:T(8,128)(2,1)}), bf16[8,8,1024]{2,1,0:T(8,128)(2,1)S(1)}, u32[]{:S(2)}, u32[]{:S(2)}) %all-to-all-start) | async-done | bytes 131104 | tf_op jit(solution)/shard_map/all_to_all | solution.py:18
  28.4 8.2 %all-to-all-start.1 = ((bf16[8,8,8,1024]{3,2,1,0:T(8,128)(2,1)}), bf16[8,8,8,1024]{3,2,1,0:T(8,128)(2,1)S(1)}, u32[]{:S(2)}, u32[]{:S(2)}) async-start(bf16[8,8,8,1024]{3,2,1,0:T(8,128)(2,1)} %broadcast_in_dim.10), calls=%async_computation.1 | async-start | bytes 2097152 | tf_op jit(solution)/shard_map/all_to_all | solution.py:18
  39.2 1.8 %collective-permute-start.10 = (bf16[128,1024]{1,0:T(8,128)(2,1)S(1)}, bf16[128,1024]{1,0:T(8,128)(2,1)S(1)}, u32[]{:S(2)}, u32[]{:S(2)}) collective-permute-start(bf16[128,1024]{1,0:T(8,128)(2,1)S(1)} %slice.75), channel_id=1, source_target_pairs={{0,192},{64,0},{128,64},{192,128},{1,193},{65,1},{129,65},{193,129... | collective-permute-start | bytes 786440 | tf_op jit(solution)/shard_map/ppermute | solution.py:23
  41.3 2.0 %collective-permute-done.6 = bf16[64,1024]{1,0:T(8,128)(2,1)S(1)} collective-permute-done((bf16[64,1024]{1,0:T(8,128)(2,1)S(1)}, bf16[64,1024]{1,0:T(8,128)(2,1)S(1)}, u32[]{:S(2)}, u32[]{:S(2)}) %collective-permute-start.6) | collective-permute-done | bytes 131104 | tf_op jit(solution)/shard_map/ppermute | solution.py:23
  43.3 1.3 %collective-permute-done.5 = bf16[64,1024]{1,0:T(8,128)(2,1)S(1)} collective-permute-done((bf16[64,1024]{1,0:T(8,128)(2,1)S(1)}, bf16[64,1024]{1,0:T(8,128)(2,1)S(1)}, u32[]{:S(2)}, u32[]{:S(2)}) %collective-permute-start.5) | collective-permute-done | bytes 131104 | tf_op jit(solution)/shard_map/ppermute | solution.py:23
  44.7 3.8 %collective-permute-start.8 = (bf16[4,64,1024]{2,1,0:T(8,128)(2,1)S(1)}, bf16[4,64,1024]{2,1,0:T(8,128)(2,1)S(1)}, u32[]{:S(2)}, u32[]{:S(2)}) collective-permute-start(bf16[4,64,1024]{2,1,0:T(8,128)(2,1)S(1)} %pad_maximum_fusion.own), channel_id=1, source_target_pairs={{0,1},{1,0},{2,3},{3,2},{4,5},{5,4},{6,7},{7,6},{8,9},{9,8},{10,11... | collective-permute-start | bytes 1572872 | tf_op jit(solution)/shard_map/ppermute | solution.py:23
  50.1 3.4 %shard_map.77 = f32[8,8,8,1024]{3,2,1,0:T(8,128)} custom-call(s32[3]{0:T(128)S(1)} %pad_add_fusion.where, bf16[4,64,1024]{2,1,0:T(8,128)(2,1)S(1)} %pad_maximum_fusion.own, bf16[4,64,1024]{2,1,0:T(8,128)(2,1)S(1)} %collective-permute-done.8.other, bf16[256,1024]{1,0:T(8,128)(2,1)S(1)} %copy-done, bf16[256,1024]{1,0:T(8,128)(2,1)S(1)} %collective-permute-done.3.w1, ...), custom_call_target="tpu_custom_call" | custom-call | flops 1073741824 | bytes 2684354 | tf_op jit(solution)/shard_map/pallas_call | solution.py:72
  55.1 10.7 %all-to-all-done.1.g = bf16[8,8,8,1024]{3,2,1,0:T(8,128)(2,1)S(1)} async-done(((bf16[8,8,8,1024]{3,2,1,0:T(8,128)(2,1)}), bf16[8,8,8,1024]{3,2,1,0:T(8,128)(2,1)S(1)}, u32[]{:S(2)}, u32[]{:S(2)}) %all-to-all-start.1) | async-done | bytes 1048608 | tf_op jit(solution)/shard_map/all_to_all | solution.py:18
  66.8 2.1 %shard_map.76 = (f32[4,4,64,256]{3,2,1,0:T(8,128)S(1)}, bf16[4,4,64,256]{3,2,1,0:T(8,128)(2,1)S(1)}, bf16[512,1024]{1,0:T(8,128)(2,1)S(1)}) custom-call(s32[3]{0:T(128)S(1)} %pad_add_fusion.where, bf16[8,8,8,1024]{3,2,1,0:T(8,128)(2,1)S(1)} %all-to-all-done.1.g, bf16[256,1024]{1,0:T(8,128)(2,1)S(1)} %copy-done, ...), custom_call_target="tpu_custom_call" | custom-call | flops 68719476736 | bytes 171798688 | tf_op jit(solution)/shard_map/pallas_call | solution.py:72
  69.7 1.3 %fusion.5 = (bf16[1024,1024]{1,0:T(8,128)(2,1)S(1)}, f32[1024,1024]{1,0:T(8,128)S(1)}) fusion(bf16[512,1024]{1,0:T(8,128)(2,1)S(1)} %bitcast.57, bf16[512,1024]{1,0:T(8,128)(2,1)S(1)} %get-tuple-element.41), kind=kOutput, calls=%fused_computation.29 | convolution fusion | flops 1074790400 | bytes 8388608 | tf_op jit(solution)/shard_map/dot_general | solution.py:132
  71.1 2.3 %collective-permute-start.13 = (bf16[128,1024]{1,0:T(8,128)(2,1)S(1)}, bf16[128,1024]{1,0:T(8,128)(2,1)S(1)}, u32[]{:S(2)}, u32[]{:S(2)}) collective-permute-start(bf16[128,1024]{1,0:T(8,128)(2,1)S(1)} %get-tuple-element.51), channel_id=1, source_target_pairs={{0,64},{64,128},{128,192},{192,0},{1,65},{65,129},{129,193},{193,1... | collective-permute-start | bytes 786440 | tf_op jit(solution)/shard_map/ppermute | solution.py:23
  74.8 3.6 %all-to-all-start.3 = ((bf16[16,64,256]{2,1,0:T(8,128)(2,1)}), bf16[16,64,256]{2,1,0:T(8,128)(2,1)S(1)}, u32[]{:S(2)}, u32[]{:S(2)}) async-start(bf16[16,64,256]{2,1,0:T(8,128)(2,1)} %bitcast.26), calls=%async_computation.4 | async-start | bytes 1048576 | tf_op jit(solution)/shard_map/all_to_all | solution.py:18
  78.4 2.5 %fusion.4 = (bf16[256,1024]{1,0:T(8,128)(2,1)S(1)}, bf16[256,1024]{1,0:T(8,128)(2,1)}) fusion(f32[1024,1024]{1,0:T(8,128)} %copy-done.3), kind=kLoop, calls=%fused_computation.28 | loop fusion | bytes 2097152 | tf_op jit(solution)/shard_map/slice | solution.py:135
  81.0 2.1 %fusion.1 = (bf16[2,128,1024]{2,1,0:T(8,128)(2,1)S(1)}, bf16[2,128,1024]{2,1,0:T(8,128)(2,1)}) fusion(bf16[2,128,1024]{2,1,0:T(8,128)(2,1)S(1)} %bitcast.63, f32[1024,1024]{1,0:T(8,128)} %copy-done.3, bf16[128,1024]{1,0:T(8,128)(2,1)S(1)} %collective-permute-done.13, bf16[2,128,1024]{2,1,0:T(8,128)(2,1)} %bitcast.16, ...), kind=kLoop, calls=%fused_computation.5 | loop fusion | flops 524288 | bytes 2621440 | tf_op jit(solution)/shard_map/scatter-add | solution.py:135
  84.3 1.4 %collective-permute-start.12 = (bf16[2,128,1024]{2,1,0:T(8,128)(2,1)}, bf16[2,128,1024]{2,1,0:T(8,128)(2,1)S(1)}, u32[]{:S(2)}, u32[]{:S(2)}) collective-permute-start(bf16[2,128,1024]{2,1,0:T(8,128)(2,1)} %get-tuple-element.48), channel_id=1, source_target_pairs={{0,192},{64,0},{128,64},{192,128},{1,193},{65,1},{129,65},{193,129... | collective-permute-start | bytes 1572872 | tf_op jit(solution)/shard_map/ppermute | solution.py:23
  85.7 3.1 %all-to-all-done.3 = bf16[16,64,256]{2,1,0:T(8,128)(2,1)S(1)} async-done(((bf16[16,64,256]{2,1,0:T(8,128)(2,1)}), bf16[16,64,256]{2,1,0:T(8,128)(2,1)S(1)}, u32[]{:S(2)}, u32[]{:S(2)}) %all-to-all-start.3) | async-done | bytes 524320 | tf_op jit(solution)/shard_map/all_to_all | solution.py:18
  88.9 3.4 %reduce-scatter.2.cloned.1.call-done = f32[1,8,8,1024]{3,2,1,0:T(8,128)} async-done(((f32[8,8,8,1024]{3,2,1,0:T(8,128)}), f32[1,8,8,1024]{3,2,1,0:T(8,128)}) %reduce-scatter.2.cloned.1.call-update) | async-done | bytes 262160 | tf_op jit(solution)/shard_map/reduce_scatter | solution.py:114
  92.3 1.6 %convert_bitcast_fusion = bf16[8,8,1024]{2,1,0:T(8,128)(2,1)} fusion(f32[1,8,8,1024]{3,2,1,0:T(8,128)} %reduce-scatter.2.cloned.1.call-done), kind=kLoop, calls=%fused_computation.15 | loop fusion | flops 65536 | bytes 393216 | tf_op jit(solution)/shard_map/convert_element_type | solution.py:114
  94.0 8.8 %all-to-all-start.2 = ((bf16[8,8,1024]{2,1,0:T(8,128)(2,1)}), bf16[8,8,1024]{2,1,0:T(8,128)(2,1)S(1)}, u32[]{:S(2)}, u32[]{:S(2)}) async-start(bf16[8,8,1024]{2,1,0:T(8,128)(2,1)} %convert_bitcast_fusion), calls=%async_computation.3 | async-start | bytes 262144 | tf_op jit(solution)/shard_map/all_to_all | solution.py:18
  103.5 4.6 %all-to-all-done.2 = bf16[8,8,1024]{2,1,0:T(8,128)(2,1)S(1)} async-done(((bf16[8,8,1024]{2,1,0:T(8,128)(2,1)}), bf16[8,8,1024]{2,1,0:T(8,128)(2,1)S(1)}, u32[]{:S(2)}, u32[]{:S(2)}) %all-to-all-start.2) | async-done | bytes 131104 | tf_op jit(solution)/shard_map/all_to_all | solution.py:18
  (59 shorter events, 18.6 us)
Async XLA Ops:
  7.2 42.9 %copy-start = (bf16[256,1024]{1,0:T(8,128)(2,1)S(1)}, bf16[256,1024]{1,0:T(8,128)(2,1)}, u32[]{:S(2)}) copy-start(bf16[256,1024]{1,0:T(8,128)(2,1)} %w0.3) | copy-start | bytes 1572868
  7.2 20.2 %collective-permute-start.4 = (bf16[256,1024]{1,0:T(8,128)(2,1)}, bf16[256,1024]{1,0:T(8,128)(2,1)S(1)}, u32[]{:S(2)}, u32[]{:S(2)}) collective-permute-start(bf16[256,1024]{1,0:T(8,128)(2,1)} %w0.3), channel_id=1, source_target_pairs={{0,192},{64,0},{128,64},{192,128},{1,193},{65,1},{129,65},{193,129... | collective-permute-start | bytes 1572872 | tf_op jit(solution)/shard_map/ppermute | solution.py:23
  10.8 16.5 %collective-permute-start.3 = (bf16[256,1024]{1,0:T(8,128)(2,1)}, bf16[256,1024]{1,0:T(8,128)(2,1)S(1)}, u32[]{:S(2)}, u32[]{:S(2)}) collective-permute-start(bf16[256,1024]{1,0:T(8,128)(2,1)} %w0.3), channel_id=1, source_target_pairs={{0,64},{64,128},{128,192},{192,0},{1,65},{65,129},{129,193},{193,1... | collective-permute-start | bytes 1572872 | tf_op jit(solution)/shard_map/ppermute | solution.py:23
  12.5 10.4 %collective-permute-start.2 = (bf16[64,256]{1,0:T(8,128)(2,1)S(1)}, bf16[64,256]{1,0:T(8,128)(2,1)S(1)}, u32[]{:S(2)}, u32[]{:S(2)}) collective-permute-start(bf16[64,256]{1,0:T(8,128)(2,1)S(1)} %get-tuple-element.54), channel_id=1, source_target_pairs={{0,192},{64,0},{128,64},{192,128},{1,193},{65,1},{129,65},{193,129... | collective-permute-start | bytes 98312 | tf_op jit(solution)/shard_map/ppermute | solution.py:23
  15.3 8.8 %collective-permute-start.1 = (bf16[64,256]{1,0:T(8,128)(2,1)S(1)}, bf16[64,256]{1,0:T(8,128)(2,1)S(1)}, u32[]{:S(2)}, u32[]{:S(2)}) collective-permute-start(bf16[64,256]{1,0:T(8,128)(2,1)S(1)} %get-tuple-element.55), channel_id=1, source_target_pairs={{0,128},{64,192},{128,0},{192,64},{1,129},{65,193},{129,1},{193,65... | collective-permute-start | bytes 98312 | tf_op jit(solution)/shard_map/ppermute | solution.py:23
  15.3 10.5 %collective-permute-start = (bf16[64,256]{1,0:T(8,128)(2,1)S(1)}, bf16[64,256]{1,0:T(8,128)(2,1)S(1)}, u32[]{:S(2)}, u32[]{:S(2)}) collective-permute-start(bf16[64,256]{1,0:T(8,128)(2,1)S(1)} %get-tuple-element.56), channel_id=1, source_target_pairs={{0,64},{64,128},{128,192},{192,0},{1,65},{65,129},{129,193},{193,1... | collective-permute-start | bytes 98312 | tf_op jit(solution)/shard_map/ppermute | solution.py:23
  16.0 11.4 %all-to-all-start = ((bf16[8,8,1024]{2,1,0:T(8,128)(2,1)}), bf16[8,8,1024]{2,1,0:T(8,128)(2,1)S(1)}, u32[]{:S(2)}, u32[]{:S(2)}) async-start(bf16[8,8,1024]{2,1,0:T(8,128)(2,1)} %bitcast.67), calls=%async_computation | async-start | bytes 262144 | tf_op jit(solution)/shard_map/all_to_all | solution.py:18
  28.4 37.4 %all-to-all-start.1 = ((bf16[8,8,8,1024]{3,2,1,0:T(8,128)(2,1)}), bf16[8,8,8,1024]{3,2,1,0:T(8,128)(2,1)S(1)}, u32[]{:S(2)}, u32[]{:S(2)}) async-start(bf16[8,8,8,1024]{3,2,1,0:T(8,128)(2,1)} %broadcast_in_dim.10), calls=%async_computation.1 | async-start | bytes 2097152 | tf_op jit(solution)/shard_map/all_to_all | solution.py:18
  36.6 55.7 %reduce-scatter.2.cloned.1.call-start = ((), (), s32[]{:S(2)}) async-start(), calls=%async_computation.5 | async-start | bytes 2359296 | tf_op jit(solution)/shard_map/reduce_scatter | solution.py:114
  36.7 4.6 %collective-permute-start.7 = (bf16[64,1024]{1,0:T(8,128)(2,1)S(1)}, bf16[64,1024]{1,0:T(8,128)(2,1)S(1)}, u32[]{:S(2)}, u32[]{:S(2)}) collective-permute-start(bf16[64,1024]{1,0:T(8,128)(2,1)S(1)} %pad_maximum_fusion.1), channel_id=1, source_target_pairs={{0,6},{2,0},{4,2},{6,4},{1,7},{3,1},{5,3},{7,5},{8,14},{10,8},{12,... | collective-permute-start | bytes 393224 | tf_op jit(solution)/shard_map/ppermute | solution.py:23
  37.9 5.4 %collective-permute-start.6 = (bf16[64,1024]{1,0:T(8,128)(2,1)S(1)}, bf16[64,1024]{1,0:T(8,128)(2,1)S(1)}, u32[]{:S(2)}, u32[]{:S(2)}) collective-permute-start(bf16[64,1024]{1,0:T(8,128)(2,1)S(1)} %pad_maximum_fusion.1), channel_id=1, source_target_pairs={{0,4},{2,6},{4,0},{6,2},{1,5},{3,7},{5,1},{7,3},{8,12},{10,14},{12... | collective-permute-start | bytes 393224 | tf_op jit(solution)/shard_map/ppermute | solution.py:23
  39.1 5.5 %collective-permute-start.5 = (bf16[64,1024]{1,0:T(8,128)(2,1)S(1)}, bf16[64,1024]{1,0:T(8,128)(2,1)S(1)}, u32[]{:S(2)}, u32[]{:S(2)}) collective-permute-start(bf16[64,1024]{1,0:T(8,128)(2,1)S(1)} %pad_maximum_fusion.1), channel_id=1, source_target_pairs={{0,2},{2,4},{4,6},{6,0},{1,3},{3,5},{5,7},{7,1},{8,10},{10,12},{12... | collective-permute-start | bytes 393224 | tf_op jit(solution)/shard_map/ppermute | solution.py:23
  39.2 9.4 %collective-permute-start.10 = (bf16[128,1024]{1,0:T(8,128)(2,1)S(1)}, bf16[128,1024]{1,0:T(8,128)(2,1)S(1)}, u32[]{:S(2)}, u32[]{:S(2)}) collective-permute-start(bf16[128,1024]{1,0:T(8,128)(2,1)S(1)} %slice.75), channel_id=1, source_target_pairs={{0,192},{64,0},{128,64},{192,128},{1,193},{65,1},{129,65},{193,129... | collective-permute-start | bytes 786440 | tf_op jit(solution)/shard_map/ppermute | solution.py:23
  41.0 7.6 %collective-permute-start.9 = (bf16[128,1024]{1,0:T(8,128)(2,1)S(1)}, bf16[128,1024]{1,0:T(8,128)(2,1)S(1)}, u32[]{:S(2)}, u32[]{:S(2)}) collective-permute-start(bf16[128,1024]{1,0:T(8,128)(2,1)S(1)} %slice.74), channel_id=1, source_target_pairs={{0,64},{64,128},{128,192},{192,0},{1,65},{65,129},{129,193},{193,1... | collective-permute-start | bytes 786440 | tf_op jit(solution)/shard_map/ppermute | solution.py:23
  44.7 5.3 %collective-permute-start.8 = (bf16[4,64,1024]{2,1,0:T(8,128)(2,1)S(1)}, bf16[4,64,1024]{2,1,0:T(8,128)(2,1)S(1)}, u32[]{:S(2)}, u32[]{:S(2)}) collective-permute-start(bf16[4,64,1024]{2,1,0:T(8,128)(2,1)S(1)} %pad_maximum_fusion.own), channel_id=1, source_target_pairs={{0,1},{1,0},{2,3},{3,2},{4,5},{5,4},{6,7},{7,6},{8,9},{9,8},{10,11... | collective-permute-start | bytes 1572872 | tf_op jit(solution)/shard_map/ppermute | solution.py:23
  66.8 2.9 %copy-start.5 = (bf16[8,64,1024]{2,1,0:T(8,128)(2,1)S(1)}, bf16[8,64,1024]{2,1,0:T(8,128)(2,1)}, u32[]{:S(2)}) copy-start(bf16[8,64,1024]{2,1,0:T(8,128)(2,1)} %constant_dynamic-update-slice_fusion) | copy-start | bytes 3145732
  68.9 5.0 %collective-permute-start.15 = (bf16[4,4,64,256]{3,2,1,0:T(8,128)(2,1)S(1)}, bf16[4,4,64,256]{3,2,1,0:T(8,128)(2,1)S(1)}, u32[]{:S(2)}, u32[]{:S(2)}) collective-permute-start(bf16[4,4,64,256]{3,2,1,0:T(8,128)(2,1)S(1)} %get-tuple-element.44), channel_id=1, source_target_pairs={{0,1},{1,0},{2,3},{3,2},{4,5},{5,4},{6,7},{7,6},{8,9},{9,8},{10,11... | collective-permute-start | bytes 1572872 | tf_op jit(solution)/shard_map/ppermute | solution.py:23
  71.0 3.8 %copy-start.3 = (f32[1024,1024]{1,0:T(8,128)}, f32[1024,1024]{1,0:T(8,128)S(1)}, u32[]{:S(2)}) copy-start(f32[1024,1024]{1,0:T(8,128)S(1)} %get-tuple-element.58) | copy-start | bytes 12582916
  71.1 9.9 %collective-permute-start.13 = (bf16[128,1024]{1,0:T(8,128)(2,1)S(1)}, bf16[128,1024]{1,0:T(8,128)(2,1)S(1)}, u32[]{:S(2)}, u32[]{:S(2)}) collective-permute-start(bf16[128,1024]{1,0:T(8,128)(2,1)S(1)} %get-tuple-element.51), channel_id=1, source_target_pairs={{0,64},{64,128},{128,192},{192,0},{1,65},{65,129},{129,193},{193,1... | collective-permute-start | bytes 786440 | tf_op jit(solution)/shard_map/ppermute | solution.py:23
  73.4 7.6 %collective-permute-start.11 = (bf16[128,1024]{1,0:T(8,128)(2,1)S(1)}, bf16[128,1024]{1,0:T(8,128)(2,1)S(1)}, u32[]{:S(2)}, u32[]{:S(2)}) collective-permute-start(bf16[128,1024]{1,0:T(8,128)(2,1)S(1)} %get-tuple-element.52), channel_id=1, source_target_pairs={{0,192},{64,0},{128,64},{192,128},{1,193},{65,1},{129,65},{193,129... | collective-permute-start | bytes 786440 | tf_op jit(solution)/shard_map/ppermute | solution.py:23
  74.8 14.0 %all-to-all-start.3 = ((bf16[16,64,256]{2,1,0:T(8,128)(2,1)}), bf16[16,64,256]{2,1,0:T(8,128)(2,1)S(1)}, u32[]{:S(2)}, u32[]{:S(2)}) async-start(bf16[16,64,256]{2,1,0:T(8,128)(2,1)} %bitcast.26), calls=%async_computation.4 | async-start | bytes 1048576 | tf_op jit(solution)/shard_map/all_to_all | solution.py:18
  83.1 20.4 %collective-permute-start.14 = (bf16[2,128,1024]{2,1,0:T(8,128)(2,1)S(1)}, bf16[2,128,1024]{2,1,0:T(8,128)(2,1)S(1)}, u32[]{:S(2)}, u32[]{:S(2)}) collective-permute-start(bf16[2,128,1024]{2,1,0:T(8,128)(2,1)S(1)} %get-tuple-element.47), channel_id=1, source_target_pairs={{0,64},{64,128},{128,192},{192,0},{1,65},{65,129},{129,193},{193,1... | collective-permute-start | bytes 1572872 | tf_op jit(solution)/shard_map/ppermute | solution.py:23
  84.3 19.2 %collective-permute-start.12 = (bf16[2,128,1024]{2,1,0:T(8,128)(2,1)}, bf16[2,128,1024]{2,1,0:T(8,128)(2,1)S(1)}, u32[]{:S(2)}, u32[]{:S(2)}) collective-permute-start(bf16[2,128,1024]{2,1,0:T(8,128)(2,1)} %get-tuple-element.48), channel_id=1, source_target_pairs={{0,192},{64,0},{128,64},{192,128},{1,193},{65,1},{129,65},{193,129... | collective-permute-start | bytes 1572872 | tf_op jit(solution)/shard_map/ppermute | solution.py:23
  94.0 14.1 %all-to-all-start.2 = ((bf16[8,8,1024]{2,1,0:T(8,128)(2,1)}), bf16[8,8,1024]{2,1,0:T(8,128)(2,1)S(1)}, u32[]{:S(2)}, u32[]{:S(2)}) async-start(bf16[8,8,1024]{2,1,0:T(8,128)(2,1)} %convert_bitcast_fusion), calls=%async_computation.3 | async-start | bytes 262144 | tf_op jit(solution)/shard_map/all_to_all | solution.py:18
  (3 other events, 2.6 us)
Sparse Core Ops, SparseCore 0:
  54.4 37.9 reduce-scatter.1

commit v7 on v6

--- a/solution.py
+++ b/solution.py
@@ -9,7 +9,7 @@
 F32 = jnp.float32
 XC = ("x", "c")
 FWD = 2**30
-BWD = 2**36
+BWD = 7 * 2**31
 VMEM = pl.BlockSpec(memory_space=pltpu.VMEM)
 SMEM = pl.BlockSpec(memory_space=pltpu.SMEM)
 
@@ -104,6 +104,7 @@
     g = exchange(jnp.broadcast_to(g[None], (nz,) + g.shape), "z")
     a = jnp.stack([a] + [shift(a, "x", s) for s in range(1, nx)])
     w2a, w2b = shift(w1[:half], "y", 1), shift(w3[half:], "y", -1)
+    a, w2a, w2b = lax.optimization_barrier((a, w2a, w2b))
     other = shift(a, "c", 1)
     w = (w_out, w1, w2a, w2b, w3)
 

time: 117 us -> 119 us (1.017)
  waiting for transfers between devices: 31 us -> 27.4 us
  local copies, waits for them, and re-layouts: 8.05 us -> 10.6 us
  other arithmetic: 8.36 us -> 10.4 us
    reduce_scatter x1, waiting for transfers between devices: 3.43 us -> 0.02 us  [shards(): lax.psum_scatter(part, 'z', scatter_dimension=0, tiled=False).astype(BF)]
    unnamed x17 -> x21, local copies, waits for them, and re-layouts: 3.32 us -> 6.04 us
    ppermute x16, starting transfers between devices: 21.6 us -> 23.2 us  [shift(): return lax.ppermute(v, axis, [(i, (i + s) % n) for i in range(n)])]
    all_to_all x4, starting transfers between devices: 26.7 us -> 25.1 us  [exchange(): return lax.all_to_all(v, axes, split_axis=0, concat_axis=0, tiled=False)]
    all_to_all x4, waiting for transfers between devices: 20 us -> 18.5 us  [exchange(): return lax.all_to_all(v, axes, split_axis=0, concat_axis=0, tiled=False)]
    ppermute x16, waiting for transfers between devices: 7.59 us -> 8.96 us  [shift(): return lax.ppermute(v, axis, [(i, (i + s) % n) for i in range(n)])]
  transfers between devices with their start and end apart: 21 -> 21, of which waited for: 11 -> 9; matrix products, arithmetic and copies ran while one was open for 10% -> 12% of each run, Pallas kernels for 5% -> 5%
where the time goes in v7:
time: 119 us; the launch traced here: 118 us
  starting transfers between devices  48.3 us (41%)
  waiting for transfers between devices  27.4 us (23%)
  between operations  14.2 us (12%)
  local copies, waits for them, and re-layouts  10.6 us (9%)
  other arithmetic  10.4 us (9%)
  Pallas kernels  5.6 us (5%)
  matrix products  1.29 us (1%)
    all_to_all x4, starting transfers between devices, exchange(): return lax.all_to_all(v, axes, split_axis=0, concat_axis=0, tiled=False)  25.1 us
    ppermute x16, starting transfers between devices, shift(): return lax.ppermute(v, axis, [(i, (i + s) % n) for i in range(n)])  23.2 us
    all_to_all x4, waiting for transfers between devices, exchange(): return lax.all_to_all(v, axes, split_axis=0, concat_axis=0, tiled=False)  18.5 us
    ppermute x16, waiting for transfers between devices, shift(): return lax.ppermute(v, axis, [(i, (i + s) % n) for i in range(n)])  8.96 us
    unnamed x21, local copies, waits for them, and re-layouts  6.04 us
    pallas_call x2, Pallas kernels, call(): pl.pallas_call(kernel, out_shape=out_shape, in_specs=[SMEM] + [VMEM] * (l...  5.6 us
    slice x1, local copies, waits for them, and re-layouts, shards(): far = gw[3].at[1].add(shift(gw[2, 1].astype(BF), 'y', 1).astype(F32))  2.53 us
  transfers between devices with their start and end apart: 21, of which 9 were waited for; matrix products, arithmetic and copies ran while one was open for 12% of the time, Pallas kernels for 5%

profile of v7, /device:TPU:1, one launch (start us, length us, event | category | flops | bytes accessed | tf_op | source)
XLA Modules:
  0.0 117.9 jit_solution(16723810847586701178)
XLA Ops:
  7.2 3.6 %collective-permute-start.4 = (bf16[256,1024]{1,0:T(8,128)(2,1)}, bf16[256,1024]{1,0:T(8,128)(2,1)S(1)}, u32[]{:S(2)}, u32[]{:S(2)}) collective-permute-start(bf16[256,1024]{1,0:T(8,128)(2,1)} %w0.3), channel_id=1, source_target_pairs={{0,192},{64,0},{128,64},{192,128},{1,193},{65,1},{129,65},{193,129... | collective-permute-start | bytes 1572872 | tf_op jit(solution)/shard_map/ppermute | solution.py:23
  12.5 2.8 %collective-permute-start.2 = (bf16[64,256]{1,0:T(8,128)(2,1)S(1)}, bf16[64,256]{1,0:T(8,128)(2,1)S(1)}, u32[]{:S(2)}, u32[]{:S(2)}) collective-permute-start(bf16[64,256]{1,0:T(8,128)(2,1)S(1)} %get-tuple-element.60), channel_id=1, source_target_pairs={{0,192},{64,0},{128,64},{192,128},{1,193},{65,1},{129,65},{193,129... | collective-permute-start | bytes 98312 | tf_op jit(solution)/shard_map/ppermute | solution.py:23
  15.9 6.1 %all-to-all-start = ((bf16[8,8,1024]{2,1,0:T(8,128)(2,1)}), bf16[8,8,1024]{2,1,0:T(8,128)(2,1)S(1)}, u32[]{:S(2)}, u32[]{:S(2)}) async-start(bf16[8,8,1024]{2,1,0:T(8,128)(2,1)} %bitcast.60), calls=%async_computation | async-start | bytes 262144 | tf_op jit(solution)/shard_map/all_to_all | solution.py:18
  24.1 1.7 %collective-permute-done = bf16[64,256]{1,0:T(8,128)(2,1)S(1)} collective-permute-done((bf16[64,256]{1,0:T(8,128)(2,1)S(1)}, bf16[64,256]{1,0:T(8,128)(2,1)S(1)}, u32[]{:S(2)}, u32[]{:S(2)}) %collective-permute-start) | collective-permute-done | bytes 32800 | tf_op jit(solution)/shard_map/ppermute | solution.py:23
  25.8 1.5 %all-to-all-done = bf16[8,8,1024]{2,1,0:T(8,128)(2,1)S(1)} async-done(((bf16[8,8,1024]{2,1,0:T(8,128)(2,1)}), bf16[8,8,1024]{2,1,0:T(8,128)(2,1)S(1)}, u32[]{:S(2)}, u32[]{:S(2)}) %all-to-all-start) | async-done | bytes 131104 | tf_op jit(solution)/shard_map/all_to_all | solution.py:18
  28.1 2.0 %collective-permute-start.9 = (bf16[128,1024]{1,0:T(8,128)(2,1)}, bf16[128,1024]{1,0:T(8,128)(2,1)S(1)}, u32[]{:S(2)}, u32[]{:S(2)}) collective-permute-start(bf16[128,1024]{1,0:T(8,128)(2,1)} %slice.75), channel_id=1, source_target_pairs={{0,192},{64,0},{128,64},{192,128},{1,193},{65,1},{129,65},{193,129... | collective-permute-start | bytes 786440 | tf_op jit(solution)/shard_map/ppermute | solution.py:23
  33.5 8.2 %all-to-all-start.1 = ((bf16[8,8,8,1024]{3,2,1,0:T(8,128)(2,1)}), bf16[8,8,8,1024]{3,2,1,0:T(8,128)(2,1)S(1)}, u32[]{:S(2)}, u32[]{:S(2)}) async-start(bf16[8,8,8,1024]{3,2,1,0:T(8,128)(2,1)} %broadcast_in_dim.10), calls=%async_computation.1 | async-start | bytes 2097152 | tf_op jit(solution)/shard_map/all_to_all | solution.py:18
  44.3 3.1 %collective-permute-start.10 = (bf16[4,64,1024]{2,1,0:T(8,128)(2,1)S(1)}, bf16[4,64,1024]{2,1,0:T(8,128)(2,1)S(1)}, u32[]{:S(2)}, u32[]{:S(2)}) collective-permute-start(bf16[4,64,1024]{2,1,0:T(8,128)(2,1)S(1)} %pad_maximum_fusion.1.own), channel_id=1, source_target_pairs={{0,1},{1,0},{2,3},{3,2},{4,5},{5,4},{6,7},{7,6},{8,9},{9,8},{10,11... | collective-permute-start | bytes 1572872 | tf_op jit(solution)/shard_map/ppermute | solution.py:23
  47.5 1.5 %collective-permute-done.10.other = bf16[4,64,1024]{2,1,0:T(8,128)(2,1)S(1)} collective-permute-done((bf16[4,64,1024]{2,1,0:T(8,128)(2,1)S(1)}, bf16[4,64,1024]{2,1,0:T(8,128)(2,1)S(1)}, u32[]{:S(2)}, u32[]{:S(2)}) %collective-permute-start.10) | collective-permute-done | bytes 524320 | tf_op jit(solution)/shard_map/ppermute | solution.py:23
  50.9 3.4 %shard_map.77 = f32[8,8,8,1024]{3,2,1,0:T(8,128)} custom-call(s32[3]{0:T(128)S(1)} %pad_add_fusion.where, bf16[4,64,1024]{2,1,0:T(8,128)(2,1)S(1)} %pad_maximum_fusion.1.own, bf16[4,64,1024]{2,1,0:T(8,128)(2,1)S(1)} %collective-permute-done.10.other, bf16[256,1024]{1,0:T(8,128)(2,1)S(1)} %copy-done, bf16[256,1024]{1,0:T(8,128)(2,1)S(1)} %collective-permute-done.3.w1, ...), custom_call_target="tpu_custom_call" | custom-call | flops 1073741824 | bytes 2684354 | tf_op jit(solution)/shard_map/pallas_call | solution.py:72
  55.5 13.0 %all-to-all-done.1.g = bf16[8,8,8,1024]{3,2,1,0:T(8,128)(2,1)S(1)} async-done(((bf16[8,8,8,1024]{3,2,1,0:T(8,128)(2,1)}), bf16[8,8,8,1024]{3,2,1,0:T(8,128)(2,1)S(1)}, u32[]{:S(2)}, u32[]{:S(2)}) %all-to-all-start.1) | async-done | bytes 1048608 | tf_op jit(solution)/shard_map/all_to_all | solution.py:18
  70.5 2.2 %shard_map.76 = (f32[4,4,64,256]{3,2,1,0:T(8,128)S(1)}, bf16[4,4,64,256]{3,2,1,0:T(8,128)(2,1)S(1)}, bf16[512,1024]{1,0:T(8,128)(2,1)S(1)}) custom-call(s32[3]{0:T(128)S(1)} %pad_add_fusion.where, bf16[8,8,8,1024]{3,2,1,0:T(8,128)(2,1)S(1)} %all-to-all-done.1.g, bf16[256,1024]{1,0:T(8,128)(2,1)S(1)} %copy-done.1, ...), custom_call_target="tpu_custom_call" | custom-call | flops 15032385536 | bytes 37580964 | tf_op jit(solution)/shard_map/pallas_call | solution.py:72
  72.6 3.3 %collective-permute-start.15 = (bf16[4,4,64,256]{3,2,1,0:T(8,128)(2,1)S(1)}, bf16[4,4,64,256]{3,2,1,0:T(8,128)(2,1)S(1)}, u32[]{:S(2)}, u32[]{:S(2)}) collective-permute-start(bf16[4,4,64,256]{3,2,1,0:T(8,128)(2,1)S(1)} %get-tuple-element.50), channel_id=1, source_target_pairs={{0,1},{1,0},{2,3},{3,2},{4,5},{5,4},{6,7},{7,6},{8,9},{9,8},{10,11... | collective-permute-start | bytes 1572872 | tf_op jit(solution)/shard_map/ppermute | solution.py:23
  77.3 1.4 %collective-permute-start.13 = (bf16[128,1024]{1,0:T(8,128)(2,1)S(1)}, bf16[128,1024]{1,0:T(8,128)(2,1)S(1)}, u32[]{:S(2)}, u32[]{:S(2)}) collective-permute-start(bf16[128,1024]{1,0:T(8,128)(2,1)S(1)} %get-tuple-element.57), channel_id=1, source_target_pairs={{0,64},{64,128},{128,192},{192,0},{1,65},{65,129},{129,193},{193,1... | collective-permute-start | bytes 786440 | tf_op jit(solution)/shard_map/ppermute | solution.py:23
  78.7 1.3 %collective-permute-start.11 = (bf16[128,1024]{1,0:T(8,128)(2,1)S(1)}, bf16[128,1024]{1,0:T(8,128)(2,1)S(1)}, u32[]{:S(2)}, u32[]{:S(2)}) collective-permute-start(bf16[128,1024]{1,0:T(8,128)(2,1)S(1)} %get-tuple-element.58), channel_id=1, source_target_pairs={{0,192},{64,0},{128,64},{192,128},{1,193},{65,1},{129,65},{193,129... | collective-permute-start | bytes 786440 | tf_op jit(solution)/shard_map/ppermute | solution.py:23
  81.1 5.2 %all-to-all-start.3 = ((bf16[16,64,256]{2,1,0:T(8,128)(2,1)}), bf16[16,64,256]{2,1,0:T(8,128)(2,1)S(1)}, u32[]{:S(2)}, u32[]{:S(2)}) async-start(bf16[16,64,256]{2,1,0:T(8,128)(2,1)} %bitcast.26), calls=%async_computation.4 | async-start | bytes 1048576 | tf_op jit(solution)/shard_map/all_to_all | solution.py:18
  86.3 2.5 %fusion.4 = (bf16[256,1024]{1,0:T(8,128)(2,1)S(1)}, bf16[256,1024]{1,0:T(8,128)(2,1)}) fusion(f32[1024,1024]{1,0:T(8,128)} %copy-done.5), kind=kLoop, calls=%fused_computation.24 | loop fusion | bytes 2097152 | tf_op jit(solution)/shard_map/slice | solution.py:136
  88.9 2.1 %fusion.1 = (bf16[2,128,1024]{2,1,0:T(8,128)(2,1)S(1)}, bf16[2,128,1024]{2,1,0:T(8,128)(2,1)}) fusion(bf16[2,128,1024]{2,1,0:T(8,128)(2,1)S(1)} %bitcast.58, f32[1024,1024]{1,0:T(8,128)} %copy-done.5, bf16[128,1024]{1,0:T(8,128)(2,1)S(1)} %collective-permute-done.13, bf16[2,128,1024]{2,1,0:T(8,128)(2,1)} %bitcast.16, ...), kind=kLoop, calls=%fused_computation.6 | loop fusion | flops 524288 | bytes 2621440 | tf_op jit(solution)/shard_map/scatter-add | solution.py:136
  90.9 1.4 %collective-permute-start.14 = (bf16[2,128,1024]{2,1,0:T(8,128)(2,1)S(1)}, bf16[2,128,1024]{2,1,0:T(8,128)(2,1)S(1)}, u32[]{:S(2)}, u32[]{:S(2)}) collective-permute-start(bf16[2,128,1024]{2,1,0:T(8,128)(2,1)S(1)} %get-tuple-element.53), channel_id=1, source_target_pairs={{0,64},{64,128},{128,192},{192,0},{1,65},{65,129},{129,193},{193,1... | collective-permute-start | bytes 1572872 | tf_op jit(solution)/shard_map/ppermute | solution.py:23
  92.3 1.3 %collective-permute-start.12 = (bf16[2,128,1024]{2,1,0:T(8,128)(2,1)}, bf16[2,128,1024]{2,1,0:T(8,128)(2,1)S(1)}, u32[]{:S(2)}, u32[]{:S(2)}) collective-permute-start(bf16[2,128,1024]{2,1,0:T(8,128)(2,1)} %get-tuple-element.54), channel_id=1, source_target_pairs={{0,192},{64,0},{128,64},{192,128},{1,193},{65,1},{129,65},{193,129... | collective-permute-start | bytes 1572872 | tf_op jit(solution)/shard_map/ppermute | solution.py:23
  93.6 3.0 %all-to-all-done.3 = bf16[16,64,256]{2,1,0:T(8,128)(2,1)S(1)} async-done(((bf16[16,64,256]{2,1,0:T(8,128)(2,1)}), bf16[16,64,256]{2,1,0:T(8,128)(2,1)S(1)}, u32[]{:S(2)}, u32[]{:S(2)}) %all-to-all-start.3) | async-done | bytes 524320 | tf_op jit(solution)/shard_map/all_to_all | solution.py:18
  96.7 1.6 %convert_bitcast_fusion = bf16[8,8,1024]{2,1,0:T(8,128)(2,1)} fusion(f32[1,8,8,1024]{3,2,1,0:T(8,128)} %reduce-scatter.2.cloned.1.call-done), kind=kLoop, calls=%fused_computation.16 | loop fusion | flops 65536 | bytes 393216 | tf_op jit(solution)/shard_map/convert_element_type | solution.py:115
  98.4 5.6 %all-to-all-start.2 = ((bf16[8,8,1024]{2,1,0:T(8,128)(2,1)}), bf16[8,8,1024]{2,1,0:T(8,128)(2,1)S(1)}, u32[]{:S(2)}, u32[]{:S(2)}) async-start(bf16[8,8,1024]{2,1,0:T(8,128)(2,1)} %convert_bitcast_fusion), calls=%async_computation.3 | async-start | bytes 262144 | tf_op jit(solution)/shard_map/all_to_all | solution.py:18
  104.6 3.8 %collective-permute-done.14 = bf16[2,128,1024]{2,1,0:T(8,128)(2,1)S(1)} collective-permute-done((bf16[2,128,1024]{2,1,0:T(8,128)(2,1)S(1)}, bf16[2,128,1024]{2,1,0:T(8,128)(2,1)S(1)}, u32[]{:S(2)}, u32[]{:S(2)}) %collective-permute-start.14) | collective-permute-done | bytes 524320 | tf_op jit(solution)/shard_map/ppermute | solution.py:23
  (63 shorter events, 22.1 us)
Async XLA Ops:
  7.2 20.2 %collective-permute-start.4 = (bf16[256,1024]{1,0:T(8,128)(2,1)}, bf16[256,1024]{1,0:T(8,128)(2,1)S(1)}, u32[]{:S(2)}, u32[]{:S(2)}) collective-permute-start(bf16[256,1024]{1,0:T(8,128)(2,1)} %w0.3), channel_id=1, source_target_pairs={{0,192},{64,0},{128,64},{192,128},{1,193},{65,1},{129,65},{193,129... | collective-permute-start | bytes 1572872 | tf_op jit(solution)/shard_map/ppermute | solution.py:23
  10.8 16.5 %collective-permute-start.3 = (bf16[256,1024]{1,0:T(8,128)(2,1)}, bf16[256,1024]{1,0:T(8,128)(2,1)S(1)}, u32[]{:S(2)}, u32[]{:S(2)}) collective-permute-start(bf16[256,1024]{1,0:T(8,128)(2,1)} %w0.3), channel_id=1, source_target_pairs={{0,64},{64,128},{128,192},{192,0},{1,65},{65,129},{129,193},{193,1... | collective-permute-start | bytes 1572872 | tf_op jit(solution)/shard_map/ppermute | solution.py:23
  12.5 10.4 %collective-permute-start.2 = (bf16[64,256]{1,0:T(8,128)(2,1)S(1)}, bf16[64,256]{1,0:T(8,128)(2,1)S(1)}, u32[]{:S(2)}, u32[]{:S(2)}) collective-permute-start(bf16[64,256]{1,0:T(8,128)(2,1)S(1)} %get-tuple-element.60), channel_id=1, source_target_pairs={{0,192},{64,0},{128,64},{192,128},{1,193},{65,1},{129,65},{193,129... | collective-permute-start | bytes 98312 | tf_op jit(solution)/shard_map/ppermute | solution.py:23
  15.3 8.8 %collective-permute-start.1 = (bf16[64,256]{1,0:T(8,128)(2,1)S(1)}, bf16[64,256]{1,0:T(8,128)(2,1)S(1)}, u32[]{:S(2)}, u32[]{:S(2)}) collective-permute-start(bf16[64,256]{1,0:T(8,128)(2,1)S(1)} %get-tuple-element.61), channel_id=1, source_target_pairs={{0,128},{64,192},{128,0},{192,64},{1,129},{65,193},{129,1},{193,65... | collective-permute-start | bytes 98312 | tf_op jit(solution)/shard_map/ppermute | solution.py:23
  15.3 10.5 %collective-permute-start = (bf16[64,256]{1,0:T(8,128)(2,1)S(1)}, bf16[64,256]{1,0:T(8,128)(2,1)S(1)}, u32[]{:S(2)}, u32[]{:S(2)}) collective-permute-start(bf16[64,256]{1,0:T(8,128)(2,1)S(1)} %get-tuple-element.62), channel_id=1, source_target_pairs={{0,64},{64,128},{128,192},{192,0},{1,65},{65,129},{129,193},{193,1... | collective-permute-start | bytes 98312 | tf_op jit(solution)/shard_map/ppermute | solution.py:23
  15.9 11.4 %all-to-all-start = ((bf16[8,8,1024]{2,1,0:T(8,128)(2,1)}), bf16[8,8,1024]{2,1,0:T(8,128)(2,1)S(1)}, u32[]{:S(2)}, u32[]{:S(2)}) async-start(bf16[8,8,1024]{2,1,0:T(8,128)(2,1)} %bitcast.60), calls=%async_computation | async-start | bytes 262144 | tf_op jit(solution)/shard_map/all_to_all | solution.py:18
  28.1 15.5 %collective-permute-start.9 = (bf16[128,1024]{1,0:T(8,128)(2,1)}, bf16[128,1024]{1,0:T(8,128)(2,1)S(1)}, u32[]{:S(2)}, u32[]{:S(2)}) collective-permute-start(bf16[128,1024]{1,0:T(8,128)(2,1)} %slice.75), channel_id=1, source_target_pairs={{0,192},{64,0},{128,64},{192,128},{1,193},{65,1},{129,65},{193,129... | collective-permute-start | bytes 786440 | tf_op jit(solution)/shard_map/ppermute | solution.py:23
  30.1 13.5 %collective-permute-start.8 = (bf16[128,1024]{1,0:T(8,128)(2,1)S(1)}, bf16[128,1024]{1,0:T(8,128)(2,1)S(1)}, u32[]{:S(2)}, u32[]{:S(2)}) collective-permute-start(bf16[128,1024]{1,0:T(8,128)(2,1)S(1)} %slice.74), channel_id=1, source_target_pairs={{0,64},{64,128},{128,192},{192,0},{1,65},{65,129},{129,193},{193,1... | collective-permute-start | bytes 786440 | tf_op jit(solution)/shard_map/ppermute | solution.py:23
  30.3 11.4 %collective-permute-start.7 = (bf16[64,1024]{1,0:T(8,128)(2,1)S(1)}, bf16[64,1024]{1,0:T(8,128)(2,1)S(1)}, u32[]{:S(2)}, u32[]{:S(2)}) collective-permute-start(bf16[64,1024]{1,0:T(8,128)(2,1)S(1)} %pad_maximum_fusion.2), channel_id=1, source_target_pairs={{0,6},{2,0},{4,2},{6,4},{1,7},{3,1},{5,3},{7,5},{8,14},{10,8},{12,... | collective-permute-start | bytes 393224 | tf_op jit(solution)/shard_map/ppermute | solution.py:23
  31.2 10.5 %collective-permute-start.6 = (bf16[64,1024]{1,0:T(8,128)(2,1)S(1)}, bf16[64,1024]{1,0:T(8,128)(2,1)S(1)}, u32[]{:S(2)}, u32[]{:S(2)}) collective-permute-start(bf16[64,1024]{1,0:T(8,128)(2,1)S(1)} %pad_maximum_fusion.2), channel_id=1, source_target_pairs={{0,4},{2,6},{4,0},{6,2},{1,5},{3,7},{5,1},{7,3},{8,12},{10,14},{12... | collective-permute-start | bytes 393224 | tf_op jit(solution)/shard_map/ppermute | solution.py:23
  32.4 9.4 %collective-permute-start.5 = (bf16[64,1024]{1,0:T(8,128)(2,1)S(1)}, bf16[64,1024]{1,0:T(8,128)(2,1)S(1)}, u32[]{:S(2)}, u32[]{:S(2)}) collective-permute-start(bf16[64,1024]{1,0:T(8,128)(2,1)S(1)} %pad_maximum_fusion.2), channel_id=1, source_target_pairs={{0,2},{2,4},{4,6},{6,0},{1,3},{3,5},{5,7},{7,1},{8,10},{10,12},{12... | collective-permute-start | bytes 393224 | tf_op jit(solution)/shard_map/ppermute | solution.py:23
  33.5 35.0 %all-to-all-start.1 = ((bf16[8,8,8,1024]{3,2,1,0:T(8,128)(2,1)}), bf16[8,8,8,1024]{3,2,1,0:T(8,128)(2,1)S(1)}, u32[]{:S(2)}, u32[]{:S(2)}) async-start(bf16[8,8,8,1024]{3,2,1,0:T(8,128)(2,1)} %broadcast_in_dim.10), calls=%async_computation.1 | async-start | bytes 2097152 | tf_op jit(solution)/shard_map/all_to_all | solution.py:18
  41.7 55.1 %reduce-scatter.2.cloned.1.call-start = ((), (), s32[]{:S(2)}) async-start(), calls=%async_computation.5 | async-start | bytes 2359296 | tf_op jit(solution)/shard_map/reduce_scatter | solution.py:115
  44.3 4.7 %collective-permute-start.10 = (bf16[4,64,1024]{2,1,0:T(8,128)(2,1)S(1)}, bf16[4,64,1024]{2,1,0:T(8,128)(2,1)S(1)}, u32[]{:S(2)}, u32[]{:S(2)}) collective-permute-start(bf16[4,64,1024]{2,1,0:T(8,128)(2,1)S(1)} %pad_maximum_fusion.1.own), channel_id=1, source_target_pairs={{0,1},{1,0},{2,3},{3,2},{4,5},{5,4},{6,7},{7,6},{8,9},{9,8},{10,11... | collective-permute-start | bytes 1572872 | tf_op jit(solution)/shard_map/ppermute | solution.py:23
  68.5 1.0 copy-start.1
  70.5 5.5 %copy-start.6 = (bf16[8,64,1024]{2,1,0:T(8,128)(2,1)S(1)}, bf16[8,64,1024]{2,1,0:T(8,128)(2,1)}, u32[]{:S(2)}) copy-start(bf16[8,64,1024]{2,1,0:T(8,128)(2,1)} %pad_maximum_fusion) | copy-start | bytes 3145732
  72.6 7.5 %collective-permute-start.15 = (bf16[4,4,64,256]{3,2,1,0:T(8,128)(2,1)S(1)}, bf16[4,4,64,256]{3,2,1,0:T(8,128)(2,1)S(1)}, u32[]{:S(2)}, u32[]{:S(2)}) collective-permute-start(bf16[4,4,64,256]{3,2,1,0:T(8,128)(2,1)S(1)} %get-tuple-element.50), channel_id=1, source_target_pairs={{0,1},{1,0},{2,3},{3,2},{4,5},{5,4},{6,7},{7,6},{8,9},{9,8},{10,11... | collective-permute-start | bytes 1572872 | tf_op jit(solution)/shard_map/ppermute | solution.py:23
  77.2 3.9 %copy-start.5 = (f32[1024,1024]{1,0:T(8,128)}, f32[1024,1024]{1,0:T(8,128)S(1)}, u32[]{:S(2)}) copy-start(f32[1024,1024]{1,0:T(8,128)S(1)} %get-tuple-element.64) | copy-start | bytes 12582916
  77.3 11.6 %collective-permute-start.13 = (bf16[128,1024]{1,0:T(8,128)(2,1)S(1)}, bf16[128,1024]{1,0:T(8,128)(2,1)S(1)}, u32[]{:S(2)}, u32[]{:S(2)}) collective-permute-start(bf16[128,1024]{1,0:T(8,128)(2,1)S(1)} %get-tuple-element.57), channel_id=1, source_target_pairs={{0,64},{64,128},{128,192},{192,0},{1,65},{65,129},{129,193},{193,1... | collective-permute-start | bytes 786440 | tf_op jit(solution)/shard_map/ppermute | solution.py:23
  78.7 10.2 %collective-permute-start.11 = (bf16[128,1024]{1,0:T(8,128)(2,1)S(1)}, bf16[128,1024]{1,0:T(8,128)(2,1)S(1)}, u32[]{:S(2)}, u32[]{:S(2)}) collective-permute-start(bf16[128,1024]{1,0:T(8,128)(2,1)S(1)} %get-tuple-element.58), channel_id=1, source_target_pairs={{0,192},{64,0},{128,64},{192,128},{1,193},{65,1},{129,65},{193,129... | collective-permute-start | bytes 786440 | tf_op jit(solution)/shard_map/ppermute | solution.py:23
  81.1 15.6 %all-to-all-start.3 = ((bf16[16,64,256]{2,1,0:T(8,128)(2,1)}), bf16[16,64,256]{2,1,0:T(8,128)(2,1)S(1)}, u32[]{:S(2)}, u32[]{:S(2)}) async-start(bf16[16,64,256]{2,1,0:T(8,128)(2,1)} %bitcast.26), calls=%async_computation.4 | async-start | bytes 1048576 | tf_op jit(solution)/shard_map/all_to_all | solution.py:18
  90.9 17.4 %collective-permute-start.14 = (bf16[2,128,1024]{2,1,0:T(8,128)(2,1)S(1)}, bf16[2,128,1024]{2,1,0:T(8,128)(2,1)S(1)}, u32[]{:S(2)}, u32[]{:S(2)}) collective-permute-start(bf16[2,128,1024]{2,1,0:T(8,128)(2,1)S(1)} %get-tuple-element.53), channel_id=1, source_target_pairs={{0,64},{64,128},{128,192},{192,0},{1,65},{65,129},{129,193},{193,1... | collective-permute-start | bytes 1572872 | tf_op jit(solution)/shard_map/ppermute | solution.py:23
  92.3 16.1 %collective-permute-start.12 = (bf16[2,128,1024]{2,1,0:T(8,128)(2,1)}, bf16[2,128,1024]{2,1,0:T(8,128)(2,1)S(1)}, u32[]{:S(2)}, u32[]{:S(2)}) collective-permute-start(bf16[2,128,1024]{2,1,0:T(8,128)(2,1)} %get-tuple-element.54), channel_id=1, source_target_pairs={{0,192},{64,0},{128,64},{192,128},{1,193},{65,1},{129,65},{193,129... | collective-permute-start | bytes 1572872 | tf_op jit(solution)/shard_map/ppermute | solution.py:23
  98.4 10.8 %all-to-all-start.2 = ((bf16[8,8,1024]{2,1,0:T(8,128)(2,1)}), bf16[8,8,1024]{2,1,0:T(8,128)(2,1)S(1)}, u32[]{:S(2)}, u32[]{:S(2)}) async-start(bf16[8,8,1024]{2,1,0:T(8,128)(2,1)} %convert_bitcast_fusion), calls=%async_computation.3 | async-start | bytes 262144 | tf_op jit(solution)/shard_map/all_to_all | solution.py:18
  (7 other events, 5.7 us)
Sparse Core Ops, SparseCore 0:
  54.5 38.7 reduce-scatter.1

commit v8 on v6

--- a/solution.py
+++ b/solution.py
@@ -40,7 +40,7 @@
         total += jnp.dot(rows[:, 2 * r + half : 3 * r], w2b[...], preferred_element_type=F32)
         total += jnp.dot(rows[:, 3 * r :], w3[...], preferred_element_type=F32)
         for s in range(nx):
-            out[:, place(where, e, s, nx)] = total[s * ty : (s + 1) * ty].reshape(nz, j, n)
+            out[:, place(where, e, s, nx)] = total[s * ty : (s + 1) * ty].reshape(nz, j, n).astype(BF)
 
 
 def backward(where, g, w0, w1, w2a, w2b, w3, own, other, g_rel, rows):
@@ -101,17 +101,18 @@
     a = [a[0]] + [shift(a[s], "y", s) for s in range(1, ny)]
     a = jnp.concatenate(a, axis=1)
     a, g, w1, w3 = lax.optimization_barrier((a, g, w1, w3))
-    g = exchange(jnp.broadcast_to(g[None], (nz,) + g.shape), "z")
+    g = lax.all_gather(g.reshape(nx * nc * j, n), "z", axis=0, tiled=True)
+    g = g.reshape(nz, nx * nc, j, n)
     a = jnp.stack([a] + [shift(a, "x", s) for s in range(1, nx)])
     w2a, w2b = shift(w1[:half], "y", 1), shift(w3[half:], "y", -1)
     other = shift(a, "c", 1)
     w = (w_out, w1, w2a, w2b, w3)
 
     part = call(
-        forward, jax.ShapeDtypeStruct((nz, nx * nc, j, n), F32), where, a, other, *w,
+        forward, jax.ShapeDtypeStruct((nz, nx * nc, j, n), BF), where, a, other, *w,
         flops=FWD,
     )
-    proj = lax.psum_scatter(part, "z", scatter_dimension=0, tiled=False).astype(BF)
+    proj = exchange(part, "z").astype(F32).sum(axis=0).astype(BF)
 
     own, back, g_rel = call(
         backward,

time: 117 us -> 131 us (1.12)
  waiting for transfers between devices: 31 us -> 42.2 us
  starting transfers between devices: 48.3 us -> 50.1 us
    all_gather x0 -> x1, waiting for transfers between devices: none -> 15.7 us  [shards(): g = lax.all_gather(g.reshape(nx * nc * j, n), 'z', axis=0, tiled=True)]
    all_to_all x4, waiting for transfers between devices: 20 us -> 12.4 us  [exchange(): return lax.all_to_all(v, axes, split_axis=0, concat_axis=0, tiled=False)]
    ppermute x16, waiting for transfers between devices: 7.59 us -> 14.1 us  [shift(): return lax.ppermute(v, axis, [(i, (i + s) % n) for i in range(n)])]
    ppermute x16, starting transfers between devices: 21.6 us -> 27.3 us  [shift(): return lax.ppermute(v, axis, [(i, (i + s) % n) for i in range(n)])]
    all_to_all x4, starting transfers between devices: 26.7 us -> 22.8 us  [exchange(): return lax.all_to_all(v, axes, split_axis=0, concat_axis=0, tiled=False)]
    reduce_scatter x1 -> x0, waiting for transfers between devices: 3.43 us -> none  [shards(): lax.psum_scatter(part, 'z', scatter_dimension=0, tiled=False).astype(BF)]
    reduce_sum x0 -> x1, other arithmetic: none -> 2.09 us  [shards(): proj = exchange(part, 'z').astype(F32).sum(axis=0).astype(BF)]
    unnamed x17 -> x21, local copies, waits for them, and re-layouts: 3.32 us -> 5.16 us
  transfers between devices with their start and end apart: 21 -> 21, of which waited for: 11 -> 12; matrix products, arithmetic and copies ran while one was open for 10% -> 10% of each run, Pallas kernels for 5% -> 4%
where the time goes in v8:
time: 131 us
  starting transfers between devices  50.1 us (38%)
  waiting for transfers between devices  42.2 us (32%)
  between operations  14.2 us (11%)
  other arithmetic  8.93 us (7%)
  local copies, waits for them, and re-layouts  8.6 us (7%)
  Pallas kernels  5.19 us (4%)
    ppermute x16, starting transfers between devices, shift(): return lax.ppermute(v, axis, [(i, (i + s) % n) for i in range(n)])  27.3 us
    all_to_all x4, starting transfers between devices, exchange(): return lax.all_to_all(v, axes, split_axis=0, concat_axis=0, tiled=False)  22.8 us
    all_gather x1, waiting for transfers between devices, shards(): g = lax.all_gather(g.reshape(nx * nc * j, n), 'z', axis=0, tiled=True)  15.7 us
    ppermute x16, waiting for transfers between devices, shift(): return lax.ppermute(v, axis, [(i, (i + s) % n) for i in range(n)])  14.1 us
    all_to_all x4, waiting for transfers between devices, exchange(): return lax.all_to_all(v, axes, split_axis=0, concat_axis=0, tiled=False)  12.4 us
    pallas_call x2, Pallas kernels, call(): pl.pallas_call(kernel, out_shape=out_shape, in_specs=[SMEM] + [VMEM] * (l...  5.19 us
    unnamed x21, local copies, waits for them, and re-layouts  5.16 us
  transfers between devices with their start and end apart: 21, of which 12 were waited for; matrix products, arithmetic and copies ran while one was open for 10% of the time, Pallas kernels for 4%

profile of v8, /device:TPU:1, one launch (start us, length us, event | category | flops | bytes accessed | tf_op | source)
XLA Modules:
  0.0 130.5 jit_solution(13018228227160856268)
XLA Ops:
  7.2 3.6 %collective-permute-start.4 = (bf16[256,1024]{1,0:T(8,128)(2,1)}, bf16[256,1024]{1,0:T(8,128)(2,1)S(1)}, u32[]{:S(2)}, u32[]{:S(2)}) collective-permute-start(bf16[256,1024]{1,0:T(8,128)(2,1)} %w0.3), channel_id=1, source_target_pairs={{0,192},{64,0},{128,64},{192,128},{1,193},{65,1},{129,65},{193,129... | collective-permute-start | bytes 1572872 | tf_op jit(solution)/shard_map/ppermute | solution.py:23
  12.5 2.8 %collective-permute-start.2 = (bf16[64,256]{1,0:T(8,128)(2,1)S(1)}, bf16[64,256]{1,0:T(8,128)(2,1)S(1)}, u32[]{:S(2)}, u32[]{:S(2)}) collective-permute-start(bf16[64,256]{1,0:T(8,128)(2,1)S(1)} %get-tuple-element.54), channel_id=1, source_target_pairs={{0,192},{64,0},{128,64},{192,128},{1,193},{65,1},{129,65},{193,129... | collective-permute-start | bytes 98312 | tf_op jit(solution)/shard_map/ppermute | solution.py:23
  16.0 6.1 %all-to-all-start = ((bf16[8,8,1024]{2,1,0:T(8,128)(2,1)}), bf16[8,8,1024]{2,1,0:T(8,128)(2,1)S(1)}, u32[]{:S(2)}, u32[]{:S(2)}) async-start(bf16[8,8,1024]{2,1,0:T(8,128)(2,1)} %bitcast.68), calls=%async_computation | async-start | bytes 262144 | tf_op jit(solution)/shard_map/all_to_all | solution.py:18
  24.1 1.7 %collective-permute-done = bf16[64,256]{1,0:T(8,128)(2,1)S(1)} collective-permute-done((bf16[64,256]{1,0:T(8,128)(2,1)S(1)}, bf16[64,256]{1,0:T(8,128)(2,1)S(1)}, u32[]{:S(2)}, u32[]{:S(2)}) %collective-permute-start) | collective-permute-done | bytes 32800 | tf_op jit(solution)/shard_map/ppermute | solution.py:23
  25.8 1.5 %all-to-all-done = bf16[8,8,1024]{2,1,0:T(8,128)(2,1)S(1)} async-done(((bf16[8,8,1024]{2,1,0:T(8,128)(2,1)}), bf16[8,8,1024]{2,1,0:T(8,128)(2,1)S(1)}, u32[]{:S(2)}, u32[]{:S(2)}) %all-to-all-start) | async-done | bytes 131104 | tf_op jit(solution)/shard_map/all_to_all | solution.py:18
  30.5 1.8 %collective-permute-start.10 = (bf16[128,1024]{1,0:T(8,128)(2,1)S(1)}, bf16[128,1024]{1,0:T(8,128)(2,1)S(1)}, u32[]{:S(2)}, u32[]{:S(2)}) collective-permute-start(bf16[128,1024]{1,0:T(8,128)(2,1)S(1)} %slice.75), channel_id=1, source_target_pairs={{0,192},{64,0},{128,64},{192,128},{1,193},{65,1},{129,65},{193,129... | collective-permute-start | bytes 786440 | tf_op jit(solution)/shard_map/ppermute | solution.py:23
  32.7 2.0 %collective-permute-done.6 = bf16[64,1024]{1,0:T(8,128)(2,1)S(1)} collective-permute-done((bf16[64,1024]{1,0:T(8,128)(2,1)S(1)}, bf16[64,1024]{1,0:T(8,128)(2,1)S(1)}, u32[]{:S(2)}, u32[]{:S(2)}) %collective-permute-start.6) | collective-permute-done | bytes 131104 | tf_op jit(solution)/shard_map/ppermute | solution.py:23
  34.7 1.7 %collective-permute-done.5 = bf16[64,1024]{1,0:T(8,128)(2,1)S(1)} collective-permute-done((bf16[64,1024]{1,0:T(8,128)(2,1)S(1)}, bf16[64,1024]{1,0:T(8,128)(2,1)S(1)}, u32[]{:S(2)}, u32[]{:S(2)}) %collective-permute-start.5) | collective-permute-done | bytes 131104 | tf_op jit(solution)/shard_map/ppermute | solution.py:23
  36.4 3.3 %collective-permute-start.8 = (bf16[4,64,1024]{2,1,0:T(8,128)(2,1)S(1)}, bf16[4,64,1024]{2,1,0:T(8,128)(2,1)S(1)}, u32[]{:S(2)}, u32[]{:S(2)}) collective-permute-start(bf16[4,64,1024]{2,1,0:T(8,128)(2,1)S(1)} %pad_maximum_fusion.own), channel_id=1, source_target_pairs={{0,1},{1,0},{2,3},{3,2},{4,5},{5,4},{6,7},{7,6},{8,9},{9,8},{10,11... | collective-permute-start | bytes 1572872 | tf_op jit(solution)/shard_map/ppermute | solution.py:23
  41.2 3.0 %shard_map.77 = bf16[8,8,8,1024]{3,2,1,0:T(8,128)(2,1)} custom-call(s32[3]{0:T(128)S(1)} %pad_add_fusion.where, bf16[4,64,1024]{2,1,0:T(8,128)(2,1)S(1)} %pad_maximum_fusion.own, bf16[4,64,1024]{2,1,0:T(8,128)(2,1)S(1)} %collective-permute-done.8.other, bf16[256,1024]{1,0:T(8,128)(2,1)S(1)} %copy-done, bf16[256,1024]{1,0:T(8,128)(2,1)S(1)} %collective-permute-done.3.w1, ...), custom_call_target="tpu_custom_call" | custom-call | flops 1073741824 | bytes 2684354 | tf_op jit(solution)/shard_map/pallas_call | solution.py:72
  44.9 8.2 %all-to-all-start.1 = ((bf16[8,8,8,1024]{3,2,1,0:T(8,128)(2,1)}), bf16[8,8,8,1024]{3,2,1,0:T(8,128)(2,1)}, u32[]{:S(2)}, u32[]{:S(2)}) async-start(bf16[8,8,8,1024]{3,2,1,0:T(8,128)(2,1)} %shard_map.77), calls=%async_computation.1 | async-start | bytes 2097152 | tf_op jit(solution)/shard_map/all_to_all | solution.py:18
  54.0 15.7 %all-gather.2.cloned.1.call-done = bf16[512,1024]{1,0:T(8,128)(2,1)} async-done(((bf16[64,1024]{1,0:T(8,128)(2,1)}), bf16[512,1024]{1,0:T(8,128)(2,1)}) %all-gather.2.cloned.1.call-update) | async-done | bytes 1048592 | tf_op jit(solution)/shard_map/all_gather | solution.py:104
  71.8 2.2 %shard_map.76 = (f32[4,4,64,256]{3,2,1,0:T(8,128)S(1)}, bf16[4,4,64,256]{3,2,1,0:T(8,128)(2,1)S(1)}, bf16[512,1024]{1,0:T(8,128)(2,1)S(1)}) custom-call(s32[3]{0:T(128)S(1)} %pad_add_fusion.where, bf16[8,8,8,1024]{3,2,1,0:T(8,128)(2,1)S(1)} %bitcast.55, bf16[256,1024]{1,0:T(8,128)(2,1)S(1)} %copy-done, bf16[256,1024]{1,0:T(8,128)(2,1)S(1)} %collective-permute-done.3.w1, ...), custom_call_target="tpu_custom_call" | custom-call | flops 68719476736 | bytes 171798688 | tf_op jit(solution)/shard_map/pallas_call | solution.py:72
  74.0 7.0 %collective-permute-start.15 = (bf16[4,4,64,256]{3,2,1,0:T(8,128)(2,1)S(1)}, bf16[4,4,64,256]{3,2,1,0:T(8,128)(2,1)S(1)}, u32[]{:S(2)}, u32[]{:S(2)}) collective-permute-start(bf16[4,4,64,256]{3,2,1,0:T(8,128)(2,1)S(1)} %get-tuple-element.44), channel_id=1, source_target_pairs={{0,1},{1,0},{2,3},{3,2},{4,5},{5,4},{6,7},{7,6},{8,9},{9,8},{10,11... | collective-permute-start | bytes 1572872 | tf_op jit(solution)/shard_map/ppermute | solution.py:23
  82.3 2.5 %collective-permute-start.13 = (bf16[128,1024]{1,0:T(8,128)(2,1)S(1)}, bf16[128,1024]{1,0:T(8,128)(2,1)S(1)}, u32[]{:S(2)}, u32[]{:S(2)}) collective-permute-start(bf16[128,1024]{1,0:T(8,128)(2,1)S(1)} %get-tuple-element.51), channel_id=1, source_target_pairs={{0,64},{64,128},{128,192},{192,0},{1,65},{65,129},{129,193},{193,1... | collective-permute-start | bytes 786440 | tf_op jit(solution)/shard_map/ppermute | solution.py:23
  86.2 5.3 %collective-permute-done.13 = bf16[128,1024]{1,0:T(8,128)(2,1)S(1)} collective-permute-done((bf16[128,1024]{1,0:T(8,128)(2,1)S(1)}, bf16[128,1024]{1,0:T(8,128)(2,1)S(1)}, u32[]{:S(2)}, u32[]{:S(2)}) %collective-permute-start.13) | collective-permute-done | bytes 262176 | tf_op jit(solution)/shard_map/ppermute | solution.py:23
  93.8 2.3 %collective-permute-start.12 = (bf16[2,128,1024]{2,1,0:T(8,128)(2,1)}, bf16[2,128,1024]{2,1,0:T(8,128)(2,1)}, u32[]{:S(2)}, u32[]{:S(2)}) collective-permute-start(bf16[2,128,1024]{2,1,0:T(8,128)(2,1)} %get-tuple-element.48), channel_id=1, source_target_pairs={{0,192},{64,0},{128,64},{192,128},{1,193},{65,1},{129,65},{193,129... | collective-permute-start | bytes 1572872 | tf_op jit(solution)/shard_map/ppermute | solution.py:23
  96.0 2.1 %reduce_sum.21 = bf16[8,8,1024]{2,1,0:T(8,128)(2,1)} reduce(bf16[8,8,8,1024]{3,2,1,0:T(8,128)(2,1)} %all-to-all-done.1, bf16[]{:T(256)} %constant.107.clone.1), dimensions={0}, to_apply=%region_0.1 | reduce | flops 458752 | bytes 1179650 | tf_op jit(solution)/shard_map/reduce_sum | solution.py:115
  98.1 5.0 %all-to-all-start.2 = ((bf16[8,8,1024]{2,1,0:T(8,128)(2,1)}), bf16[8,8,1024]{2,1,0:T(8,128)(2,1)S(1)}, u32[]{:S(2)}, u32[]{:S(2)}) async-start(bf16[8,8,1024]{2,1,0:T(8,128)(2,1)} %reduce_sum.21), calls=%async_computation.2 | async-start | bytes 262144 | tf_op jit(solution)/shard_map/all_to_all | solution.py:18
  104.1 4.3 %all-to-all-done.2 = bf16[8,8,1024]{2,1,0:T(8,128)(2,1)S(1)} async-done(((bf16[8,8,1024]{2,1,0:T(8,128)(2,1)}), bf16[8,8,1024]{2,1,0:T(8,128)(2,1)S(1)}, u32[]{:S(2)}, u32[]{:S(2)}) %all-to-all-start.2) | async-done | bytes 131104 | tf_op jit(solution)/shard_map/all_to_all | solution.py:18
  108.4 3.6 %all-to-all-start.3 = ((bf16[16,64,256]{2,1,0:T(8,128)(2,1)}), bf16[16,64,256]{2,1,0:T(8,128)(2,1)S(1)}, u32[]{:S(2)}, u32[]{:S(2)}) async-start(bf16[16,64,256]{2,1,0:T(8,128)(2,1)} %bitcast.27), calls=%async_computation.3 | async-start | bytes 1048576 | tf_op jit(solution)/shard_map/all_to_all | solution.py:18
  112.0 1.3 %slice.89 = f32[256,1024]{1,0:T(8,128)S(1)} slice(f32[1024,1024]{1,0:T(8,128)} %copy-done.4), slice={[0:256], [0:1024]} | slice | bytes 2097152 | tf_op jit(solution)/shard_map/slice | solution.py:140
  113.3 2.4 %convert_add_fusion = f32[2,128,1024]{2,1,0:T(8,128)} fusion(bf16[2,128,1024]{2,1,0:T(8,128)(2,1)} %collective-permute-done.14, f32[2,128,1024]{2,1,0:T(8,128)S(1)} %bitcast.57, bf16[2,128,1024]{2,1,0:T(8,128)(2,1)} %collective-permute-done.12), kind=kLoop, calls=%fused_computation.1 | loop fusion | flops 1048576 | bytes 3145728 | tf_op jit(solution)/shard_map/add | solution.py:140
  115.7 6.6 %all-to-all-done.3 = bf16[16,64,256]{2,1,0:T(8,128)(2,1)S(1)} async-done(((bf16[16,64,256]{2,1,0:T(8,128)(2,1)}), bf16[16,64,256]{2,1,0:T(8,128)(2,1)S(1)}, u32[]{:S(2)}, u32[]{:S(2)}) %all-to-all-start.3) | async-done | bytes 524320 | tf_op jit(solution)/shard_map/all_to_all | solution.py:18
  (62 shorter events, 20.6 us)
Async XLA Ops:
  7.2 34.0 %copy-start = (bf16[256,1024]{1,0:T(8,128)(2,1)S(1)}, bf16[256,1024]{1,0:T(8,128)(2,1)}, u32[]{:S(2)}) copy-start(bf16[256,1024]{1,0:T(8,128)(2,1)} %w0.3) | copy-start | bytes 1572868
  7.2 20.2 %collective-permute-start.4 = (bf16[256,1024]{1,0:T(8,128)(2,1)}, bf16[256,1024]{1,0:T(8,128)(2,1)S(1)}, u32[]{:S(2)}, u32[]{:S(2)}) collective-permute-start(bf16[256,1024]{1,0:T(8,128)(2,1)} %w0.3), channel_id=1, source_target_pairs={{0,192},{64,0},{128,64},{192,128},{1,193},{65,1},{129,65},{193,129... | collective-permute-start | bytes 1572872 | tf_op jit(solution)/shard_map/ppermute | solution.py:23
  10.8 16.5 %collective-permute-start.3 = (bf16[256,1024]{1,0:T(8,128)(2,1)}, bf16[256,1024]{1,0:T(8,128)(2,1)S(1)}, u32[]{:S(2)}, u32[]{:S(2)}) collective-permute-start(bf16[256,1024]{1,0:T(8,128)(2,1)} %w0.3), channel_id=1, source_target_pairs={{0,64},{64,128},{128,192},{192,0},{1,65},{65,129},{129,193},{193,1... | collective-permute-start | bytes 1572872 | tf_op jit(solution)/shard_map/ppermute | solution.py:23
  12.5 10.4 %collective-permute-start.2 = (bf16[64,256]{1,0:T(8,128)(2,1)S(1)}, bf16[64,256]{1,0:T(8,128)(2,1)S(1)}, u32[]{:S(2)}, u32[]{:S(2)}) collective-permute-start(bf16[64,256]{1,0:T(8,128)(2,1)S(1)} %get-tuple-element.54), channel_id=1, source_target_pairs={{0,192},{64,0},{128,64},{192,128},{1,193},{65,1},{129,65},{193,129... | collective-permute-start | bytes 98312 | tf_op jit(solution)/shard_map/ppermute | solution.py:23
  15.3 8.8 %collective-permute-start.1 = (bf16[64,256]{1,0:T(8,128)(2,1)S(1)}, bf16[64,256]{1,0:T(8,128)(2,1)S(1)}, u32[]{:S(2)}, u32[]{:S(2)}) collective-permute-start(bf16[64,256]{1,0:T(8,128)(2,1)S(1)} %get-tuple-element.55), channel_id=1, source_target_pairs={{0,128},{64,192},{128,0},{192,64},{1,129},{65,193},{129,1},{193,65... | collective-permute-start | bytes 98312 | tf_op jit(solution)/shard_map/ppermute | solution.py:23
  15.3 10.5 %collective-permute-start = (bf16[64,256]{1,0:T(8,128)(2,1)S(1)}, bf16[64,256]{1,0:T(8,128)(2,1)S(1)}, u32[]{:S(2)}, u32[]{:S(2)}) collective-permute-start(bf16[64,256]{1,0:T(8,128)(2,1)S(1)} %get-tuple-element.56), channel_id=1, source_target_pairs={{0,64},{64,128},{128,192},{192,0},{1,65},{65,129},{129,193},{193,1... | collective-permute-start | bytes 98312 | tf_op jit(solution)/shard_map/ppermute | solution.py:23
  16.0 11.4 %all-to-all-start = ((bf16[8,8,1024]{2,1,0:T(8,128)(2,1)}), bf16[8,8,1024]{2,1,0:T(8,128)(2,1)S(1)}, u32[]{:S(2)}, u32[]{:S(2)}) async-start(bf16[8,8,1024]{2,1,0:T(8,128)(2,1)} %bitcast.68), calls=%async_computation | async-start | bytes 262144 | tf_op jit(solution)/shard_map/all_to_all | solution.py:18
  22.0 47.6 %all-gather.2.cloned.1.call-start = ((), (), s32[]{:S(2)}) async-start(), calls=%async_computation.4 | async-start | bytes 1179648 | tf_op jit(solution)/shard_map/all_gather | solution.py:104
  28.1 4.6 %collective-permute-start.7 = (bf16[64,1024]{1,0:T(8,128)(2,1)S(1)}, bf16[64,1024]{1,0:T(8,128)(2,1)S(1)}, u32[]{:S(2)}, u32[]{:S(2)}) collective-permute-start(bf16[64,1024]{1,0:T(8,128)(2,1)S(1)} %pad_maximum_fusion.1), channel_id=1, source_target_pairs={{0,6},{2,0},{4,2},{6,4},{1,7},{3,1},{5,3},{7,5},{8,14},{10,8},{12,... | collective-permute-start | bytes 393224 | tf_op jit(solution)/shard_map/ppermute | solution.py:23
  29.3 5.4 %collective-permute-start.6 = (bf16[64,1024]{1,0:T(8,128)(2,1)S(1)}, bf16[64,1024]{1,0:T(8,128)(2,1)S(1)}, u32[]{:S(2)}, u32[]{:S(2)}) collective-permute-start(bf16[64,1024]{1,0:T(8,128)(2,1)S(1)} %pad_maximum_fusion.1), channel_id=1, source_target_pairs={{0,4},{2,6},{4,0},{6,2},{1,5},{3,7},{5,1},{7,3},{8,12},{10,14},{12... | collective-permute-start | bytes 393224 | tf_op jit(solution)/shard_map/ppermute | solution.py:23
  30.5 5.9 %collective-permute-start.5 = (bf16[64,1024]{1,0:T(8,128)(2,1)S(1)}, bf16[64,1024]{1,0:T(8,128)(2,1)S(1)}, u32[]{:S(2)}, u32[]{:S(2)}) collective-permute-start(bf16[64,1024]{1,0:T(8,128)(2,1)S(1)} %pad_maximum_fusion.1), channel_id=1, source_target_pairs={{0,2},{2,4},{4,6},{6,0},{1,3},{3,5},{5,7},{7,1},{8,10},{10,12},{12... | collective-permute-start | bytes 393224 | tf_op jit(solution)/shard_map/ppermute | solution.py:23
  30.5 9.2 %collective-permute-start.10 = (bf16[128,1024]{1,0:T(8,128)(2,1)S(1)}, bf16[128,1024]{1,0:T(8,128)(2,1)S(1)}, u32[]{:S(2)}, u32[]{:S(2)}) collective-permute-start(bf16[128,1024]{1,0:T(8,128)(2,1)S(1)} %slice.75), channel_id=1, source_target_pairs={{0,192},{64,0},{128,64},{192,128},{1,193},{65,1},{129,65},{193,129... | collective-permute-start | bytes 786440 | tf_op jit(solution)/shard_map/ppermute | solution.py:23
  32.3 7.4 %collective-permute-start.9 = (bf16[128,1024]{1,0:T(8,128)(2,1)S(1)}, bf16[128,1024]{1,0:T(8,128)(2,1)S(1)}, u32[]{:S(2)}, u32[]{:S(2)}) collective-permute-start(bf16[128,1024]{1,0:T(8,128)(2,1)S(1)} %slice.74), channel_id=1, source_target_pairs={{0,64},{64,128},{128,192},{192,0},{1,65},{65,129},{129,193},{193,1... | collective-permute-start | bytes 786440 | tf_op jit(solution)/shard_map/ppermute | solution.py:23
  36.4 4.8 %collective-permute-start.8 = (bf16[4,64,1024]{2,1,0:T(8,128)(2,1)S(1)}, bf16[4,64,1024]{2,1,0:T(8,128)(2,1)S(1)}, u32[]{:S(2)}, u32[]{:S(2)}) collective-permute-start(bf16[4,64,1024]{2,1,0:T(8,128)(2,1)S(1)} %pad_maximum_fusion.own), channel_id=1, source_target_pairs={{0,1},{1,0},{2,3},{3,2},{4,5},{5,4},{6,7},{7,6},{8,9},{9,8},{10,11... | collective-permute-start | bytes 1572872 | tf_op jit(solution)/shard_map/ppermute | solution.py:23
  44.9 51.1 %all-to-all-start.1 = ((bf16[8,8,8,1024]{3,2,1,0:T(8,128)(2,1)}), bf16[8,8,8,1024]{3,2,1,0:T(8,128)(2,1)}, u32[]{:S(2)}, u32[]{:S(2)}) async-start(bf16[8,8,8,1024]{3,2,1,0:T(8,128)(2,1)} %shard_map.77), calls=%async_computation.1 | async-start | bytes 2097152 | tf_op jit(solution)/shard_map/all_to_all | solution.py:18
  71.8 9.2 %copy-start.6 = (bf16[8,64,1024]{2,1,0:T(8,128)(2,1)S(1)}, bf16[8,64,1024]{2,1,0:T(8,128)(2,1)}, u32[]{:S(2)}) copy-start(bf16[8,64,1024]{2,1,0:T(8,128)(2,1)} %constant_dynamic-update-slice_fusion) | copy-start | bytes 3145732
  74.0 29.1 %collective-permute-start.15 = (bf16[4,4,64,256]{3,2,1,0:T(8,128)(2,1)S(1)}, bf16[4,4,64,256]{3,2,1,0:T(8,128)(2,1)S(1)}, u32[]{:S(2)}, u32[]{:S(2)}) collective-permute-start(bf16[4,4,64,256]{3,2,1,0:T(8,128)(2,1)S(1)} %get-tuple-element.44), channel_id=1, source_target_pairs={{0,1},{1,0},{2,3},{3,2},{4,5},{5,4},{6,7},{7,6},{8,9},{9,8},{10,11... | collective-permute-start | bytes 1572872 | tf_op jit(solution)/shard_map/ppermute | solution.py:23
  82.3 10.1 %copy-start.4 = (f32[1024,1024]{1,0:T(8,128)}, f32[1024,1024]{1,0:T(8,128)S(1)}, u32[]{:S(2)}) copy-start(f32[1024,1024]{1,0:T(8,128)S(1)} %get-tuple-element.58) | copy-start | bytes 12582916
  82.3 9.2 %collective-permute-start.13 = (bf16[128,1024]{1,0:T(8,128)(2,1)S(1)}, bf16[128,1024]{1,0:T(8,128)(2,1)S(1)}, u32[]{:S(2)}, u32[]{:S(2)}) collective-permute-start(bf16[128,1024]{1,0:T(8,128)(2,1)S(1)} %get-tuple-element.51), channel_id=1, source_target_pairs={{0,64},{64,128},{128,192},{192,0},{1,65},{65,129},{129,193},{193,1... | collective-permute-start | bytes 786440 | tf_op jit(solution)/shard_map/ppermute | solution.py:23
  84.8 7.6 %collective-permute-start.11 = (bf16[128,1024]{1,0:T(8,128)(2,1)S(1)}, bf16[128,1024]{1,0:T(8,128)(2,1)S(1)}, u32[]{:S(2)}, u32[]{:S(2)}) collective-permute-start(bf16[128,1024]{1,0:T(8,128)(2,1)S(1)} %get-tuple-element.52), channel_id=1, source_target_pairs={{0,192},{64,0},{128,64},{192,128},{1,193},{65,1},{129,65},{193,129... | collective-permute-start | bytes 786440 | tf_op jit(solution)/shard_map/ppermute | solution.py:23
  93.4 19.9 %collective-permute-start.14 = (bf16[2,128,1024]{2,1,0:T(8,128)(2,1)}, bf16[2,128,1024]{2,1,0:T(8,128)(2,1)}, u32[]{:S(2)}, u32[]{:S(2)}) collective-permute-start(bf16[2,128,1024]{2,1,0:T(8,128)(2,1)} %get-tuple-element.47), channel_id=1, source_target_pairs={{0,64},{64,128},{128,192},{192,0},{1,65},{65,129},{129,193},{193,1... | collective-permute-start | bytes 1572872 | tf_op jit(solution)/shard_map/ppermute | solution.py:23
  93.8 19.5 %collective-permute-start.12 = (bf16[2,128,1024]{2,1,0:T(8,128)(2,1)}, bf16[2,128,1024]{2,1,0:T(8,128)(2,1)}, u32[]{:S(2)}, u32[]{:S(2)}) collective-permute-start(bf16[2,128,1024]{2,1,0:T(8,128)(2,1)} %get-tuple-element.48), channel_id=1, source_target_pairs={{0,192},{64,0},{128,64},{192,128},{1,193},{65,1},{129,65},{193,129... | collective-permute-start | bytes 1572872 | tf_op jit(solution)/shard_map/ppermute | solution.py:23
  98.1 10.3 %all-to-all-start.2 = ((bf16[8,8,1024]{2,1,0:T(8,128)(2,1)}), bf16[8,8,1024]{2,1,0:T(8,128)(2,1)S(1)}, u32[]{:S(2)}, u32[]{:S(2)}) async-start(bf16[8,8,1024]{2,1,0:T(8,128)(2,1)} %reduce_sum.21), calls=%async_computation.2 | async-start | bytes 262144 | tf_op jit(solution)/shard_map/all_to_all | solution.py:18
  108.4 13.9 %all-to-all-start.3 = ((bf16[16,64,256]{2,1,0:T(8,128)(2,1)}), bf16[16,64,256]{2,1,0:T(8,128)(2,1)S(1)}, u32[]{:S(2)}, u32[]{:S(2)}) async-start(bf16[16,64,256]{2,1,0:T(8,128)(2,1)} %bitcast.27), calls=%async_computation.3 | async-start | bytes 1048576 | tf_op jit(solution)/shard_map/all_to_all | solution.py:18
  (5 other events, 4.5 us)
Sparse Core Ops, SparseCore 0:
  28.1 41.4 all-gather.1

commit v9 on v6

--- a/solution.py
+++ b/solution.py
@@ -9,7 +9,7 @@
 F32 = jnp.float32
 XC = ("x", "c")
 FWD = 2**30
-BWD = 2**36
+BWD = 2**34
 VMEM = pl.BlockSpec(memory_space=pltpu.VMEM)
 SMEM = pl.BlockSpec(memory_space=pltpu.SMEM)
 

time: 117 us -> 123 us (1.051)
  local copies, waits for them, and re-layouts: 8.05 us -> 14.9 us
  waiting for transfers between devices: 31 us -> 24.5 us
  starting transfers between devices: 48.3 us -> 51.2 us
  matrix products: 1.29 us -> 2.52 us
    all_to_all x4, waiting for transfers between devices: 20 us -> 9.97 us  [exchange(): return lax.all_to_all(v, axes, split_axis=0, concat_axis=0, tiled=False)]
    unnamed x17, local copies, waits for them, and re-layouts: 3.32 us -> 8.78 us
    ppermute x16, waiting for transfers between devices: 7.59 us -> 11.6 us  [shift(): return lax.ppermute(v, axis, [(i, (i + s) % n) for i in range(n)])]
    all_to_all x4, starting transfers between devices: 26.7 us -> 28.4 us  [exchange(): return lax.all_to_all(v, axes, split_axis=0, concat_axis=0, tiled=False)]
    slice x2, local copies, waits for them, and re-layouts: 0.04 us -> 1.42 us  [shards(): w2a, w2b = (shift(w1[:half], 'y', 1), shift(w3[half:], 'y', -1))]
  transfers between devices with their start and end apart: 21 -> 21, of which waited for: 11 -> 10; matrix products, arithmetic and copies ran while one was open for 10% -> 17% of each run, Pallas kernels for 5% -> 5%
where the time goes in v9:
time: 123 us; the launch traced here: 122 us
  starting transfers between devices  51.2 us (42%)
  waiting for transfers between devices  24.5 us (20%)
  local copies, waits for them, and re-layouts  14.9 us (12%)
  between operations  14.2 us (12%)
  other arithmetic  8.37 us (7%)
  Pallas kernels  6.44 us (5%)
  matrix products  2.52 us (2%)
    all_to_all x4, starting transfers between devices, exchange(): return lax.all_to_all(v, axes, split_axis=0, concat_axis=0, tiled=False)  28.4 us
    ppermute x16, starting transfers between devices, shift(): return lax.ppermute(v, axis, [(i, (i + s) % n) for i in range(n)])  22.7 us
    ppermute x16, waiting for transfers between devices, shift(): return lax.ppermute(v, axis, [(i, (i + s) % n) for i in range(n)])  11.6 us
    all_to_all x4, waiting for transfers between devices, exchange(): return lax.all_to_all(v, axes, split_axis=0, concat_axis=0, tiled=False)  9.97 us
    unnamed x17, local copies, waits for them, and re-layouts  8.78 us
    pallas_call x2, Pallas kernels, call(): pl.pallas_call(kernel, out_shape=out_shape, in_specs=[SMEM] + [VMEM] * (l...  6.44 us
    reduce_scatter x1, waiting for transfers between devices, shards(): lax.psum_scatter(part, 'z', scatter_dimension=0, tiled=False).astype(BF)  2.86 us
    slice x1, local copies, waits for them, and re-layouts, shards(): far = gw[3].at[1].add(shift(gw[2, 1].astype(BF), 'y', 1).astype(F32))  2.54 us
  transfers between devices with their start and end apart: 21, of which 10 were waited for; matrix products, arithmetic and copies ran while one was open for 17% of the time, Pallas kernels for 5%

profile of v9, /device:TPU:1, one launch (start us, length us, event | category | flops | bytes accessed | tf_op | source)
XLA Modules:
  0.0 122.0 jit_solution(17329176653718816689)
XLA Ops:
  7.2 3.6 %collective-permute-start.4 = (bf16[256,1024]{1,0:T(8,128)(2,1)}, bf16[256,1024]{1,0:T(8,128)(2,1)S(1)}, u32[]{:S(2)}, u32[]{:S(2)}) collective-permute-start(bf16[256,1024]{1,0:T(8,128)(2,1)} %w0.3), channel_id=1, source_target_pairs={{0,192},{64,0},{128,64},{192,128},{1,193},{65,1},{129,65},{193,129... | collective-permute-start | bytes 1572872 | tf_op jit(solution)/shard_map/ppermute | solution.py:23
  12.5 2.8 %collective-permute-start.2 = (bf16[64,256]{1,0:T(8,128)(2,1)S(1)}, bf16[64,256]{1,0:T(8,128)(2,1)S(1)}, u32[]{:S(2)}, u32[]{:S(2)}) collective-permute-start(bf16[64,256]{1,0:T(8,128)(2,1)S(1)} %get-tuple-element.54), channel_id=1, source_target_pairs={{0,192},{64,0},{128,64},{192,128},{1,193},{65,1},{129,65},{193,129... | collective-permute-start | bytes 98312 | tf_op jit(solution)/shard_map/ppermute | solution.py:23
  15.9 6.1 %all-to-all-start = ((bf16[8,8,1024]{2,1,0:T(8,128)(2,1)}), bf16[8,8,1024]{2,1,0:T(8,128)(2,1)S(1)}, u32[]{:S(2)}, u32[]{:S(2)}) async-start(bf16[8,8,1024]{2,1,0:T(8,128)(2,1)} %bitcast.66), calls=%async_computation | async-start | bytes 262144 | tf_op jit(solution)/shard_map/all_to_all | solution.py:18
  24.1 1.7 %collective-permute-done = bf16[64,256]{1,0:T(8,128)(2,1)S(1)} collective-permute-done((bf16[64,256]{1,0:T(8,128)(2,1)S(1)}, bf16[64,256]{1,0:T(8,128)(2,1)S(1)}, u32[]{:S(2)}, u32[]{:S(2)}) %collective-permute-start) | collective-permute-done | bytes 32800 | tf_op jit(solution)/shard_map/ppermute | solution.py:23
  25.8 1.5 %all-to-all-done = bf16[8,8,1024]{2,1,0:T(8,128)(2,1)S(1)} async-done(((bf16[8,8,1024]{2,1,0:T(8,128)(2,1)}), bf16[8,8,1024]{2,1,0:T(8,128)(2,1)S(1)}, u32[]{:S(2)}, u32[]{:S(2)}) %all-to-all-start) | async-done | bytes 131104 | tf_op jit(solution)/shard_map/all_to_all | solution.py:18
  30.8 8.2 %all-to-all-start.1 = ((bf16[8,8,8,1024]{3,2,1,0:T(8,128)(2,1)}), bf16[8,8,8,1024]{3,2,1,0:T(8,128)(2,1)S(1)}, u32[]{:S(2)}, u32[]{:S(2)}) async-start(bf16[8,8,8,1024]{3,2,1,0:T(8,128)(2,1)} %broadcast_in_dim.10), calls=%async_computation.1 | async-start | bytes 2097152 | tf_op jit(solution)/shard_map/all_to_all | solution.py:18
  39.8 3.2 %collective-permute-start.8 = (bf16[4,64,1024]{2,1,0:T(8,128)(2,1)S(1)}, bf16[4,64,1024]{2,1,0:T(8,128)(2,1)S(1)}, u32[]{:S(2)}, u32[]{:S(2)}) collective-permute-start(bf16[4,64,1024]{2,1,0:T(8,128)(2,1)S(1)} %pad_maximum_fusion.own), channel_id=1, source_target_pairs={{0,1},{1,0},{2,3},{3,2},{4,5},{5,4},{6,7},{7,6},{8,9},{9,8},{10,11... | collective-permute-start | bytes 1572872 | tf_op jit(solution)/shard_map/ppermute | solution.py:23
  46.0 6.7 %collective-permute-done.10.w2b = bf16[128,1024]{1,0:T(8,128)(2,1)S(1)} collective-permute-done((bf16[128,1024]{1,0:T(8,128)(2,1)}, bf16[128,1024]{1,0:T(8,128)(2,1)S(1)}, u32[]{:S(2)}, u32[]{:S(2)}) %collective-permute-start.10) | collective-permute-done | bytes 262176 | tf_op jit(solution)/shard_map/ppermute | solution.py:23
  55.0 3.9 %shard_map.77 = f32[8,8,8,1024]{3,2,1,0:T(8,128)} custom-call(s32[3]{0:T(128)S(1)} %pad_add_fusion.where, bf16[4,64,1024]{2,1,0:T(8,128)(2,1)S(1)} %pad_maximum_fusion.own, bf16[4,64,1024]{2,1,0:T(8,128)(2,1)S(1)} %collective-permute-done.8.other, bf16[256,1024]{1,0:T(8,128)(2,1)S(1)} %copy-done, bf16[256,1024]{1,0:T(8,128)(2,1)S(1)} %collective-permute-done.3.w1, ...), custom_call_target="tpu_custom_call" | custom-call | flops 1073741824 | bytes 2684354 | tf_op jit(solution)/shard_map/pallas_call | solution.py:72
  59.5 1.6 %constant_dynamic-update-slice_fusion.3 = bf16[8,64,1024]{2,1,0:T(8,128)(2,1)} fusion(bf16[8,64,1024]{2,1,0:T(8,128)(2,1)} %constant_dynamic-update-slice_fusion.4, bf16[64,1024]{1,0:T(8,128)(2,1)} %copy-done.5), kind=kLoop, calls=%fused_computation.23 | loop fusion | bytes 262144
  61.1 1.6 %constant_dynamic-update-slice_fusion.2 = bf16[8,64,1024]{2,1,0:T(8,128)(2,1)} fusion(bf16[8,64,1024]{2,1,0:T(8,128)(2,1)} %constant_dynamic-update-slice_fusion.3, bf16[64,1024]{1,0:T(8,128)(2,1)} %copy-done.4), kind=kLoop, calls=%fused_computation.22 | loop fusion | bytes 262144
  62.6 1.6 %constant_dynamic-update-slice_fusion.1 = bf16[8,64,1024]{2,1,0:T(8,128)(2,1)} fusion(bf16[8,64,1024]{2,1,0:T(8,128)(2,1)} %constant_dynamic-update-slice_fusion.2, bf16[64,1024]{1,0:T(8,128)(2,1)} %copy-done.3), kind=kLoop, calls=%fused_computation.21 | loop fusion | bytes 262144
  66.8 2.6 %shard_map.76 = (f32[4,4,64,256]{3,2,1,0:T(8,128)S(1)}, bf16[4,4,64,256]{3,2,1,0:T(8,128)(2,1)S(1)}, bf16[512,1024]{1,0:T(8,128)(2,1)S(1)}) custom-call(s32[3]{0:T(128)S(1)} %pad_add_fusion.where, bf16[8,8,8,1024]{3,2,1,0:T(8,128)(2,1)S(1)} %all-to-all-done.1.g, bf16[256,1024]{1,0:T(8,128)(2,1)S(1)} %copy-done.1, ...), custom_call_target="tpu_custom_call" | custom-call | flops 17179869184 | bytes 42949672 | tf_op jit(solution)/shard_map/pallas_call | solution.py:72
  69.4 3.2 %collective-permute-start.15 = (bf16[4,4,64,256]{3,2,1,0:T(8,128)(2,1)S(1)}, bf16[4,4,64,256]{3,2,1,0:T(8,128)(2,1)S(1)}, u32[]{:S(2)}, u32[]{:S(2)}) collective-permute-start(bf16[4,4,64,256]{3,2,1,0:T(8,128)(2,1)S(1)} %get-tuple-element.44), channel_id=1, source_target_pairs={{0,1},{1,0},{2,3},{3,2},{4,5},{5,4},{6,7},{7,6},{8,9},{9,8},{10,11... | collective-permute-start | bytes 1572872 | tf_op jit(solution)/shard_map/ppermute | solution.py:23
  72.6 2.5 %fusion.5 = (bf16[1024,1024]{1,0:T(8,128)(2,1)S(1)}, f32[1024,1024]{1,0:T(8,128)S(1)}) fusion(bf16[512,1024]{1,0:T(8,128)(2,1)} %bitcast.12, bf16[512,1024]{1,0:T(8,128)(2,1)S(1)} %get-tuple-element.41), kind=kOutput, calls=%fused_computation.29 | convolution fusion | flops 1074790400 | bytes 8388608 | tf_op jit(solution)/shard_map/dot_general | solution.py:132
  75.2 2.0 %collective-permute-start.13 = (bf16[128,1024]{1,0:T(8,128)(2,1)S(1)}, bf16[128,1024]{1,0:T(8,128)(2,1)S(1)}, u32[]{:S(2)}, u32[]{:S(2)}) collective-permute-start(bf16[128,1024]{1,0:T(8,128)(2,1)S(1)} %get-tuple-element.51), channel_id=1, source_target_pairs={{0,64},{64,128},{128,192},{192,0},{1,65},{65,129},{129,193},{193,1... | collective-permute-start | bytes 786440 | tf_op jit(solution)/shard_map/ppermute | solution.py:23
  79.0 5.2 %all-to-all-start.3 = ((bf16[16,64,256]{2,1,0:T(8,128)(2,1)}), bf16[16,64,256]{2,1,0:T(8,128)(2,1)S(1)}, u32[]{:S(2)}, u32[]{:S(2)}) async-start(bf16[16,64,256]{2,1,0:T(8,128)(2,1)} %bitcast.26), calls=%async_computation.4 | async-start | bytes 1048576 | tf_op jit(solution)/shard_map/all_to_all | solution.py:18
  84.2 2.5 %fusion.4 = (bf16[256,1024]{1,0:T(8,128)(2,1)S(1)}, bf16[256,1024]{1,0:T(8,128)(2,1)}) fusion(f32[1024,1024]{1,0:T(8,128)} %copy-done.2), kind=kLoop, calls=%fused_computation.28 | loop fusion | bytes 2097152 | tf_op jit(solution)/shard_map/slice | solution.py:135
  86.7 2.1 %fusion.1 = (bf16[2,128,1024]{2,1,0:T(8,128)(2,1)S(1)}, bf16[2,128,1024]{2,1,0:T(8,128)(2,1)}) fusion(bf16[2,128,1024]{2,1,0:T(8,128)(2,1)S(1)} %bitcast.62, f32[1024,1024]{1,0:T(8,128)} %copy-done.2, bf16[128,1024]{1,0:T(8,128)(2,1)S(1)} %collective-permute-done.13, bf16[2,128,1024]{2,1,0:T(8,128)(2,1)} %bitcast.16, ...), kind=kLoop, calls=%fused_computation.5 | loop fusion | flops 524288 | bytes 2621440 | tf_op jit(solution)/shard_map/scatter-add | solution.py:135
  91.5 3.1 %all-to-all-done.3 = bf16[16,64,256]{2,1,0:T(8,128)(2,1)S(1)} async-done(((bf16[16,64,256]{2,1,0:T(8,128)(2,1)}), bf16[16,64,256]{2,1,0:T(8,128)(2,1)S(1)}, u32[]{:S(2)}, u32[]{:S(2)}) %all-to-all-start.3) | async-done | bytes 524320 | tf_op jit(solution)/shard_map/all_to_all | solution.py:18
  94.6 2.9 %reduce-scatter.2.cloned.1.call-done = f32[1,8,8,1024]{3,2,1,0:T(8,128)} async-done(((f32[8,8,8,1024]{3,2,1,0:T(8,128)}), f32[1,8,8,1024]{3,2,1,0:T(8,128)}) %reduce-scatter.2.cloned.1.call-update) | async-done | bytes 262160 | tf_op jit(solution)/shard_map/reduce_scatter | solution.py:114
  97.5 1.6 %convert_bitcast_fusion = bf16[8,8,1024]{2,1,0:T(8,128)(2,1)} fusion(f32[1,8,8,1024]{3,2,1,0:T(8,128)} %reduce-scatter.2.cloned.1.call-done), kind=kLoop, calls=%fused_computation.15 | loop fusion | flops 65536 | bytes 393216 | tf_op jit(solution)/shard_map/convert_element_type | solution.py:114
  99.1 8.9 %all-to-all-start.2 = ((bf16[8,8,1024]{2,1,0:T(8,128)(2,1)}), bf16[8,8,1024]{2,1,0:T(8,128)(2,1)S(1)}, u32[]{:S(2)}, u32[]{:S(2)}) async-start(bf16[8,8,1024]{2,1,0:T(8,128)(2,1)} %convert_bitcast_fusion), calls=%async_computation.3 | async-start | bytes 262144 | tf_op jit(solution)/shard_map/all_to_all | solution.py:18
  108.7 4.6 %all-to-all-done.2 = bf16[8,8,1024]{2,1,0:T(8,128)(2,1)S(1)} async-done(((bf16[8,8,1024]{2,1,0:T(8,128)(2,1)}), bf16[8,8,1024]{2,1,0:T(8,128)(2,1)S(1)}, u32[]{:S(2)}, u32[]{:S(2)}) %all-to-all-start.2) | async-done | bytes 131104 | tf_op jit(solution)/shard_map/all_to_all | solution.py:18
  (59 shorter events, 24.3 us)
Async XLA Ops:
  7.2 20.2 %collective-permute-start.4 = (bf16[256,1024]{1,0:T(8,128)(2,1)}, bf16[256,1024]{1,0:T(8,128)(2,1)S(1)}, u32[]{:S(2)}, u32[]{:S(2)}) collective-permute-start(bf16[256,1024]{1,0:T(8,128)(2,1)} %w0.3), channel_id=1, source_target_pairs={{0,192},{64,0},{128,64},{192,128},{1,193},{65,1},{129,65},{193,129... | collective-permute-start | bytes 1572872 | tf_op jit(solution)/shard_map/ppermute | solution.py:23
  10.8 16.5 %collective-permute-start.3 = (bf16[256,1024]{1,0:T(8,128)(2,1)}, bf16[256,1024]{1,0:T(8,128)(2,1)S(1)}, u32[]{:S(2)}, u32[]{:S(2)}) collective-permute-start(bf16[256,1024]{1,0:T(8,128)(2,1)} %w0.3), channel_id=1, source_target_pairs={{0,64},{64,128},{128,192},{192,0},{1,65},{65,129},{129,193},{193,1... | collective-permute-start | bytes 1572872 | tf_op jit(solution)/shard_map/ppermute | solution.py:23
  12.5 10.4 %collective-permute-start.2 = (bf16[64,256]{1,0:T(8,128)(2,1)S(1)}, bf16[64,256]{1,0:T(8,128)(2,1)S(1)}, u32[]{:S(2)}, u32[]{:S(2)}) collective-permute-start(bf16[64,256]{1,0:T(8,128)(2,1)S(1)} %get-tuple-element.54), channel_id=1, source_target_pairs={{0,192},{64,0},{128,64},{192,128},{1,193},{65,1},{129,65},{193,129... | collective-permute-start | bytes 98312 | tf_op jit(solution)/shard_map/ppermute | solution.py:23
  15.3 8.8 %collective-permute-start.1 = (bf16[64,256]{1,0:T(8,128)(2,1)S(1)}, bf16[64,256]{1,0:T(8,128)(2,1)S(1)}, u32[]{:S(2)}, u32[]{:S(2)}) collective-permute-start(bf16[64,256]{1,0:T(8,128)(2,1)S(1)} %get-tuple-element.55), channel_id=1, source_target_pairs={{0,128},{64,192},{128,0},{192,64},{1,129},{65,193},{129,1},{193,65... | collective-permute-start | bytes 98312 | tf_op jit(solution)/shard_map/ppermute | solution.py:23
  15.3 10.5 %collective-permute-start = (bf16[64,256]{1,0:T(8,128)(2,1)S(1)}, bf16[64,256]{1,0:T(8,128)(2,1)S(1)}, u32[]{:S(2)}, u32[]{:S(2)}) collective-permute-start(bf16[64,256]{1,0:T(8,128)(2,1)S(1)} %get-tuple-element.56), channel_id=1, source_target_pairs={{0,64},{64,128},{128,192},{192,0},{1,65},{65,129},{129,193},{193,1... | collective-permute-start | bytes 98312 | tf_op jit(solution)/shard_map/ppermute | solution.py:23
  15.9 11.4 %all-to-all-start = ((bf16[8,8,1024]{2,1,0:T(8,128)(2,1)}), bf16[8,8,1024]{2,1,0:T(8,128)(2,1)S(1)}, u32[]{:S(2)}, u32[]{:S(2)}) async-start(bf16[8,8,1024]{2,1,0:T(8,128)(2,1)} %bitcast.66), calls=%async_computation | async-start | bytes 262144 | tf_op jit(solution)/shard_map/all_to_all | solution.py:18
  27.3 11.7 %collective-permute-start.7 = (bf16[64,1024]{1,0:T(8,128)(2,1)S(1)}, bf16[64,1024]{1,0:T(8,128)(2,1)S(1)}, u32[]{:S(2)}, u32[]{:S(2)}) collective-permute-start(bf16[64,1024]{1,0:T(8,128)(2,1)S(1)} %pad_maximum_fusion.1), channel_id=1, source_target_pairs={{0,6},{2,0},{4,2},{6,4},{1,7},{3,1},{5,3},{7,5},{8,14},{10,8},{12,... | collective-permute-start | bytes 393224 | tf_op jit(solution)/shard_map/ppermute | solution.py:23
  28.5 10.5 %collective-permute-start.6 = (bf16[64,1024]{1,0:T(8,128)(2,1)S(1)}, bf16[64,1024]{1,0:T(8,128)(2,1)S(1)}, u32[]{:S(2)}, u32[]{:S(2)}) collective-permute-start(bf16[64,1024]{1,0:T(8,128)(2,1)S(1)} %pad_maximum_fusion.1), channel_id=1, source_target_pairs={{0,4},{2,6},{4,0},{6,2},{1,5},{3,7},{5,1},{7,3},{8,12},{10,14},{12... | collective-permute-start | bytes 393224 | tf_op jit(solution)/shard_map/ppermute | solution.py:23
  29.7 9.4 %collective-permute-start.5 = (bf16[64,1024]{1,0:T(8,128)(2,1)S(1)}, bf16[64,1024]{1,0:T(8,128)(2,1)S(1)}, u32[]{:S(2)}, u32[]{:S(2)}) collective-permute-start(bf16[64,1024]{1,0:T(8,128)(2,1)S(1)} %pad_maximum_fusion.1), channel_id=1, source_target_pairs={{0,2},{2,4},{4,6},{6,0},{1,3},{3,5},{5,7},{7,1},{8,10},{10,12},{12... | collective-permute-start | bytes 393224 | tf_op jit(solution)/shard_map/ppermute | solution.py:23
  30.8 35.0 %all-to-all-start.1 = ((bf16[8,8,8,1024]{3,2,1,0:T(8,128)(2,1)}), bf16[8,8,8,1024]{3,2,1,0:T(8,128)(2,1)S(1)}, u32[]{:S(2)}, u32[]{:S(2)}) async-start(bf16[8,8,8,1024]{3,2,1,0:T(8,128)(2,1)} %broadcast_in_dim.10), calls=%async_computation.1 | async-start | bytes 2097152 | tf_op jit(solution)/shard_map/all_to_all | solution.py:18
  39.0 58.5 %reduce-scatter.2.cloned.1.call-start = ((), (), s32[]{:S(2)}) async-start(), calls=%async_computation.5 | async-start | bytes 2359296 | tf_op jit(solution)/shard_map/reduce_scatter | solution.py:114
  39.8 14.1 %collective-permute-start.8 = (bf16[4,64,1024]{2,1,0:T(8,128)(2,1)S(1)}, bf16[4,64,1024]{2,1,0:T(8,128)(2,1)S(1)}, u32[]{:S(2)}, u32[]{:S(2)}) collective-permute-start(bf16[4,64,1024]{2,1,0:T(8,128)(2,1)S(1)} %pad_maximum_fusion.own), channel_id=1, source_target_pairs={{0,1},{1,0},{2,3},{3,2},{4,5},{5,4},{6,7},{7,6},{8,9},{9,8},{10,11... | collective-permute-start | bytes 1572872 | tf_op jit(solution)/shard_map/ppermute | solution.py:23
  44.5 8.2 %collective-permute-start.10 = (bf16[128,1024]{1,0:T(8,128)(2,1)}, bf16[128,1024]{1,0:T(8,128)(2,1)S(1)}, u32[]{:S(2)}, u32[]{:S(2)}) collective-permute-start(bf16[128,1024]{1,0:T(8,128)(2,1)} %slice.75), channel_id=1, source_target_pairs={{0,192},{64,0},{128,64},{192,128},{1,193},{65,1},{129,65},{193,129... | collective-permute-start | bytes 786440 | tf_op jit(solution)/shard_map/ppermute | solution.py:23
  44.8 9.1 %collective-permute-start.9 = (bf16[128,1024]{1,0:T(8,128)(2,1)}, bf16[128,1024]{1,0:T(8,128)(2,1)}, u32[]{:S(2)}, u32[]{:S(2)}) collective-permute-start(bf16[128,1024]{1,0:T(8,128)(2,1)} %slice.74), channel_id=1, source_target_pairs={{0,64},{64,128},{128,192},{192,0},{1,65},{65,129},{129,193},{193,1... | collective-permute-start | bytes 786440 | tf_op jit(solution)/shard_map/ppermute | solution.py:23
  53.9 1.0 copy-start
  65.8 1.0 copy-start.1
  69.4 8.6 %collective-permute-start.15 = (bf16[4,4,64,256]{3,2,1,0:T(8,128)(2,1)S(1)}, bf16[4,4,64,256]{3,2,1,0:T(8,128)(2,1)S(1)}, u32[]{:S(2)}, u32[]{:S(2)}) collective-permute-start(bf16[4,4,64,256]{3,2,1,0:T(8,128)(2,1)S(1)} %get-tuple-element.44), channel_id=1, source_target_pairs={{0,1},{1,0},{2,3},{3,2},{4,5},{5,4},{6,7},{7,6},{8,9},{9,8},{10,11... | collective-permute-start | bytes 1572872 | tf_op jit(solution)/shard_map/ppermute | solution.py:23
  75.1 3.9 %copy-start.2 = (f32[1024,1024]{1,0:T(8,128)}, f32[1024,1024]{1,0:T(8,128)S(1)}, u32[]{:S(2)}) copy-start(f32[1024,1024]{1,0:T(8,128)S(1)} %get-tuple-element.58) | copy-start | bytes 12582916
  75.2 11.5 %collective-permute-start.13 = (bf16[128,1024]{1,0:T(8,128)(2,1)S(1)}, bf16[128,1024]{1,0:T(8,128)(2,1)S(1)}, u32[]{:S(2)}, u32[]{:S(2)}) collective-permute-start(bf16[128,1024]{1,0:T(8,128)(2,1)S(1)} %get-tuple-element.51), channel_id=1, source_target_pairs={{0,64},{64,128},{128,192},{192,0},{1,65},{65,129},{129,193},{193,1... | collective-permute-start | bytes 786440 | tf_op jit(solution)/shard_map/ppermute | solution.py:23
  77.2 9.6 %collective-permute-start.11 = (bf16[128,1024]{1,0:T(8,128)(2,1)S(1)}, bf16[128,1024]{1,0:T(8,128)(2,1)S(1)}, u32[]{:S(2)}, u32[]{:S(2)}) collective-permute-start(bf16[128,1024]{1,0:T(8,128)(2,1)S(1)} %get-tuple-element.52), channel_id=1, source_target_pairs={{0,192},{64,0},{128,64},{192,128},{1,193},{65,1},{129,65},{193,129... | collective-permute-start | bytes 786440 | tf_op jit(solution)/shard_map/ppermute | solution.py:23
  79.0 15.6 %all-to-all-start.3 = ((bf16[16,64,256]{2,1,0:T(8,128)(2,1)}), bf16[16,64,256]{2,1,0:T(8,128)(2,1)S(1)}, u32[]{:S(2)}, u32[]{:S(2)}) async-start(bf16[16,64,256]{2,1,0:T(8,128)(2,1)} %bitcast.26), calls=%async_computation.4 | async-start | bytes 1048576 | tf_op jit(solution)/shard_map/all_to_all | solution.py:18
  88.8 19.9 %collective-permute-start.14 = (bf16[2,128,1024]{2,1,0:T(8,128)(2,1)S(1)}, bf16[2,128,1024]{2,1,0:T(8,128)(2,1)S(1)}, u32[]{:S(2)}, u32[]{:S(2)}) collective-permute-start(bf16[2,128,1024]{2,1,0:T(8,128)(2,1)S(1)} %get-tuple-element.47), channel_id=1, source_target_pairs={{0,64},{64,128},{128,192},{192,0},{1,65},{65,129},{129,193},{193,1... | collective-permute-start | bytes 1572872 | tf_op jit(solution)/shard_map/ppermute | solution.py:23
  90.2 18.5 %collective-permute-start.12 = (bf16[2,128,1024]{2,1,0:T(8,128)(2,1)}, bf16[2,128,1024]{2,1,0:T(8,128)(2,1)S(1)}, u32[]{:S(2)}, u32[]{:S(2)}) collective-permute-start(bf16[2,128,1024]{2,1,0:T(8,128)(2,1)} %get-tuple-element.48), channel_id=1, source_target_pairs={{0,192},{64,0},{128,64},{192,128},{1,193},{65,1},{129,65},{193,129... | collective-permute-start | bytes 1572872 | tf_op jit(solution)/shard_map/ppermute | solution.py:23
  99.1 14.2 %all-to-all-start.2 = ((bf16[8,8,1024]{2,1,0:T(8,128)(2,1)}), bf16[8,8,1024]{2,1,0:T(8,128)(2,1)S(1)}, u32[]{:S(2)}, u32[]{:S(2)}) async-start(bf16[8,8,1024]{2,1,0:T(8,128)(2,1)} %convert_bitcast_fusion), calls=%async_computation.3 | async-start | bytes 262144 | tf_op jit(solution)/shard_map/all_to_all | solution.py:18
  (3 other events, 2.0 us)
Sparse Core Ops, SparseCore 0:
  59.0 38.4 reduce-scatter.1

commit v10 on v6

--- a/solution.py
+++ b/solution.py
@@ -134,8 +134,8 @@
     near = gw[1].at[0].add(shift(gw[2, 0].astype(BF), "y", -1).astype(F32))
     far = gw[3].at[1].add(shift(gw[2, 1].astype(BF), "y", 1).astype(F32))
     near, far = shift(near.astype(BF), "y", -1), shift(far.astype(BF), "y", 1)
+    near, far, proj = lax.optimization_barrier((near, far, proj))
     proj = exchange(proj, XC)
-    near, far, proj = lax.optimization_barrier((near, far, proj))
     grad_w = (gw[0] + near.astype(F32) + far.astype(F32)).reshape(r, n)
     proj_out = proj.transpose(1, 0, 2).reshape(j, d)
     return (proj_out, grad_attn, grad_w)

time: 117 us -> 118 us (level)
  waiting for transfers between devices: 31 us -> 36.1 us
  starting transfers between devices: 48.3 us -> 43.5 us
    ppermute x16, waiting for transfers between devices: 7.59 us -> 14 us  [shift(): return lax.ppermute(v, axis, [(i, (i + s) % n) for i in range(n)])]
    all_to_all x4, starting transfers between devices: 26.7 us -> 21.9 us  [exchange(): return lax.all_to_all(v, axes, split_axis=0, concat_axis=0, tiled=False)]
  transfers between devices with their start and end apart: 21 -> 21, of which waited for: 11 -> 12; matrix products, arithmetic and copies ran while one was open for 10% -> 11% of each run, Pallas kernels for 5% -> 5%
where the time goes in v10:
time: 118 us; the launch traced here: 117 us
  starting transfers between devices  43.5 us (37%)
  waiting for transfers between devices  36.1 us (31%)
  between operations  14.2 us (12%)
  other arithmetic  8.38 us (7%)
  local copies, waits for them, and re-layouts  8.05 us (7%)
  Pallas kernels  5.6 us (5%)
  matrix products  1.29 us (1%)
    all_to_all x4, starting transfers between devices, exchange(): return lax.all_to_all(v, axes, split_axis=0, concat_axis=0, tiled=False)  21.9 us
    ppermute x16, starting transfers between devices, shift(): return lax.ppermute(v, axis, [(i, (i + s) % n) for i in range(n)])  21.6 us
    all_to_all x4, waiting for transfers between devices, exchange(): return lax.all_to_all(v, axes, split_axis=0, concat_axis=0, tiled=False)  19.4 us
    ppermute x16, waiting for transfers between devices, shift(): return lax.ppermute(v, axis, [(i, (i + s) % n) for i in range(n)])  14 us
    pallas_call x2, Pallas kernels, call(): pl.pallas_call(kernel, out_shape=out_shape, in_specs=[SMEM] + [VMEM] * (l...  5.6 us
    unnamed x17, local copies, waits for them, and re-layouts  3.33 us
    reduce_scatter x1, waiting for transfers between devices, shards(): lax.psum_scatter(part, 'z', scatter_dimension=0, tiled=False).astype(BF)  2.74 us
    slice x1, local copies, waits for them, and re-layouts, shards(): far = gw[3].at[1].add(shift(gw[2, 1].astype(BF), 'y', 1).astype(F32))  2.54 us
  transfers between devices with their start and end apart: 21, of which 12 were waited for; matrix products, arithmetic and copies ran while one was open for 11% of the time, Pallas kernels for 5%

profile of v10, /device:TPU:1, one launch (start us, length us, event | category | flops | bytes accessed | tf_op | source)
XLA Modules:
  0.0 117.1 jit_solution(2352263502365923217)
XLA Ops:
  7.2 3.6 %collective-permute-start.4 = (bf16[256,1024]{1,0:T(8,128)(2,1)}, bf16[256,1024]{1,0:T(8,128)(2,1)S(1)}, u32[]{:S(2)}, u32[]{:S(2)}) collective-permute-start(bf16[256,1024]{1,0:T(8,128)(2,1)} %w0.3), channel_id=1, source_target_pairs={{0,192},{64,0},{128,64},{192,128},{1,193},{65,1},{129,65},{193,129... | collective-permute-start | bytes 1572872 | tf_op jit(solution)/shard_map/ppermute | solution.py:23
  12.5 2.8 %collective-permute-start.2 = (bf16[64,256]{1,0:T(8,128)(2,1)S(1)}, bf16[64,256]{1,0:T(8,128)(2,1)S(1)}, u32[]{:S(2)}, u32[]{:S(2)}) collective-permute-start(bf16[64,256]{1,0:T(8,128)(2,1)S(1)} %get-tuple-element.54), channel_id=1, source_target_pairs={{0,192},{64,0},{128,64},{192,128},{1,193},{65,1},{129,65},{193,129... | collective-permute-start | bytes 98312 | tf_op jit(solution)/shard_map/ppermute | solution.py:23
  16.0 6.1 %all-to-all-start = ((bf16[8,8,1024]{2,1,0:T(8,128)(2,1)}), bf16[8,8,1024]{2,1,0:T(8,128)(2,1)S(1)}, u32[]{:S(2)}, u32[]{:S(2)}) async-start(bf16[8,8,1024]{2,1,0:T(8,128)(2,1)} %bitcast.67), calls=%async_computation | async-start | bytes 262144 | tf_op jit(solution)/shard_map/all_to_all | solution.py:18
  24.1 1.7 %collective-permute-done = bf16[64,256]{1,0:T(8,128)(2,1)S(1)} collective-permute-done((bf16[64,256]{1,0:T(8,128)(2,1)S(1)}, bf16[64,256]{1,0:T(8,128)(2,1)S(1)}, u32[]{:S(2)}, u32[]{:S(2)}) %collective-permute-start) | collective-permute-done | bytes 32800 | tf_op jit(solution)/shard_map/ppermute | solution.py:23
  25.8 1.5 %all-to-all-done = bf16[8,8,1024]{2,1,0:T(8,128)(2,1)S(1)} async-done(((bf16[8,8,1024]{2,1,0:T(8,128)(2,1)}), bf16[8,8,1024]{2,1,0:T(8,128)(2,1)S(1)}, u32[]{:S(2)}, u32[]{:S(2)}) %all-to-all-start) | async-done | bytes 131104 | tf_op jit(solution)/shard_map/all_to_all | solution.py:18
  28.4 8.2 %all-to-all-start.1 = ((bf16[8,8,8,1024]{3,2,1,0:T(8,128)(2,1)}), bf16[8,8,8,1024]{3,2,1,0:T(8,128)(2,1)S(1)}, u32[]{:S(2)}, u32[]{:S(2)}) async-start(bf16[8,8,8,1024]{3,2,1,0:T(8,128)(2,1)} %broadcast_in_dim.10), calls=%async_computation.1 | async-start | bytes 2097152 | tf_op jit(solution)/shard_map/all_to_all | solution.py:18
  39.2 1.8 %collective-permute-start.10 = (bf16[128,1024]{1,0:T(8,128)(2,1)S(1)}, bf16[128,1024]{1,0:T(8,128)(2,1)S(1)}, u32[]{:S(2)}, u32[]{:S(2)}) collective-permute-start(bf16[128,1024]{1,0:T(8,128)(2,1)S(1)} %slice.75), channel_id=1, source_target_pairs={{0,192},{64,0},{128,64},{192,128},{1,193},{65,1},{129,65},{193,129... | collective-permute-start | bytes 786440 | tf_op jit(solution)/shard_map/ppermute | solution.py:23
  41.3 2.0 %collective-permute-done.6 = bf16[64,1024]{1,0:T(8,128)(2,1)S(1)} collective-permute-done((bf16[64,1024]{1,0:T(8,128)(2,1)S(1)}, bf16[64,1024]{1,0:T(8,128)(2,1)S(1)}, u32[]{:S(2)}, u32[]{:S(2)}) %collective-permute-start.6) | collective-permute-done | bytes 131104 | tf_op jit(solution)/shard_map/ppermute | solution.py:23
  43.3 1.3 %collective-permute-done.5 = bf16[64,1024]{1,0:T(8,128)(2,1)S(1)} collective-permute-done((bf16[64,1024]{1,0:T(8,128)(2,1)S(1)}, bf16[64,1024]{1,0:T(8,128)(2,1)S(1)}, u32[]{:S(2)}, u32[]{:S(2)}) %collective-permute-start.5) | collective-permute-done | bytes 131104 | tf_op jit(solution)/shard_map/ppermute | solution.py:23
  44.7 3.8 %collective-permute-start.8 = (bf16[4,64,1024]{2,1,0:T(8,128)(2,1)S(1)}, bf16[4,64,1024]{2,1,0:T(8,128)(2,1)S(1)}, u32[]{:S(2)}, u32[]{:S(2)}) collective-permute-start(bf16[4,64,1024]{2,1,0:T(8,128)(2,1)S(1)} %pad_maximum_fusion.own), channel_id=1, source_target_pairs={{0,1},{1,0},{2,3},{3,2},{4,5},{5,4},{6,7},{7,6},{8,9},{9,8},{10,11... | collective-permute-start | bytes 1572872 | tf_op jit(solution)/shard_map/ppermute | solution.py:23
  50.1 3.4 %shard_map.77 = f32[8,8,8,1024]{3,2,1,0:T(8,128)} custom-call(s32[3]{0:T(128)S(1)} %pad_add_fusion.where, bf16[4,64,1024]{2,1,0:T(8,128)(2,1)S(1)} %pad_maximum_fusion.own, bf16[4,64,1024]{2,1,0:T(8,128)(2,1)S(1)} %collective-permute-done.8.other, bf16[256,1024]{1,0:T(8,128)(2,1)S(1)} %copy-done, bf16[256,1024]{1,0:T(8,128)(2,1)S(1)} %collective-permute-done.3.w1, ...), custom_call_target="tpu_custom_call" | custom-call | flops 1073741824 | bytes 2684354 | tf_op jit(solution)/shard_map/pallas_call | solution.py:72
  55.1 10.7 %all-to-all-done.1.g = bf16[8,8,8,1024]{3,2,1,0:T(8,128)(2,1)S(1)} async-done(((bf16[8,8,8,1024]{3,2,1,0:T(8,128)(2,1)}), bf16[8,8,8,1024]{3,2,1,0:T(8,128)(2,1)S(1)}, u32[]{:S(2)}, u32[]{:S(2)}) %all-to-all-start.1) | async-done | bytes 1048608 | tf_op jit(solution)/shard_map/all_to_all | solution.py:18
  66.8 2.1 %shard_map.76 = (f32[4,4,64,256]{3,2,1,0:T(8,128)S(1)}, bf16[4,4,64,256]{3,2,1,0:T(8,128)(2,1)S(1)}, bf16[512,1024]{1,0:T(8,128)(2,1)S(1)}) custom-call(s32[3]{0:T(128)S(1)} %pad_add_fusion.where, bf16[8,8,8,1024]{3,2,1,0:T(8,128)(2,1)S(1)} %all-to-all-done.1.g, bf16[256,1024]{1,0:T(8,128)(2,1)S(1)} %copy-done, ...), custom_call_target="tpu_custom_call" | custom-call | flops 68719476736 | bytes 171798688 | tf_op jit(solution)/shard_map/pallas_call | solution.py:72
  71.1 2.3 %collective-permute-start.13 = (bf16[128,1024]{1,0:T(8,128)(2,1)S(1)}, bf16[128,1024]{1,0:T(8,128)(2,1)S(1)}, u32[]{:S(2)}, u32[]{:S(2)}) collective-permute-start(bf16[128,1024]{1,0:T(8,128)(2,1)S(1)} %get-tuple-element.51), channel_id=1, source_target_pairs={{0,64},{64,128},{128,192},{192,0},{1,65},{65,129},{129,193},{193,1... | collective-permute-start | bytes 786440 | tf_op jit(solution)/shard_map/ppermute | solution.py:23
  74.9 3.6 %all-to-all-start.3 = ((bf16[16,64,256]{2,1,0:T(8,128)(2,1)}), bf16[16,64,256]{2,1,0:T(8,128)(2,1)S(1)}, u32[]{:S(2)}, u32[]{:S(2)}) async-start(bf16[16,64,256]{2,1,0:T(8,128)(2,1)} %bitcast.26), calls=%async_computation.4 | async-start | bytes 1048576 | tf_op jit(solution)/shard_map/all_to_all | solution.py:18
  78.4 2.5 %fusion.4 = (bf16[256,1024]{1,0:T(8,128)(2,1)S(1)}, bf16[256,1024]{1,0:T(8,128)(2,1)}) fusion(f32[1024,1024]{1,0:T(8,128)} %copy-done.3), kind=kLoop, calls=%fused_computation.28 | loop fusion | bytes 2097152 | tf_op jit(solution)/shard_map/slice | solution.py:135
  81.0 2.1 %fusion.1 = (bf16[2,128,1024]{2,1,0:T(8,128)(2,1)S(1)}, bf16[2,128,1024]{2,1,0:T(8,128)(2,1)}) fusion(bf16[2,128,1024]{2,1,0:T(8,128)(2,1)S(1)} %bitcast.63, f32[1024,1024]{1,0:T(8,128)} %copy-done.3, bf16[128,1024]{1,0:T(8,128)(2,1)S(1)} %collective-permute-done.13, bf16[2,128,1024]{2,1,0:T(8,128)(2,1)} %bitcast.16, ...), kind=kLoop, calls=%fused_computation.5 | loop fusion | flops 524288 | bytes 2621440 | tf_op jit(solution)/shard_map/scatter-add | solution.py:135
  84.3 1.4 %collective-permute-start.12 = (bf16[2,128,1024]{2,1,0:T(8,128)(2,1)}, bf16[2,128,1024]{2,1,0:T(8,128)(2,1)S(1)}, u32[]{:S(2)}, u32[]{:S(2)}) collective-permute-start(bf16[2,128,1024]{2,1,0:T(8,128)(2,1)} %get-tuple-element.48), channel_id=1, source_target_pairs={{0,192},{64,0},{128,64},{192,128},{1,193},{65,1},{129,65},{193,129... | collective-permute-start | bytes 1572872 | tf_op jit(solution)/shard_map/ppermute | solution.py:23
  85.7 3.1 %all-to-all-done.3 = bf16[16,64,256]{2,1,0:T(8,128)(2,1)S(1)} async-done(((bf16[16,64,256]{2,1,0:T(8,128)(2,1)}), bf16[16,64,256]{2,1,0:T(8,128)(2,1)S(1)}, u32[]{:S(2)}, u32[]{:S(2)}) %all-to-all-start.3) | async-done | bytes 524320 | tf_op jit(solution)/shard_map/all_to_all | solution.py:18
  89.6 2.7 %reduce-scatter.2.cloned.1.call-done = f32[1,8,8,1024]{3,2,1,0:T(8,128)} async-done(((f32[8,8,8,1024]{3,2,1,0:T(8,128)}), f32[1,8,8,1024]{3,2,1,0:T(8,128)}) %reduce-scatter.2.cloned.1.call-update) | async-done | bytes 262160 | tf_op jit(solution)/shard_map/reduce_scatter | solution.py:114
  92.3 1.6 %convert_bitcast_fusion = bf16[8,8,1024]{2,1,0:T(8,128)(2,1)} fusion(f32[1,8,8,1024]{3,2,1,0:T(8,128)} %reduce-scatter.2.cloned.1.call-done), kind=kLoop, calls=%fused_computation.15 | loop fusion | flops 65536 | bytes 393216 | tf_op jit(solution)/shard_map/convert_element_type | solution.py:114
  94.0 6.4 %collective-permute-done.14 = bf16[2,128,1024]{2,1,0:T(8,128)(2,1)S(1)} collective-permute-done((bf16[2,128,1024]{2,1,0:T(8,128)(2,1)S(1)}, bf16[2,128,1024]{2,1,0:T(8,128)(2,1)S(1)}, u32[]{:S(2)}, u32[]{:S(2)}) %collective-permute-start.14) | collective-permute-done | bytes 524320 | tf_op jit(solution)/shard_map/ppermute | solution.py:23
  100.3 4.0 %all-to-all-start.2 = ((bf16[8,8,1024]{2,1,0:T(8,128)(2,1)}), bf16[8,8,1024]{2,1,0:T(8,128)(2,1)S(1)}, u32[]{:S(2)}, u32[]{:S(2)}) async-start(bf16[8,8,1024]{2,1,0:T(8,128)(2,1)} %convert_bitcast_fusion), calls=%async_computation.3 | async-start | bytes 262144 | tf_op jit(solution)/shard_map/all_to_all | solution.py:18
  105.6 4.1 %all-to-all-done.2 = bf16[8,8,1024]{2,1,0:T(8,128)(2,1)S(1)} async-done(((bf16[8,8,1024]{2,1,0:T(8,128)(2,1)}), bf16[8,8,1024]{2,1,0:T(8,128)(2,1)S(1)}, u32[]{:S(2)}, u32[]{:S(2)}) %all-to-all-start.2) | async-done | bytes 131104 | tf_op jit(solution)/shard_map/all_to_all | solution.py:18
  (59 shorter events, 19.9 us)
Async XLA Ops:
  7.2 42.9 %copy-start = (bf16[256,1024]{1,0:T(8,128)(2,1)S(1)}, bf16[256,1024]{1,0:T(8,128)(2,1)}, u32[]{:S(2)}) copy-start(bf16[256,1024]{1,0:T(8,128)(2,1)} %w0.3) | copy-start | bytes 1572868
  7.2 20.2 %collective-permute-start.4 = (bf16[256,1024]{1,0:T(8,128)(2,1)}, bf16[256,1024]{1,0:T(8,128)(2,1)S(1)}, u32[]{:S(2)}, u32[]{:S(2)}) collective-permute-start(bf16[256,1024]{1,0:T(8,128)(2,1)} %w0.3), channel_id=1, source_target_pairs={{0,192},{64,0},{128,64},{192,128},{1,193},{65,1},{129,65},{193,129... | collective-permute-start | bytes 1572872 | tf_op jit(solution)/shard_map/ppermute | solution.py:23
  10.8 16.5 %collective-permute-start.3 = (bf16[256,1024]{1,0:T(8,128)(2,1)}, bf16[256,1024]{1,0:T(8,128)(2,1)S(1)}, u32[]{:S(2)}, u32[]{:S(2)}) collective-permute-start(bf16[256,1024]{1,0:T(8,128)(2,1)} %w0.3), channel_id=1, source_target_pairs={{0,64},{64,128},{128,192},{192,0},{1,65},{65,129},{129,193},{193,1... | collective-permute-start | bytes 1572872 | tf_op jit(solution)/shard_map/ppermute | solution.py:23
  12.5 10.4 %collective-permute-start.2 = (bf16[64,256]{1,0:T(8,128)(2,1)S(1)}, bf16[64,256]{1,0:T(8,128)(2,1)S(1)}, u32[]{:S(2)}, u32[]{:S(2)}) collective-permute-start(bf16[64,256]{1,0:T(8,128)(2,1)S(1)} %get-tuple-element.54), channel_id=1, source_target_pairs={{0,192},{64,0},{128,64},{192,128},{1,193},{65,1},{129,65},{193,129... | collective-permute-start | bytes 98312 | tf_op jit(solution)/shard_map/ppermute | solution.py:23
  15.3 8.8 %collective-permute-start.1 = (bf16[64,256]{1,0:T(8,128)(2,1)S(1)}, bf16[64,256]{1,0:T(8,128)(2,1)S(1)}, u32[]{:S(2)}, u32[]{:S(2)}) collective-permute-start(bf16[64,256]{1,0:T(8,128)(2,1)S(1)} %get-tuple-element.55), channel_id=1, source_target_pairs={{0,128},{64,192},{128,0},{192,64},{1,129},{65,193},{129,1},{193,65... | collective-permute-start | bytes 98312 | tf_op jit(solution)/shard_map/ppermute | solution.py:23
  15.3 10.5 %collective-permute-start = (bf16[64,256]{1,0:T(8,128)(2,1)S(1)}, bf16[64,256]{1,0:T(8,128)(2,1)S(1)}, u32[]{:S(2)}, u32[]{:S(2)}) collective-permute-start(bf16[64,256]{1,0:T(8,128)(2,1)S(1)} %get-tuple-element.56), channel_id=1, source_target_pairs={{0,64},{64,128},{128,192},{192,0},{1,65},{65,129},{129,193},{193,1... | collective-permute-start | bytes 98312 | tf_op jit(solution)/shard_map/ppermute | solution.py:23
  16.0 11.4 %all-to-all-start = ((bf16[8,8,1024]{2,1,0:T(8,128)(2,1)}), bf16[8,8,1024]{2,1,0:T(8,128)(2,1)S(1)}, u32[]{:S(2)}, u32[]{:S(2)}) async-start(bf16[8,8,1024]{2,1,0:T(8,128)(2,1)} %bitcast.67), calls=%async_computation | async-start | bytes 262144 | tf_op jit(solution)/shard_map/all_to_all | solution.py:18
  28.4 37.4 %all-to-all-start.1 = ((bf16[8,8,8,1024]{3,2,1,0:T(8,128)(2,1)}), bf16[8,8,8,1024]{3,2,1,0:T(8,128)(2,1)S(1)}, u32[]{:S(2)}, u32[]{:S(2)}) async-start(bf16[8,8,8,1024]{3,2,1,0:T(8,128)(2,1)} %broadcast_in_dim.10), calls=%async_computation.1 | async-start | bytes 2097152 | tf_op jit(solution)/shard_map/all_to_all | solution.py:18
  36.6 55.7 %reduce-scatter.2.cloned.1.call-start = ((), (), s32[]{:S(2)}) async-start(), calls=%async_computation.5 | async-start | bytes 2359296 | tf_op jit(solution)/shard_map/reduce_scatter | solution.py:114
  36.7 4.6 %collective-permute-start.7 = (bf16[64,1024]{1,0:T(8,128)(2,1)S(1)}, bf16[64,1024]{1,0:T(8,128)(2,1)S(1)}, u32[]{:S(2)}, u32[]{:S(2)}) collective-permute-start(bf16[64,1024]{1,0:T(8,128)(2,1)S(1)} %pad_maximum_fusion.1), channel_id=1, source_target_pairs={{0,6},{2,0},{4,2},{6,4},{1,7},{3,1},{5,3},{7,5},{8,14},{10,8},{12,... | collective-permute-start | bytes 393224 | tf_op jit(solution)/shard_map/ppermute | solution.py:23
  37.9 5.4 %collective-permute-start.6 = (bf16[64,1024]{1,0:T(8,128)(2,1)S(1)}, bf16[64,1024]{1,0:T(8,128)(2,1)S(1)}, u32[]{:S(2)}, u32[]{:S(2)}) collective-permute-start(bf16[64,1024]{1,0:T(8,128)(2,1)S(1)} %pad_maximum_fusion.1), channel_id=1, source_target_pairs={{0,4},{2,6},{4,0},{6,2},{1,5},{3,7},{5,1},{7,3},{8,12},{10,14},{12... | collective-permute-start | bytes 393224 | tf_op jit(solution)/shard_map/ppermute | solution.py:23
  39.1 5.5 %collective-permute-start.5 = (bf16[64,1024]{1,0:T(8,128)(2,1)S(1)}, bf16[64,1024]{1,0:T(8,128)(2,1)S(1)}, u32[]{:S(2)}, u32[]{:S(2)}) collective-permute-start(bf16[64,1024]{1,0:T(8,128)(2,1)S(1)} %pad_maximum_fusion.1), channel_id=1, source_target_pairs={{0,2},{2,4},{4,6},{6,0},{1,3},{3,5},{5,7},{7,1},{8,10},{10,12},{12... | collective-permute-start | bytes 393224 | tf_op jit(solution)/shard_map/ppermute | solution.py:23
  39.2 9.4 %collective-permute-start.10 = (bf16[128,1024]{1,0:T(8,128)(2,1)S(1)}, bf16[128,1024]{1,0:T(8,128)(2,1)S(1)}, u32[]{:S(2)}, u32[]{:S(2)}) collective-permute-start(bf16[128,1024]{1,0:T(8,128)(2,1)S(1)} %slice.75), channel_id=1, source_target_pairs={{0,192},{64,0},{128,64},{192,128},{1,193},{65,1},{129,65},{193,129... | collective-permute-start | bytes 786440 | tf_op jit(solution)/shard_map/ppermute | solution.py:23
  41.0 7.6 %collective-permute-start.9 = (bf16[128,1024]{1,0:T(8,128)(2,1)S(1)}, bf16[128,1024]{1,0:T(8,128)(2,1)S(1)}, u32[]{:S(2)}, u32[]{:S(2)}) collective-permute-start(bf16[128,1024]{1,0:T(8,128)(2,1)S(1)} %slice.74), channel_id=1, source_target_pairs={{0,64},{64,128},{128,192},{192,0},{1,65},{65,129},{129,193},{193,1... | collective-permute-start | bytes 786440 | tf_op jit(solution)/shard_map/ppermute | solution.py:23
  44.7 5.3 %collective-permute-start.8 = (bf16[4,64,1024]{2,1,0:T(8,128)(2,1)S(1)}, bf16[4,64,1024]{2,1,0:T(8,128)(2,1)S(1)}, u32[]{:S(2)}, u32[]{:S(2)}) collective-permute-start(bf16[4,64,1024]{2,1,0:T(8,128)(2,1)S(1)} %pad_maximum_fusion.own), channel_id=1, source_target_pairs={{0,1},{1,0},{2,3},{3,2},{4,5},{5,4},{6,7},{7,6},{8,9},{9,8},{10,11... | collective-permute-start | bytes 1572872 | tf_op jit(solution)/shard_map/ppermute | solution.py:23
  66.8 2.9 %copy-start.5 = (bf16[8,64,1024]{2,1,0:T(8,128)(2,1)S(1)}, bf16[8,64,1024]{2,1,0:T(8,128)(2,1)}, u32[]{:S(2)}) copy-start(bf16[8,64,1024]{2,1,0:T(8,128)(2,1)} %constant_dynamic-update-slice_fusion) | copy-start | bytes 3145732
  68.9 5.0 %collective-permute-start.15 = (bf16[4,4,64,256]{3,2,1,0:T(8,128)(2,1)S(1)}, bf16[4,4,64,256]{3,2,1,0:T(8,128)(2,1)S(1)}, u32[]{:S(2)}, u32[]{:S(2)}) collective-permute-start(bf16[4,4,64,256]{3,2,1,0:T(8,128)(2,1)S(1)} %get-tuple-element.44), channel_id=1, source_target_pairs={{0,1},{1,0},{2,3},{3,2},{4,5},{5,4},{6,7},{7,6},{8,9},{9,8},{10,11... | collective-permute-start | bytes 1572872 | tf_op jit(solution)/shard_map/ppermute | solution.py:23
  71.0 3.9 %copy-start.3 = (f32[1024,1024]{1,0:T(8,128)}, f32[1024,1024]{1,0:T(8,128)S(1)}, u32[]{:S(2)}) copy-start(f32[1024,1024]{1,0:T(8,128)S(1)} %get-tuple-element.58) | copy-start | bytes 12582916
  71.1 9.9 %collective-permute-start.13 = (bf16[128,1024]{1,0:T(8,128)(2,1)S(1)}, bf16[128,1024]{1,0:T(8,128)(2,1)S(1)}, u32[]{:S(2)}, u32[]{:S(2)}) collective-permute-start(bf16[128,1024]{1,0:T(8,128)(2,1)S(1)} %get-tuple-element.51), channel_id=1, source_target_pairs={{0,64},{64,128},{128,192},{192,0},{1,65},{65,129},{129,193},{193,1... | collective-permute-start | bytes 786440 | tf_op jit(solution)/shard_map/ppermute | solution.py:23
  73.4 7.6 %collective-permute-start.11 = (bf16[128,1024]{1,0:T(8,128)(2,1)S(1)}, bf16[128,1024]{1,0:T(8,128)(2,1)S(1)}, u32[]{:S(2)}, u32[]{:S(2)}) collective-permute-start(bf16[128,1024]{1,0:T(8,128)(2,1)S(1)} %get-tuple-element.52), channel_id=1, source_target_pairs={{0,192},{64,0},{128,64},{192,128},{1,193},{65,1},{129,65},{193,129... | collective-permute-start | bytes 786440 | tf_op jit(solution)/shard_map/ppermute | solution.py:23
  74.9 14.0 %all-to-all-start.3 = ((bf16[16,64,256]{2,1,0:T(8,128)(2,1)}), bf16[16,64,256]{2,1,0:T(8,128)(2,1)S(1)}, u32[]{:S(2)}, u32[]{:S(2)}) async-start(bf16[16,64,256]{2,1,0:T(8,128)(2,1)} %bitcast.26), calls=%async_computation.4 | async-start | bytes 1048576 | tf_op jit(solution)/shard_map/all_to_all | solution.py:18
  83.1 17.3 %collective-permute-start.14 = (bf16[2,128,1024]{2,1,0:T(8,128)(2,1)S(1)}, bf16[2,128,1024]{2,1,0:T(8,128)(2,1)S(1)}, u32[]{:S(2)}, u32[]{:S(2)}) collective-permute-start(bf16[2,128,1024]{2,1,0:T(8,128)(2,1)S(1)} %get-tuple-element.47), channel_id=1, source_target_pairs={{0,64},{64,128},{128,192},{192,0},{1,65},{65,129},{129,193},{193,1... | collective-permute-start | bytes 1572872 | tf_op jit(solution)/shard_map/ppermute | solution.py:23
  84.3 16.0 %collective-permute-start.12 = (bf16[2,128,1024]{2,1,0:T(8,128)(2,1)}, bf16[2,128,1024]{2,1,0:T(8,128)(2,1)S(1)}, u32[]{:S(2)}, u32[]{:S(2)}) collective-permute-start(bf16[2,128,1024]{2,1,0:T(8,128)(2,1)} %get-tuple-element.48), channel_id=1, source_target_pairs={{0,192},{64,0},{128,64},{192,128},{1,193},{65,1},{129,65},{193,129... | collective-permute-start | bytes 1572872 | tf_op jit(solution)/shard_map/ppermute | solution.py:23
  100.3 9.3 %all-to-all-start.2 = ((bf16[8,8,1024]{2,1,0:T(8,128)(2,1)}), bf16[8,8,1024]{2,1,0:T(8,128)(2,1)S(1)}, u32[]{:S(2)}, u32[]{:S(2)}) async-start(bf16[8,8,1024]{2,1,0:T(8,128)(2,1)} %convert_bitcast_fusion), calls=%async_computation.3 | async-start | bytes 262144 | tf_op jit(solution)/shard_map/all_to_all | solution.py:18
  (3 other events, 2.6 us)
Sparse Core Ops, SparseCore 0:
  54.4 37.9 reduce-scatter.1

commit v11 on v9

--- a/solution.py
+++ b/solution.py
@@ -27,7 +27,7 @@
     return ((where[0] - s) & (nx - 1)) * 2 + (where[1] ^ e)
 
 
-def forward(where, own, other, w0, w1, w2a, w2b, w3, out):
+def forward(where, own, other, w0, w1a, w1b, w2a, w2b, w3a, w3b, out):
     nx, ty, _ = own.shape
     nz, _, j, n = out.shape
     r = w0.shape[0]
@@ -35,15 +35,14 @@
     for e, a in enumerate((own, other)):
         rows = a[...].reshape(nx * ty, a.shape[2])
         total = jnp.dot(rows[:, :r], w0[...], preferred_element_type=F32)
-        total += jnp.dot(rows[:, r : 2 * r], w1[...], preferred_element_type=F32)
-        total += jnp.dot(rows[:, 2 * r : 2 * r + half], w2a[...], preferred_element_type=F32)
-        total += jnp.dot(rows[:, 2 * r + half : 3 * r], w2b[...], preferred_element_type=F32)
-        total += jnp.dot(rows[:, 3 * r :], w3[...], preferred_element_type=F32)
+        for i, part in enumerate((w1a, w1b, w2a, w2b, w3a, w3b)):
+            cols = slice(r + i * half, r + (i + 1) * half)
+            total += jnp.dot(rows[:, cols], part[...], preferred_element_type=F32)
         for s in range(nx):
             out[:, place(where, e, s, nx)] = total[s * ty : (s + 1) * ty].reshape(nz, j, n)
 
 
-def backward(where, g, w0, w1, w2a, w2b, w3, own, other, g_rel, rows):
+def backward(where, g, w0, w1a, w1b, w2a, w2b, w3a, w3b, own, other, g_rel, rows):
     n = g.shape[3]
     nx, ny, ty, r = own.shape
     half = r // 2
@@ -58,7 +57,7 @@
             at = pl.multiple_of((e * nx + ((where[0] - s) & (nx - 1))) * ty, ty)
             g_rel[k * ty : (k + 1) * ty] = rows[pl.ds(at, ty)]
     across = (((1,), (1,)), ((), ()))
-    for s, w in enumerate(((w0,), (w1,), (w2a, w2b), (w3,))):
+    for s, w in enumerate(((w0,), (w1a, w1b), (w2a, w2b), (w3a, w3b))):
         at = (where[2] - s) & (ny - 1)
         width = r // len(w)
         for i, part in enumerate(w):
@@ -90,7 +89,9 @@
     ty = t // ny
     half = r // 2
 
-    w1, w3 = shift(w_out, "y", 1), shift(w_out, "y", -1)
+    w1a, w3b = shift(w_out[:half], "y", 1), shift(w_out[half:], "y", -1)
+    w1b, w3a = shift(w_out[half:], "y", 1), shift(w_out[:half], "y", -1)
+    w2a, w2b = shift(w1a, "y", 1), shift(w3b, "y", -1)
     g = exchange(grad_out.reshape(j, nx * nc, n).transpose(1, 0, 2), XC)
 
     gate_vals = head_mask.astype(F32) * gate_scale
@@ -100,12 +101,11 @@
     a = [lax.dynamic_index_in_dim(gated, (me + s) % ny, 0, keepdims=False) for s in range(ny)]
     a = [a[0]] + [shift(a[s], "y", s) for s in range(1, ny)]
     a = jnp.concatenate(a, axis=1)
-    a, g, w1, w3 = lax.optimization_barrier((a, g, w1, w3))
+    a, g, w2a, w2b, w1b, w3a = lax.optimization_barrier((a, g, w2a, w2b, w1b, w3a))
     g = exchange(jnp.broadcast_to(g[None], (nz,) + g.shape), "z")
     a = jnp.stack([a] + [shift(a, "x", s) for s in range(1, nx)])
-    w2a, w2b = shift(w1[:half], "y", 1), shift(w3[half:], "y", -1)
     other = shift(a, "c", 1)
-    w = (w_out, w1, w2a, w2b, w3)
+    w = (w_out, w1a, w1b, w2a, w2b, w3a, w3b)
 
     part = call(
         forward, jax.ShapeDtypeStruct((nz, nx * nc, j, n), F32), where, a, other, *w,

time: 123 us -> 140 us (1.14)
  waiting for transfers between devices: 24.5 us -> 36.1 us
  local copies, waits for them, and re-layouts: 14.9 us -> 19.2 us
    all_to_all x4, waiting for transfers between devices: 9.97 us -> 19.6 us  [exchange(): return lax.all_to_all(v, axes, split_axis=0, concat_axis=0, tiled=False)]
    ppermute x16 -> x18, waiting for transfers between devices: 11.6 us -> 16.4 us  [shift(): return lax.ppermute(v, axis, [(i, (i + s) % n) for i in range(n)])]
    unnamed x17 -> x29, local copies, waits for them, and re-layouts: 8.78 us -> 12.4 us
    reduce_scatter x1, waiting for transfers between devices: 2.86 us -> 0.02 us  [shards(): lax.psum_scatter(part, 'z', scatter_dimension=0, tiled=False).astype(BF)]
    all_to_all x4, starting transfers between devices: 28.4 us -> 26.7 us  [exchange(): return lax.all_to_all(v, axes, split_axis=0, concat_axis=0, tiled=False)]
    ppermute x16 -> x18, starting transfers between devices: 22.7 us -> 23.9 us  [shift(): return lax.ppermute(v, axis, [(i, (i + s) % n) for i in range(n)])]
  transfers between devices with their start and end apart: 21 -> 23, of which waited for: 10 -> 10; matrix products, arithmetic and copies ran while one was open for 17% -> 16% of each run, Pallas kernels for 5% -> 5%
where the time goes in v11:
time: 140 us; the launch traced here: 139 us
  starting transfers between devices  50.7 us (36%)
  waiting for transfers between devices  36.1 us (26%)
  local copies, waits for them, and re-layouts  19.2 us (14%)
  between operations  14.2 us (10%)
  other arithmetic  9.45 us (7%)
  Pallas kernels  6.67 us (5%)
  matrix products  2.52 us (2%)
    all_to_all x4, starting transfers between devices, exchange(): return lax.all_to_all(v, axes, split_axis=0, concat_axis=0, tiled=False)  26.7 us
    ppermute x18, starting transfers between devices, shift(): return lax.ppermute(v, axis, [(i, (i + s) % n) for i in range(n)])  23.9 us
    all_to_all x4, waiting for transfers between devices, exchange(): return lax.all_to_all(v, axes, split_axis=0, concat_axis=0, tiled=False)  19.6 us
    ppermute x18, waiting for transfers between devices, shift(): return lax.ppermute(v, axis, [(i, (i + s) % n) for i in range(n)])  16.4 us
    unnamed x29, local copies, waits for them, and re-layouts  12.4 us
    pallas_call x2, Pallas kernels, call(): pl.pallas_call(kernel, out_shape=out_shape, in_specs=[SMEM] + [VMEM] * (l...  6.67 us
  transfers between devices with their start and end apart: 23, of which 10 were waited for; matrix products, arithmetic and copies ran while one was open for 16% of the time, Pallas kernels for 5%

profile of v11, /device:TPU:1, one launch (start us, length us, event | category | flops | bytes accessed | tf_op | source)
XLA Modules:
  0.0 138.7 jit_solution(2511604631846742451)
XLA Ops:
  8.3 2.2 %collective-permute-start.7 = (bf16[128,1024]{1,0:T(8,128)(2,1)S(1)}, bf16[128,1024]{1,0:T(8,128)(2,1)S(1)}, u32[]{:S(2)}, u32[]{:S(2)}) collective-permute-start(bf16[128,1024]{1,0:T(8,128)(2,1)S(1)} %get-tuple-element.57), channel_id=1, source_target_pairs={{0,64},{64,128},{128,192},{192,0},{1,65},{65,129},{129,193},{193,1... | collective-permute-start | bytes 786440 | tf_op jit(solution)/shard_map/ppermute | solution.py:23
  15.2 1.9 %collective-permute-done.5.w3b = bf16[128,1024]{1,0:T(8,128)(2,1)S(1)} collective-permute-done((bf16[128,1024]{1,0:T(8,128)(2,1)S(1)}, bf16[128,1024]{1,0:T(8,128)(2,1)S(1)}, u32[]{:S(2)}, u32[]{:S(2)}) %collective-permute-start.5) | collective-permute-done | bytes 262176 | tf_op jit(solution)/shard_map/ppermute | solution.py:23
  18.5 4.5 %collective-permute-done.3.w1a = bf16[128,1024]{1,0:T(8,128)(2,1)S(1)} collective-permute-done((bf16[128,1024]{1,0:T(8,128)(2,1)S(1)}, bf16[128,1024]{1,0:T(8,128)(2,1)S(1)}, u32[]{:S(2)}, u32[]{:S(2)}) %collective-permute-start.3) | collective-permute-done | bytes 262176 | tf_op jit(solution)/shard_map/ppermute | solution.py:23
  23.1 2.6 %collective-permute-start.2 = (bf16[64,256]{1,0:T(8,128)(2,1)S(1)}, bf16[64,256]{1,0:T(8,128)(2,1)S(1)}, u32[]{:S(2)}, u32[]{:S(2)}) collective-permute-start(bf16[64,256]{1,0:T(8,128)(2,1)S(1)} %get-tuple-element.60), channel_id=1, source_target_pairs={{0,192},{64,0},{128,64},{192,128},{1,193},{65,1},{129,65},{193,129... | collective-permute-start | bytes 98312 | tf_op jit(solution)/shard_map/ppermute | solution.py:23
  25.8 3.3 %collective-permute-done.2 = bf16[64,256]{1,0:T(8,128)(2,1)S(1)} collective-permute-done((bf16[64,256]{1,0:T(8,128)(2,1)S(1)}, bf16[64,256]{1,0:T(8,128)(2,1)S(1)}, u32[]{:S(2)}, u32[]{:S(2)}) %collective-permute-start.2) | collective-permute-done | bytes 32800 | tf_op jit(solution)/shard_map/ppermute | solution.py:23
  29.0 2.9 %collective-permute-start.1 = (bf16[64,256]{1,0:T(8,128)(2,1)S(1)}, bf16[64,256]{1,0:T(8,128)(2,1)S(1)}, u32[]{:S(2)}, u32[]{:S(2)}) collective-permute-start(bf16[64,256]{1,0:T(8,128)(2,1)S(1)} %get-tuple-element.61), channel_id=1, source_target_pairs={{0,128},{64,192},{128,0},{192,64},{1,129},{65,193},{129,1},{193,65... | collective-permute-start | bytes 98312 | tf_op jit(solution)/shard_map/ppermute | solution.py:23
  34.9 7.6 %all-to-all-start = ((bf16[8,8,1024]{2,1,0:T(8,128)(2,1)}), bf16[8,8,1024]{2,1,0:T(8,128)(2,1)S(1)}, u32[]{:S(2)}, u32[]{:S(2)}) async-start(bf16[8,8,1024]{2,1,0:T(8,128)(2,1)} %bitcast.63), calls=%async_computation | async-start | bytes 262144 | tf_op jit(solution)/shard_map/all_to_all | solution.py:18
  42.5 5.3 %all-to-all-done = bf16[8,8,1024]{2,1,0:T(8,128)(2,1)S(1)} async-done(((bf16[8,8,1024]{2,1,0:T(8,128)(2,1)}), bf16[8,8,1024]{2,1,0:T(8,128)(2,1)S(1)}, u32[]{:S(2)}, u32[]{:S(2)}) %all-to-all-start) | async-done | bytes 131104 | tf_op jit(solution)/shard_map/all_to_all | solution.py:18
  51.0 8.2 %all-to-all-start.1 = ((bf16[8,8,8,1024]{3,2,1,0:T(8,128)(2,1)}), bf16[8,8,8,1024]{3,2,1,0:T(8,128)(2,1)S(1)}, u32[]{:S(2)}, u32[]{:S(2)}) async-start(bf16[8,8,8,1024]{3,2,1,0:T(8,128)(2,1)} %broadcast_in_dim.10), calls=%async_computation.1 | async-start | bytes 2097152 | tf_op jit(solution)/shard_map/all_to_all | solution.py:18
  61.1 2.0 %collective-permute-start.12 = (bf16[4,64,1024]{2,1,0:T(8,128)(2,1)S(1)}, bf16[4,64,1024]{2,1,0:T(8,128)(2,1)S(1)}, u32[]{:S(2)}, u32[]{:S(2)}) collective-permute-start(bf16[4,64,1024]{2,1,0:T(8,128)(2,1)S(1)} %pad_maximum_fusion.own), channel_id=1, source_target_pairs={{0,1},{1,0},{2,3},{3,2},{4,5},{5,4},{6,7},{7,6},{8,9},{9,8},{10,11... | collective-permute-start | bytes 1572872 | tf_op jit(solution)/shard_map/ppermute | solution.py:23
  67.4 4.0 %shard_map.77 = f32[8,8,8,1024]{3,2,1,0:T(8,128)} custom-call(s32[3]{0:T(128)S(1)} %pad_add_fusion.where, bf16[4,64,1024]{2,1,0:T(8,128)(2,1)S(1)} %pad_maximum_fusion.own, bf16[4,64,1024]{2,1,0:T(8,128)(2,1)S(1)} %collective-permute-done.12.other, bf16[256,1024]{1,0:T(8,128)(2,1)S(1)} %copy-done, bf16[128,1024]{1,0:T(8,128)(2,1)S(1)} %copy-done.2, ...), custom_call_target="tpu_custom_call" | custom-call | flops 1073741824 | bytes 2684354 | tf_op jit(solution)/shard_map/pallas_call | solution.py:71
  73.6 1.6 %constant_dynamic-update-slice_fusion.2 = bf16[8,64,1024]{2,1,0:T(8,128)(2,1)} fusion(bf16[8,64,1024]{2,1,0:T(8,128)(2,1)} %constant_dynamic-update-slice_fusion.3, bf16[64,1024]{1,0:T(8,128)(2,1)} %collective-permute-done.10), kind=kLoop, calls=%fused_computation.22 | loop fusion | bytes 262144
  75.2 1.6 %constant_dynamic-update-slice_fusion.1 = bf16[8,64,1024]{2,1,0:T(8,128)(2,1)} fusion(bf16[8,64,1024]{2,1,0:T(8,128)(2,1)} %constant_dynamic-update-slice_fusion.2, bf16[64,1024]{1,0:T(8,128)(2,1)} %collective-permute-done.11), kind=kLoop, calls=%fused_computation.21 | loop fusion | bytes 262144
  77.6 10.8 %all-to-all-done.1.g = bf16[8,8,8,1024]{3,2,1,0:T(8,128)(2,1)S(1)} async-done(((bf16[8,8,8,1024]{3,2,1,0:T(8,128)(2,1)}), bf16[8,8,8,1024]{3,2,1,0:T(8,128)(2,1)S(1)}, u32[]{:S(2)}, u32[]{:S(2)}) %all-to-all-start.1) | async-done | bytes 1048608 | tf_op jit(solution)/shard_map/all_to_all | solution.py:18
  91.3 2.7 %shard_map.76 = (f32[4,4,64,256]{3,2,1,0:T(8,128)S(1)}, bf16[4,4,64,256]{3,2,1,0:T(8,128)(2,1)S(1)}, bf16[512,1024]{1,0:T(8,128)(2,1)S(1)}) custom-call(s32[3]{0:T(128)S(1)} %pad_add_fusion.where, bf16[8,8,8,1024]{3,2,1,0:T(8,128)(2,1)S(1)} %all-to-all-done.1.g, bf16[256,1024]{1,0:T(8,128)(2,1)S(1)} %copy-done, bf16[128,1024]{1,0:T(8,128)(2,1)S(1)} %copy-done.3, ...), custom_call_target="tpu_custom_call" | custom-call | flops 17179869184 | bytes 42949672 | tf_op jit(solution)/shard_map/pallas_call | solution.py:71
  94.7 2.5 %fusion.6 = (bf16[1024,1024]{1,0:T(8,128)(2,1)S(1)}, f32[1024,1024]{1,0:T(8,128)S(1)}) fusion(bf16[512,1024]{1,0:T(8,128)(2,1)} %bitcast.12, bf16[512,1024]{1,0:T(8,128)(2,1)S(1)} %get-tuple-element.45), kind=kOutput, calls=%fused_computation.30 | convolution fusion | flops 1074790400 | bytes 8388608 | tf_op jit(solution)/shard_map/dot_general | solution.py:132
  98.9 1.8 %collective-permute-start.13 = (bf16[128,1024]{1,0:T(8,128)(2,1)S(1)}, bf16[128,1024]{1,0:T(8,128)(2,1)S(1)}, u32[]{:S(2)}, u32[]{:S(2)}) collective-permute-start(bf16[128,1024]{1,0:T(8,128)(2,1)S(1)} %get-tuple-element.56), channel_id=1, source_target_pairs={{0,192},{64,0},{128,64},{192,128},{1,193},{65,1},{129,65},{193,129... | collective-permute-start | bytes 786440 | tf_op jit(solution)/shard_map/ppermute | solution.py:23
  101.8 5.5 %all-to-all-start.3 = ((bf16[16,64,256]{2,1,0:T(8,128)(2,1)}), bf16[16,64,256]{2,1,0:T(8,128)(2,1)S(1)}, u32[]{:S(2)}, u32[]{:S(2)}) async-start(bf16[16,64,256]{2,1,0:T(8,128)(2,1)} %bitcast.26), calls=%async_computation.4 | async-start | bytes 1048576 | tf_op jit(solution)/shard_map/all_to_all | solution.py:18
  107.3 2.7 %fusion.4 = (bf16[256,1024]{1,0:T(8,128)(2,1)}, bf16[256,1024]{1,0:T(8,128)(2,1)}) fusion(f32[1024,1024]{1,0:T(8,128)} %copy-done.10), kind=kLoop, calls=%fused_computation.28 | loop fusion | bytes 2097152 | tf_op jit(solution)/shard_map/slice | solution.py:135
  110.0 2.2 %fusion.1 = (bf16[2,128,1024]{2,1,0:T(8,128)(2,1)}, bf16[2,128,1024]{2,1,0:T(8,128)(2,1)}) fusion(bf16[2,128,1024]{2,1,0:T(8,128)(2,1)} %bitcast.20, f32[1024,1024]{1,0:T(8,128)} %copy-done.10, bf16[128,1024]{1,0:T(8,128)(2,1)S(1)} %collective-permute-done.15, bf16[2,128,1024]{2,1,0:T(8,128)(2,1)} %bitcast.16, bf16[128,1024]{1,0:T(8,128)(2,1)S(1)} %collective-permute-done.13), kind=kLoop, calls=%fused_computation.5 | loop fusion | flops 524288 | bytes 2621440 | tf_op jit(solution)/shard_map/scatter-add | solution.py:135
  114.8 2.8 %all-to-all-done.3 = bf16[16,64,256]{2,1,0:T(8,128)(2,1)S(1)} async-done(((bf16[16,64,256]{2,1,0:T(8,128)(2,1)}), bf16[16,64,256]{2,1,0:T(8,128)(2,1)S(1)}, u32[]{:S(2)}, u32[]{:S(2)}) %all-to-all-start.3) | async-done | bytes 524320 | tf_op jit(solution)/shard_map/all_to_all | solution.py:18
  117.7 1.6 %convert_bitcast_fusion = bf16[8,8,1024]{2,1,0:T(8,128)(2,1)} fusion(f32[1,8,8,1024]{3,2,1,0:T(8,128)} %reduce-scatter.2.cloned.1.call-done), kind=kLoop, calls=%fused_computation.15 | loop fusion | flops 65536 | bytes 393216 | tf_op jit(solution)/shard_map/convert_element_type | solution.py:114
  119.3 5.4 %all-to-all-start.2 = ((bf16[8,8,1024]{2,1,0:T(8,128)(2,1)}), bf16[8,8,1024]{2,1,0:T(8,128)(2,1)S(1)}, u32[]{:S(2)}, u32[]{:S(2)}) async-start(bf16[8,8,1024]{2,1,0:T(8,128)(2,1)} %convert_bitcast_fusion), calls=%async_computation.3 | async-start | bytes 262144 | tf_op jit(solution)/shard_map/all_to_all | solution.py:18
  125.4 3.8 %collective-permute-done.16 = bf16[2,128,1024]{2,1,0:T(8,128)(2,1)S(1)} collective-permute-done((bf16[2,128,1024]{2,1,0:T(8,128)(2,1)}, bf16[2,128,1024]{2,1,0:T(8,128)(2,1)S(1)}, u32[]{:S(2)}, u32[]{:S(2)}) %collective-permute-start.16) | collective-permute-done | bytes 524320 | tf_op jit(solution)/shard_map/ppermute | solution.py:23
  (74 shorter events, 35.2 us)
Async XLA Ops:
  7.2 57.4 %copy-start = (bf16[256,1024]{1,0:T(8,128)(2,1)S(1)}, bf16[256,1024]{1,0:T(8,128)(2,1)}, u32[]{:S(2)}) copy-start(bf16[256,1024]{1,0:T(8,128)(2,1)} %w0.3) | copy-start | bytes 1572868
  8.3 39.4 %collective-permute-start.7 = (bf16[128,1024]{1,0:T(8,128)(2,1)S(1)}, bf16[128,1024]{1,0:T(8,128)(2,1)S(1)}, u32[]{:S(2)}, u32[]{:S(2)}) collective-permute-start(bf16[128,1024]{1,0:T(8,128)(2,1)S(1)} %get-tuple-element.57), channel_id=1, source_target_pairs={{0,64},{64,128},{128,192},{192,0},{1,65},{65,129},{129,193},{193,1... | collective-permute-start | bytes 786440 | tf_op jit(solution)/shard_map/ppermute | solution.py:23
  10.5 6.6 %collective-permute-start.5 = (bf16[128,1024]{1,0:T(8,128)(2,1)S(1)}, bf16[128,1024]{1,0:T(8,128)(2,1)S(1)}, u32[]{:S(2)}, u32[]{:S(2)}) collective-permute-start(bf16[128,1024]{1,0:T(8,128)(2,1)S(1)} %get-tuple-element.57), channel_id=1, source_target_pairs={{0,192},{64,0},{128,64},{192,128},{1,193},{65,1},{129,65},{193,129... | collective-permute-start | bytes 786440 | tf_op jit(solution)/shard_map/ppermute | solution.py:23
  12.0 35.7 %collective-permute-start.8 = (bf16[128,1024]{1,0:T(8,128)(2,1)S(1)}, bf16[128,1024]{1,0:T(8,128)(2,1)S(1)}, u32[]{:S(2)}, u32[]{:S(2)}) collective-permute-start(bf16[128,1024]{1,0:T(8,128)(2,1)S(1)} %get-tuple-element.58), channel_id=1, source_target_pairs={{0,192},{64,0},{128,64},{192,128},{1,193},{65,1},{129,65},{193,129... | collective-permute-start | bytes 786440 | tf_op jit(solution)/shard_map/ppermute | solution.py:23
  13.4 9.6 %collective-permute-start.3 = (bf16[128,1024]{1,0:T(8,128)(2,1)S(1)}, bf16[128,1024]{1,0:T(8,128)(2,1)S(1)}, u32[]{:S(2)}, u32[]{:S(2)}) collective-permute-start(bf16[128,1024]{1,0:T(8,128)(2,1)S(1)} %get-tuple-element.58), channel_id=1, source_target_pairs={{0,64},{64,128},{128,192},{192,0},{1,65},{65,129},{129,193},{193,1... | collective-permute-start | bytes 786440 | tf_op jit(solution)/shard_map/ppermute | solution.py:23
  17.1 30.6 %collective-permute-start.6 = (bf16[128,1024]{1,0:T(8,128)(2,1)S(1)}, bf16[128,1024]{1,0:T(8,128)(2,1)S(1)}, u32[]{:S(2)}, u32[]{:S(2)}) collective-permute-start(bf16[128,1024]{1,0:T(8,128)(2,1)S(1)} %collective-permute-done.5.w3b), channel_id=1, source_target_pairs={{0,192},{64,0},{128,64},{192,128},{1,193},{65,1},{129,65},{193,129... | collective-permute-start | bytes 786440 | tf_op jit(solution)/shard_map/ppermute | solution.py:23
  23.0 24.8 %collective-permute-start.4 = (bf16[128,1024]{1,0:T(8,128)(2,1)S(1)}, bf16[128,1024]{1,0:T(8,128)(2,1)S(1)}, u32[]{:S(2)}, u32[]{:S(2)}) collective-permute-start(bf16[128,1024]{1,0:T(8,128)(2,1)S(1)} %collective-permute-done.3.w1a), channel_id=1, source_target_pairs={{0,64},{64,128},{128,192},{192,0},{1,65},{65,129},{129,193},{193,1... | collective-permute-start | bytes 786440 | tf_op jit(solution)/shard_map/ppermute | solution.py:23
  23.1 5.9 %collective-permute-start.2 = (bf16[64,256]{1,0:T(8,128)(2,1)S(1)}, bf16[64,256]{1,0:T(8,128)(2,1)S(1)}, u32[]{:S(2)}, u32[]{:S(2)}) collective-permute-start(bf16[64,256]{1,0:T(8,128)(2,1)S(1)} %get-tuple-element.60), channel_id=1, source_target_pairs={{0,192},{64,0},{128,64},{192,128},{1,193},{65,1},{129,65},{193,129... | collective-permute-start | bytes 98312 | tf_op jit(solution)/shard_map/ppermute | solution.py:23
  29.0 4.3 %collective-permute-start.1 = (bf16[64,256]{1,0:T(8,128)(2,1)S(1)}, bf16[64,256]{1,0:T(8,128)(2,1)S(1)}, u32[]{:S(2)}, u32[]{:S(2)}) collective-permute-start(bf16[64,256]{1,0:T(8,128)(2,1)S(1)} %get-tuple-element.61), channel_id=1, source_target_pairs={{0,128},{64,192},{128,0},{192,64},{1,129},{65,193},{129,1},{193,65... | collective-permute-start | bytes 98312 | tf_op jit(solution)/shard_map/ppermute | solution.py:23
  33.3 9.2 %collective-permute-start = (bf16[64,256]{1,0:T(8,128)(2,1)S(1)}, bf16[64,256]{1,0:T(8,128)(2,1)S(1)}, u32[]{:S(2)}, u32[]{:S(2)}) collective-permute-start(bf16[64,256]{1,0:T(8,128)(2,1)S(1)} %get-tuple-element.62), channel_id=1, source_target_pairs={{0,64},{64,128},{128,192},{192,0},{1,65},{65,129},{129,193},{193,1... | collective-permute-start | bytes 98312 | tf_op jit(solution)/shard_map/ppermute | solution.py:23
  34.9 12.9 %all-to-all-start = ((bf16[8,8,1024]{2,1,0:T(8,128)(2,1)}), bf16[8,8,1024]{2,1,0:T(8,128)(2,1)S(1)}, u32[]{:S(2)}, u32[]{:S(2)}) async-start(bf16[8,8,1024]{2,1,0:T(8,128)(2,1)} %bitcast.63), calls=%async_computation | async-start | bytes 262144 | tf_op jit(solution)/shard_map/all_to_all | solution.py:18
  47.8 11.5 %collective-permute-start.11 = (bf16[64,1024]{1,0:T(8,128)(2,1)S(1)}, bf16[64,1024]{1,0:T(8,128)(2,1)}, u32[]{:S(2)}, u32[]{:S(2)}) collective-permute-start(bf16[64,1024]{1,0:T(8,128)(2,1)S(1)} %pad_maximum_fusion.1), channel_id=1, source_target_pairs={{0,6},{2,0},{4,2},{6,4},{1,7},{3,1},{5,3},{7,5},{8,14},{10,8},{12,... | collective-permute-start | bytes 393224 | tf_op jit(solution)/shard_map/ppermute | solution.py:23
  48.7 10.5 %collective-permute-start.10 = (bf16[64,1024]{1,0:T(8,128)(2,1)S(1)}, bf16[64,1024]{1,0:T(8,128)(2,1)}, u32[]{:S(2)}, u32[]{:S(2)}) collective-permute-start(bf16[64,1024]{1,0:T(8,128)(2,1)S(1)} %pad_maximum_fusion.1), channel_id=1, source_target_pairs={{0,4},{2,6},{4,0},{6,2},{1,5},{3,7},{5,1},{7,3},{8,12},{10,14},{12... | collective-permute-start | bytes 393224 | tf_op jit(solution)/shard_map/ppermute | solution.py:23
  49.9 9.4 %collective-permute-start.9 = (bf16[64,1024]{1,0:T(8,128)(2,1)S(1)}, bf16[64,1024]{1,0:T(8,128)(2,1)S(1)}, u32[]{:S(2)}, u32[]{:S(2)}) collective-permute-start(bf16[64,1024]{1,0:T(8,128)(2,1)S(1)} %pad_maximum_fusion.1), channel_id=1, source_target_pairs={{0,2},{2,4},{4,6},{6,0},{1,3},{3,5},{5,7},{7,1},{8,10},{10,12},{12... | collective-permute-start | bytes 393224 | tf_op jit(solution)/shard_map/ppermute | solution.py:23
  51.0 37.4 %all-to-all-start.1 = ((bf16[8,8,8,1024]{3,2,1,0:T(8,128)(2,1)}), bf16[8,8,8,1024]{3,2,1,0:T(8,128)(2,1)S(1)}, u32[]{:S(2)}, u32[]{:S(2)}) async-start(bf16[8,8,8,1024]{3,2,1,0:T(8,128)(2,1)} %broadcast_in_dim.10), calls=%async_computation.1 | async-start | bytes 2097152 | tf_op jit(solution)/shard_map/all_to_all | solution.py:18
  59.2 58.5 %reduce-scatter.2.cloned.1.call-start = ((), (), s32[]{:S(2)}) async-start(), calls=%async_computation.5 | async-start | bytes 2359296 | tf_op jit(solution)/shard_map/reduce_scatter | solution.py:114
  61.1 3.5 %collective-permute-start.12 = (bf16[4,64,1024]{2,1,0:T(8,128)(2,1)S(1)}, bf16[4,64,1024]{2,1,0:T(8,128)(2,1)S(1)}, u32[]{:S(2)}, u32[]{:S(2)}) collective-permute-start(bf16[4,64,1024]{2,1,0:T(8,128)(2,1)S(1)} %pad_maximum_fusion.own), channel_id=1, source_target_pairs={{0,1},{1,0},{2,3},{3,2},{4,5},{5,4},{6,7},{7,6},{8,9},{9,8},{10,11... | collective-permute-start | bytes 1572872 | tf_op jit(solution)/shard_map/ppermute | solution.py:23
  94.0 6.8 %collective-permute-start.17 = (bf16[4,4,64,256]{3,2,1,0:T(8,128)(2,1)S(1)}, bf16[4,4,64,256]{3,2,1,0:T(8,128)(2,1)S(1)}, u32[]{:S(2)}, u32[]{:S(2)}) collective-permute-start(bf16[4,4,64,256]{3,2,1,0:T(8,128)(2,1)S(1)} %get-tuple-element.48), channel_id=1, source_target_pairs={{0,1},{1,0},{2,3},{3,2},{4,5},{5,4},{6,7},{7,6},{8,9},{9,8},{10,11... | collective-permute-start | bytes 1572872 | tf_op jit(solution)/shard_map/ppermute | solution.py:23
  98.0 12.0 %collective-permute-start.15 = (bf16[128,1024]{1,0:T(8,128)(2,1)}, bf16[128,1024]{1,0:T(8,128)(2,1)S(1)}, u32[]{:S(2)}, u32[]{:S(2)}) collective-permute-start(bf16[128,1024]{1,0:T(8,128)(2,1)} %get-tuple-element.55), channel_id=1, source_target_pairs={{0,64},{64,128},{128,192},{192,0},{1,65},{65,129},{129,193},{193,1... | collective-permute-start | bytes 786440 | tf_op jit(solution)/shard_map/ppermute | solution.py:23
  98.9 11.1 %collective-permute-start.13 = (bf16[128,1024]{1,0:T(8,128)(2,1)S(1)}, bf16[128,1024]{1,0:T(8,128)(2,1)S(1)}, u32[]{:S(2)}, u32[]{:S(2)}) collective-permute-start(bf16[128,1024]{1,0:T(8,128)(2,1)S(1)} %get-tuple-element.56), channel_id=1, source_target_pairs={{0,192},{64,0},{128,64},{192,128},{1,193},{65,1},{129,65},{193,129... | collective-permute-start | bytes 786440 | tf_op jit(solution)/shard_map/ppermute | solution.py:23
  101.8 15.8 %all-to-all-start.3 = ((bf16[16,64,256]{2,1,0:T(8,128)(2,1)}), bf16[16,64,256]{2,1,0:T(8,128)(2,1)S(1)}, u32[]{:S(2)}, u32[]{:S(2)}) async-start(bf16[16,64,256]{2,1,0:T(8,128)(2,1)} %bitcast.26), calls=%async_computation.4 | async-start | bytes 1048576 | tf_op jit(solution)/shard_map/all_to_all | solution.py:18
  112.1 17.1 %collective-permute-start.16 = (bf16[2,128,1024]{2,1,0:T(8,128)(2,1)}, bf16[2,128,1024]{2,1,0:T(8,128)(2,1)S(1)}, u32[]{:S(2)}, u32[]{:S(2)}) collective-permute-start(bf16[2,128,1024]{2,1,0:T(8,128)(2,1)} %get-tuple-element.51), channel_id=1, source_target_pairs={{0,64},{64,128},{128,192},{192,0},{1,65},{65,129},{129,193},{193,1... | collective-permute-start | bytes 1572872 | tf_op jit(solution)/shard_map/ppermute | solution.py:23
  113.5 15.8 %collective-permute-start.14 = (bf16[2,128,1024]{2,1,0:T(8,128)(2,1)}, bf16[2,128,1024]{2,1,0:T(8,128)(2,1)S(1)}, u32[]{:S(2)}, u32[]{:S(2)}) collective-permute-start(bf16[2,128,1024]{2,1,0:T(8,128)(2,1)} %get-tuple-element.52), channel_id=1, source_target_pairs={{0,192},{64,0},{128,64},{192,128},{1,193},{65,1},{129,65},{193,129... | collective-permute-start | bytes 1572872 | tf_op jit(solution)/shard_map/ppermute | solution.py:23
  119.3 10.7 %all-to-all-start.2 = ((bf16[8,8,1024]{2,1,0:T(8,128)(2,1)}), bf16[8,8,1024]{2,1,0:T(8,128)(2,1)S(1)}, u32[]{:S(2)}, u32[]{:S(2)}) async-start(bf16[8,8,1024]{2,1,0:T(8,128)(2,1)} %convert_bitcast_fusion), calls=%async_computation.3 | async-start | bytes 262144 | tf_op jit(solution)/shard_map/all_to_all | solution.py:18
  (11 other events, 71.7 us)
Sparse Core Ops, SparseCore 0:
  71.5 39.9 reduce-scatter.1
